TPU v7x, 32 devices: a whole 2x2x4 slice. The times are simulated.
32 devices in a mesh: wide: 8 (over z, x), narrow: 4 (over y, core).
Axes of the slice: x: 2, y: 2, z: 4, core: 2. Of those that a mesh axis runs over, the one named last changes fastest.
Arguments:
- tokens: bfloat16 [8, 1024, 1120], P('wide', 'narrow'), may hold values from -6 to 6
- lengths: int32 [8], P('wide'), may hold values from 128 to 1024, as said below
- norm_one: float32 [1120], replicated, may hold values from 0.25 to 1.75
- qkv_weight: bfloat16 [3, 1120, 1120], P(None, None, 'narrow'), may hold values from -0.25 to 0.25
- out_weight: bfloat16 [1120, 1120], P('narrow'), may hold values from -3 to 3
- norm_two: float32 [1120], replicated, may hold values from 0.25 to 1.75
- up_weight: bfloat16 [1120, 4480], P(None, 'narrow'), may hold values from -0.1875 to 0.1875
- down_weight: bfloat16 [4480, 1120], P('narrow'), may hold values from -0.09375 to 0.09375
- grad_out: bfloat16 [8, 1024, 1120], P('wide', 'narrow'), may hold values from -6 to 6
Outputs:
- block_output: bfloat16 [8, 1024, 1120], P('wide', 'narrow')
- input_grad: bfloat16 [8, 1024, 1120], P('wide', 'narrow')
- norm_one_grad: float32 [1120], replicated
- qkv_grad: float32 [3, 1120, 1120], P(None, None, 'narrow')
- out_grad: float32 [1120, 1120], P('narrow')
- norm_two_grad: float32 [1120], replicated
- up_grad: float32 [1120, 4480], P(None, 'narrow')
- down_grad: float32 [4480, 1120], P('narrow')
Inputs may be any that keep to these rules, and one draw needn't show every extreme that they name: `lengths`: each cell's count of real genes; some cell has exactly 1024 and some other exactly 128.
All inputs are finite; a program needn't handle non-finite values.
Results may differ from a plain program's by a relative error of at most 0.013.
The roundings to bfloat16 on the way count: a program that leaves them out, or rounds other values in their place, can miss the bound.
Values may be sent and summed in bfloat16 or wider, within the bound.
No kernel may reach another device: no remote copies, remote signals or barrier semaphores. Data moves between devices by JAX's collectives and lax.ppermute only.
A program may use at most 192 MiB of HBM per device.

v0:
```python
from functools import partial

import jax
import jax.numpy as jnp
from jax import lax
from jax.experimental import pallas as pl
from jax.experimental.pallas import tpu as pltpu
from jax.sharding import PartitionSpec as P

HS = 56
HP = 64
F32 = jnp.float32
BF16 = jnp.bfloat16


def layer_stats(values):
    mean = jnp.mean(values, axis=-1, keepdims=True)
    center = values - mean
    spread = jnp.mean(center * center, axis=-1, keepdims=True)
    rstd = lax.rsqrt(spread + 1e-05)
    return center * rstd, rstd


def layer_back(grad_scaled, normal, rstd):
    first = jnp.mean(grad_scaled, axis=-1, keepdims=True)
    second = jnp.mean(grad_scaled * normal, axis=-1, keepdims=True)
    return rstd * (grad_scaled - first - normal * second)


def dot(a, b, dims):
    return lax.dot_general(a, b, (dims, ((), ())), preferred_element_type=F32)


class Narrow:
    def __init__(self, size):
        self.perm = {k: [(i, i ^ k) for i in range(size)] for k in (1, 2, 3)}

    def send(self, value, k):
        return lax.ppermute(value, "narrow", self.perm[k])

    def gather(self, value):
        across = self.send(value, 2)
        return [value, self.send(value, 1), across, self.send(across, 1)]

    def exchange(self, blocks):
        return [blocks[0]] + [self.send(blocks[k], k) for k in (1, 2, 3)]

    def scatter_sum(self, terms, rows):
        part = [terms[k * rows : (k + 1) * rows] for k in range(4)]
        got = self.send(
            jnp.concatenate([part[1].astype(BF16), part[3].astype(BF16)], axis=0), 1
        ).astype(F32)
        far = (part[2] + got[rows:]).astype(BF16)
        return part[0] + got[:rows] + self.send(far, 2).astype(F32)


class Ring:
    def __init__(self, size):
        order = list(range(0, size, 2)) + list(range(size - 1, 0, -2))
        self.size = size
        pairs = [(order[i], order[(i + 1) % size]) for i in range(size)]
        self.perm = {1: pairs, -1: [(b, a) for a, b in pairs]}
        index = lax.axis_index("wide")
        self.place = jnp.where(index % 2 == 0, index // 2, size - 1 - index // 2)

    def pick(self, chunks, at):
        return lax.dynamic_index_in_dim(chunks, jnp.mod(at, self.size), 0, keepdims=False)

    def reduce(self, chunks, way):
        current = self.pick(chunks, self.place - way)
        for step in range(self.size - 1):
            got = lax.ppermute(current, "wide", self.perm[way])
            mine = self.pick(chunks, self.place - way * (2 + step))
            current = (got.astype(F32) + mine.astype(F32)).astype(BF16)
        return current

    def spread(self, current, way):
        whole = jnp.zeros((self.size,) + current.shape, F32)
        for step in range(self.size):
            at = jnp.mod(self.place - way * step, self.size)
            whole = lax.dynamic_update_index_in_dim(whole, current.astype(F32), at, 0)
            if step < self.size - 1:
                current = lax.ppermute(current, "wide", self.perm[way])
        return whole

    def total(self, chunks, way):
        if self.size > 8:
            return lax.psum(chunks.astype(F32), "wide")
        return self.spread(self.reduce(chunks, way), way)


LOG2E = 1.4426950408889634
SCALE = HS**-0.5


def nt(a, b):
    return lax.dot_general(a, b, (((1,), (1,)), ((), ())), preferred_element_type=F32)


def nn(a, b):
    return lax.dot_general(a, b, (((1,), (0,)), ((), ())), preferred_element_type=F32)


def half_of(values, which):
    lane = lax.broadcasted_iota(jnp.int32, values.shape, 1)
    keep = lane < HP if which == 0 else lane >= HP
    return jnp.where(keep, values, jnp.zeros_like(values))


def causal_tile(rows):
    key = lax.broadcasted_iota(jnp.int32, (rows, rows), 0)
    query = lax.broadcasted_iota(jnp.int32, (rows, rows), 1)
    return key <= query


def for_pair(body, last_heads):
    last = pl.num_programs(0) - 1

    @pl.when(pl.program_id(0) < last)
    def _():
        body(2)

    @pl.when(pl.program_id(0) == last)
    def _():
        body(last_heads)


def attend_kernel(last_heads, me_ref, *refs):
    q, k, v, (o_ref, lse_ref) = refs[0:4], refs[4:8], refs[8:12], refs[12:14]
    me = me_ref[0]
    rows = q[0].shape[0]

    def body(heads):
        value_t = [v[j][...].T for j in range(4)]
        causal = causal_tile(rows)
        for a in range(4):
            outs = []
            for h in range(heads):
                query = half_of(q[a][...], h)
                score = [nt(k[j][...], query) for j in range(a + 1)]
                score[a] = jnp.where(causal, score[a], -1e30)
                top = jnp.max(score[0], axis=0, keepdims=True)
                for j in range(1, a + 1):
                    top = jnp.maximum(top, jnp.max(score[j], axis=0, keepdims=True))
                top = top * (SCALE * LOG2E)
                total = jnp.zeros((1, rows), F32)
                acc = jnp.zeros((HP, rows), F32)
                for j in range(a + 1):
                    p = jnp.exp2(score[j] * (SCALE * LOG2E) - top)
                    total = total + jnp.sum(p, axis=0, keepdims=True)
                    acc = acc + nn(value_t[j][h * HP : (h + 1) * HP], p.astype(BF16))
                outs.append(acc / total)
                lse_ref[0, a, h : h + 1, :] = top + jnp.log2(total)
            if heads == 1:
                outs.append(jnp.zeros((HP, rows), F32))
            at = pl.multiple_of(jnp.bitwise_xor(me, a) * rows, rows)
            o_ref[pl.ds(at, rows), :] = jnp.concatenate(outs, axis=0).T.astype(BF16)

    for_pair(body, last_heads)


def attend_back_kernel(last_heads, me_ref, *refs):
    q, k, v, do, o = (refs[4 * i : 4 * i + 4] for i in range(5))
    lse_ref, g_ref, dk_acc, dv_acc = refs[20:24]
    me = me_ref[0]
    rows = q[0].shape[0]

    def body(heads):
        key_t = [k[j][...].T for j in range(4)]
        causal = causal_tile(rows)
        for a in range(4):
            grad = do[a][...]
            product = (grad.astype(F32) * o[a][...].astype(F32)).T
            grads_q = []
            for h in range(heads):
                query, grad_h = half_of(q[a][...], h), half_of(grad, h)
                inner = jnp.sum(product[h * HP : (h + 1) * HP], axis=0, keepdims=True)
                lse = lse_ref[0, a, h : h + 1, :]
                dq = jnp.zeros((HP, rows), F32)
                for j in range(a + 1):
                    score = nt(k[j][...], query) * (SCALE * LOG2E) - lse
                    if j == a:
                        score = jnp.where(causal, score, -1e30)
                    p = jnp.exp2(score)
                    ds = (p * (nt(v[j][...], grad_h) - inner)).astype(BF16)
                    dv, dk = nn(p.astype(BF16), grad_h), nn(ds, query)
                    if a == j and h == 0:
                        dv_acc[j], dk_acc[j] = dv, dk
                    else:
                        dv_acc[j] = dv_acc[j] + dv
                        dk_acc[j] = dk_acc[j] + dk
                    dq = dq + nn(key_t[j][h * HP : (h + 1) * HP], ds)
                grads_q.append(dq * SCALE)
            if heads == 1:
                grads_q.append(jnp.zeros((HP, rows), F32))
            at = pl.multiple_of(jnp.bitwise_xor(me, a) * rows, rows)
            g_ref[0, pl.ds(at, rows), :] = jnp.concatenate(grads_q, axis=0).T.astype(BF16)
        for j in range(4):
            at = pl.multiple_of(jnp.bitwise_xor(me, j) * rows, rows)
            g_ref[1, pl.ds(at, rows), :] = (dk_acc[j] * SCALE).astype(BF16)
            g_ref[2, pl.ds(at, rows), :] = dv_acc[j].astype(BF16)

    for_pair(body, last_heads)


def block_specs(rows, pairs, t):
    return [
        pl.BlockSpec((rows, 128), lambda p, m, j=j: (jnp.bitwise_xor(m[0], j), t * pairs + p))
        for j in range(4)
    ]


def attend(me, proj, rows, heads):
    pairs = -(-heads // 2)
    all_rows = 4 * rows
    tiles = heads * 10 * rows * rows
    return pl.pallas_call(
        partial(attend_kernel, 2 - heads % 2),
        out_shape=(
            jax.ShapeDtypeStruct((all_rows, pairs * 128), BF16),
            jax.ShapeDtypeStruct((pairs, 4, 8, rows), F32),
        ),
        grid_spec=pltpu.PrefetchScalarGridSpec(
            num_scalar_prefetch=1,
            grid=(pairs,),
            in_specs=[s for t in range(3) for s in block_specs(rows, pairs, t)],
            out_specs=[
                pl.BlockSpec((all_rows, 128), lambda p, m: (0, p)),
                pl.BlockSpec((1, 4, 8, rows), lambda p, m: (p, 0, 0, 0)),
            ],
        ),
        cost_estimate=pl.CostEstimate(
            flops=tiles * 4 * HP, bytes_accessed=all_rows * pairs * 1024, transcendentals=tiles
        ),
    )(me, *([proj] * 12))


def attend_back(me, proj, lse, mixed, grad_mixed, rows, heads):
    pairs = -(-heads // 2)
    all_rows = 4 * rows
    tiles = heads * 10 * rows * rows
    return pl.pallas_call(
        partial(attend_back_kernel, 2 - heads % 2),
        out_shape=jax.ShapeDtypeStruct((3, all_rows, pairs * 128), BF16),
        grid_spec=pltpu.PrefetchScalarGridSpec(
            num_scalar_prefetch=1,
            grid=(pairs,),
            in_specs=[s for t in range(3) for s in block_specs(rows, pairs, t)]
            + block_specs(rows, pairs, 0) * 2
            + [pl.BlockSpec((1, 4, 8, rows), lambda p, m: (p, 0, 0, 0))],
            out_specs=pl.BlockSpec((3, all_rows, 128), lambda p, m: (0, 0, p)),
            scratch_shapes=[pltpu.VMEM((4, rows, 128), F32)] * 2,
        ),
        cost_estimate=pl.CostEstimate(
            flops=tiles * 10 * HP, bytes_accessed=all_rows * pairs * 2048, transcendentals=tiles
        ),
    )(me, *([proj] * 12), *([grad_mixed] * 4), *([mixed] * 4), lse)


def make(sizes):
    wide, parts = sizes["wide"], sizes["narrow"]

    def on_device(
        tokens, lengths, norm_one, qkv_weight, out_weight, norm_two, up_weight, down_weight, grad_out
    ):
        cell_count, rows, width = tokens.shape
        own_width = qkv_weight.shape[2]
        heads = own_width // HS
        pad_heads = heads + heads % 2
        pad_width = pad_heads * HP
        units = up_weight.shape[1]
        chunk = -(-max(width, units) // (wide * 16)) * 16
        tall = chunk * wide
        narrow, ring = Narrow(parts), Ring(wide)
        me = lax.axis_index("narrow")
        length = lengths[0]
        own_tokens, own_grad = tokens[0], grad_out[0]
        me_ref = me.reshape(1).astype(jnp.int32)
        own_live = (me * rows + lax.broadcasted_iota(jnp.int32, (rows, 1), 0) < length).astype(F32)

        token_blocks = narrow.gather(own_tokens)
        own_branch = (own_live * own_grad.astype(F32)).astype(BF16)
        out_own, own_branch, token_blocks = lax.optimization_barrier((out_weight, own_branch, token_blocks))
        out_blocks = narrow.gather(out_own)
        grad_blocks = narrow.gather(own_branch)

        def pad_cols(weight):
            split = weight.reshape(width, heads, HS)
            return jnp.pad(split, ((0, 0), (0, pad_heads - heads), (0, HP - HS))).reshape(width, pad_width)

        def pad_rows(weight):
            split = weight.reshape(heads, HS, width)
            return jnp.pad(split, ((0, pad_heads - heads), (0, HP - HS), (0, 0))).reshape(pad_width, width)

        proj = jnp.concatenate([pad_cols(qkv_weight[t]) for t in range(3)], axis=1)
        stream = own_tokens.astype(F32)
        normal_one, rstd_one = layer_stats(stream)
        rows_one = jnp.concatenate(
            [(layer_stats(b.astype(F32))[0] * norm_one).astype(BF16) for b in token_blocks], axis=0
        )
        projected = dot(rows_one, proj, ((1,), (0,))).astype(BF16)
        mixed, lse = attend(me_ref, projected, rows, heads)
        mixed_parts = narrow.exchange([mixed[k * rows : (k + 1) * rows] for k in range(4)])
        mixed_own = jnp.concatenate(mixed_parts, axis=1)
        out_all = jnp.concatenate([pad_rows(b) for b in out_blocks], axis=0)
        middle = stream + own_live * dot(mixed_own, out_all, ((1,), (0,)))
        normal_two, rstd_two = layer_stats(middle)
        rows_two = jnp.concatenate(narrow.gather((normal_two * norm_two).astype(BF16)), axis=0)
        grad_rows = jnp.concatenate(grad_blocks, axis=0)
        pre_act = dot(rows_two, up_weight, ((1,), (0,)))
        grad_hidden = dot(grad_rows, down_weight, ((1,), (1,)))
        cdf = 0.5 * (1.0 + lax.erf(pre_act * 0.5**0.5))
        slope = cdf + pre_act * jnp.exp(-0.5 * pre_act * pre_act) * (0.5 / jnp.pi) ** 0.5
        hidden = (pre_act * cdf).astype(BF16)
        grad_pre = (grad_hidden * slope).astype(BF16)

        def ring_form(left, right):
            left = jnp.pad(left, ((0, 0), (0, tall - left.shape[1])))
            return dot(left, right, ((0,), (0,))).astype(BF16).reshape(wide, chunk, right.shape[1])

        down_sum = ring.total(ring_form(hidden, grad_rows), 1)
        up_sum = ring.total(ring_form(rows_two, grad_pre), -1)
        terms_two = dot(grad_pre, up_weight, ((1,), (1,)))
        grad_normed_two = narrow.scatter_sum(terms_two, rows)
        mlp_terms = dot(hidden, down_weight, ((1,), (0,)))
        mlp_own = narrow.scatter_sum(mlp_terms, rows)
        block_output = (middle + own_live * mlp_own).astype(BF16)

        gain_two = jnp.sum(grad_normed_two * normal_two, axis=0)
        grad_middle = own_grad.astype(F32) + layer_back(grad_normed_two * norm_two, normal_two, rstd_two)
        grad_attn = (own_live * grad_middle).astype(BF16)
        grad_all = dot(grad_attn, out_all, ((1,), (1,))).astype(BF16)
        grad_mixed = jnp.concatenate(
            narrow.exchange([grad_all[:, k * pad_width : (k + 1) * pad_width] for k in range(4)]), axis=0
        )
        attn_rows = jnp.concatenate(narrow.gather(grad_attn), axis=0)
        grad_parts = attend_back(me_ref, projected, lse, mixed, grad_mixed, rows, heads)
        grad_proj = jnp.concatenate([grad_parts[t] for t in range(3)], axis=1)
        terms_one = dot(grad_proj, proj, ((1,), (1,)))
        grad_normed_one = narrow.scatter_sum(terms_one, rows)
        gain_one = jnp.sum(grad_normed_one * normal_one, axis=0)
        grad_stream = layer_back(grad_normed_one * norm_one, normal_one, rstd_one)
        input_grad = (grad_middle + grad_stream).astype(BF16)

        live_width = heads * HP
        left = jnp.concatenate(
            [grad_proj[:, t * pad_width : t * pad_width + live_width] for t in range(3)], axis=1
        )
        last = jnp.concatenate(
            [
                dot(left, rows_one, ((0,), (0,))).astype(BF16),
                dot(mixed[:, :live_width], attn_rows, ((0,), (0,))).astype(BF16),
            ],
            axis=0,
        )
        tail = -(-last.shape[0] // (wide * 16)) * 16
        last = jnp.pad(last, ((0, tail * wide - last.shape[0]), (0, 0))).reshape(wide, tail, width)
        half = tail // 2
        last_sum = jnp.concatenate(
            [ring.total(last[:, :half], 1), ring.total(last[:, half:], -1)], axis=1
        ).reshape(tail * wide, width)

        gains = jnp.stack([gain_one, gain_two])
        for k in (1, 2):
            gains = gains + narrow.send(gains, k)
        hop = 1
        while hop < wide:
            gains = gains + lax.ppermute(gains, "wide", [(i, i ^ hop) for i in range(wide)])
            hop *= 2

        split = last_sum[: 4 * live_width].reshape(4, heads, HP, width)[:, :, :HS]
        qkv_grad = split[:3].reshape(3, own_width, width).transpose(0, 2, 1)
        out_grad = split[3].reshape(own_width, width)
        down_grad = down_sum.reshape(tall, width)[:units]
        up_grad = up_sum.reshape(tall, units)[:width]
        return (
            block_output[None],
            input_grad[None],
            gains[0],
            qkv_grad,
            out_grad,
            gains[1],
            up_grad,
            down_grad,
        )

    return on_device


def solution(mesh):
    in_specs = (
        P("wide", "narrow", None),
        P("wide"),
        P(),
        P(None, None, "narrow"),
        P("narrow", None),
        P(),
        P(None, "narrow"),
        P("narrow", None),
        P("wide", "narrow", None),
    )
    out_specs = (
        P("wide", "narrow", None),
        P("wide", "narrow", None),
        P(),
        P(None, None, "narrow"),
        P("narrow", None),
        P(),
        P(None, "narrow"),
        P("narrow", None),
    )
    return jax.shard_map(
        make(dict(mesh.shape)), mesh=mesh, in_specs=in_specs, out_specs=out_specs, check_vma=False
    )
```

profile of v0, /device:TPU:0, one launch (start us, length us, event | category | flops | bytes accessed | tf_op | source)
XLA Modules:
  0.0 393.2 jit_solution(1277539659124284074)
XLA Ops:
  9.3 8.4 %collective-permute-done.1 = bf16[256,1120]{0,1:T(8,128)(2,1)} collective-permute-done((bf16[256,1120]{0,1:T(8,128)(2,1)}, bf16[256,1120]{0,1:T(8,128)(2,1)}, u32[]{:S(2)}, u32[]{:S(2)}) %collective-permute-start.1) | collective-permute-done | bytes 573472 | tf_op jit(solution)/shard_map/ppermute | solution.py:39
  29.4 7.5 %collective-permute-done.7 = bf16[280,1120]{1,0:T(8,128)(2,1)} collective-permute-done((bf16[280,1120]{1,0:T(8,128)(2,1)}, bf16[280,1120]{1,0:T(8,128)(2,1)}, u32[]{:S(2)}, u32[]{:S(2)}) %collective-permute-start.7) | collective-permute-done | bytes 627232 | tf_op jit(solution)/shard_map/ppermute | solution.py:39
  37.0 5.1 %convolution_convert_fusion.2.refs_0_.refs_1_.refs_2_.refs_3_.refs_4_.refs_5_.refs_6_.refs_7_.refs_8_.refs_9_.refs_10_.refs_11_ = bf16[1024,1152]{1,0:T(8,128)(2,1)} fusion(bf16[1120,384]{0,1:T(8,128)(2,1)S(1)} %bitcast.290, bf16[1120,384]{0,1:T(8,128)(2,1)S(1)} %bitcast.292, bf16[1120,384]{0,1:T(8,128)(2,1)S(1)} %bitcast.294, ...), kind=kOutput, calls=%fused_computation.12 | convolution fusion | flops 2660507648 | bytes 7233536 | tf_op jit(solution)/shard_map/dot_general | solution.py:31
  42.1 11.0 %shard_map.152 = (bf16[1024,384]{1,0:T(8,128)(2,1)}, f32[3,4,8,256]{3,2,1,0:T(8,128)}) custom-call(s32[1]{0:T(128)} %bitcast.2.me_ref, bf16[1024,1152]{1,0:T(8,128)(2,1)} %convolution_convert_fusion.2.refs_0_.refs_1_.refs_2_.refs_3_.refs_4_.refs_5_.refs_6_.refs_7_.refs_8_.refs_9_.refs_10_.refs_11_, ...), custom_call_target="tpu_custom_call" | custom-call | flops 838860800 | bytes 3145728 | tf_op jit(solution)/shard_map/pallas_call | solution.py:217
  70.7 8.2 %collective-permute-done.15 = bf16[256,1120]{0,1:T(8,128)(2,1)S(1)} collective-permute-done((bf16[256,1120]{0,1:T(8,128)(2,1)S(1)}, bf16[256,1120]{0,1:T(8,128)(2,1)S(1)}, u32[]{:S(2)}, u32[]{:S(2)}) %collective-permute-start.15) | collective-permute-done | bytes 573472 | tf_op jit(solution)/shard_map/ppermute | solution.py:39
  79.6 11.1 %collective-permute-done.10 = bf16[256,1120]{0,1:T(8,128)(2,1)S(1)} collective-permute-done((bf16[256,1120]{0,1:T(8,128)(2,1)S(1)}, bf16[256,1120]{0,1:T(8,128)(2,1)S(1)}, u32[]{:S(2)}, u32[]{:S(2)}) %collective-permute-start.10) | collective-permute-done | bytes 573472 | tf_op jit(solution)/shard_map/ppermute | solution.py:39
  96.5 5.2 %fusion.131 = (bf16[1024,1120]{0,1:T(8,128)(2,1)S(1)}, f32[1024,1120]{0,1:T(8,128)}) fusion(bf16[1024,1120]{0,1:T(8,128)(2,1)S(1)} %get-tuple-element.74, bf16[1120,1120]{1,0:T(8,128)(2,1)S(1)} %copy-done.37), kind=kOutput, calls=%fused_computation.263 | convolution fusion | flops 2570158080 | bytes 11683840 | tf_op jit(solution)/shard_map/dot_general | solution.py:31
  101.7 4.4 %convolution_convert_fusion = bf16[1152,1120]{0,1:T(8,128)(2,1)} fusion(bf16[1024,1120]{0,1:T(8,128)(2,1)S(1)} %constant_dynamic-update-slice_fusion, bf16[1024,1120]{0,1:T(8,128)(2,1)S(1)} %get-tuple-element.74), kind=kOutput, calls=%fused_computation | convolution fusion | flops 2643701760 | bytes 7168000 | tf_op jit(solution)/shard_map/dot_general | solution.py:31
  106.1 4.3 %fusion.4 = bf16[1024,1120]{0,1:T(8,128)(2,1)S(1)} fusion(f32[1024,1120]{0,1:T(8,128)S(1)} %get-tuple-element.75, bf16[1120,1120]{1,0:T(8,128)(2,1)S(1)} %copy-done.37, bf16[1024,1120]{0,1:T(8,128)(2,1)S(1)} %constant_dynamic-update-slice_fusion), kind=kOutput, calls=%fused_computation.11 | convolution fusion | flops 2580480000 | bytes 11683840 | tf_op jit(solution)/shard_map/dot_general | solution.py:31
  110.5 4.8 %fusion.130 = (bf16[1024,1120]{0,1:T(8,128)(2,1)S(1)}, f32[1024,1120]{0,1:T(8,128)}) fusion(bf16[1120,1120]{1,0:T(8,128)(2,1)S(1)} %copy-done, bf16[1024,1120]{0,1:T(8,128)(2,1)S(1)} %fusion.4), kind=kOutput, calls=%fused_computation.262 | convolution fusion | flops 2570158080 | bytes 11683840 | tf_op jit(solution)/shard_map/dot_general | solution.py:31
  139.5 5.6 %collective-permute-done.74 = bf16[144,1120]{1,0:T(8,128)(2,1)S(1)} collective-permute-done((bf16[144,1120]{1,0:T(8,128)(2,1)S(1)}, bf16[144,1120]{1,0:T(8,128)(2,1)S(1)}, u32[]{:S(2)}, u32[]{:S(2)}) %collective-permute-start.74) | collective-permute-done | bytes 322592 | tf_op jit(solution)/shard_map/ppermute | solution.py:72
  148.9 6.6 %collective-permute-done.75 = bf16[144,1120]{1,0:T(8,128)(2,1)S(1)} collective-permute-done((bf16[144,1120]{1,0:T(8,128)(2,1)S(1)}, bf16[144,1120]{1,0:T(8,128)(2,1)S(1)}, u32[]{:S(2)}, u32[]{:S(2)}) %collective-permute-start.75) | collective-permute-done | bytes 322592 | tf_op jit(solution)/shard_map/ppermute | solution.py:72
  158.8 6.2 %collective-permute-done.76 = bf16[144,1120]{1,0:T(8,128)(2,1)S(1)} collective-permute-done((bf16[144,1120]{1,0:T(8,128)(2,1)S(1)}, bf16[144,1120]{1,0:T(8,128)(2,1)S(1)}, u32[]{:S(2)}, u32[]{:S(2)}) %collective-permute-start.76) | collective-permute-done | bytes 322592 | tf_op jit(solution)/shard_map/ppermute | solution.py:72
  176.8 5.1 %collective-permute-done.64 = bf16[144,1120]{1,0:T(8,128)(2,1)S(1)} collective-permute-done((bf16[144,1120]{1,0:T(8,128)(2,1)S(1)}, bf16[144,1120]{1,0:T(8,128)(2,1)S(1)}, u32[]{:S(2)}, u32[]{:S(2)}) %collective-permute-start.64) | collective-permute-done | bytes 322592 | tf_op jit(solution)/shard_map/ppermute | solution.py:72
  187.3 7.0 %collective-permute-done.13 = bf16[256,1120]{0,1:T(8,128)(2,1)S(1)} collective-permute-done((bf16[256,1120]{0,1:T(8,128)(2,1)S(1)}, bf16[256,1120]{0,1:T(8,128)(2,1)S(1)}, u32[]{:S(2)}, u32[]{:S(2)}) %collective-permute-start.13) | collective-permute-done | bytes 573472 | tf_op jit(solution)/shard_map/ppermute | solution.py:39
  196.7 5.6 %convolution_convert_fusion.5 = bf16[256,1536]{1,0:T(8,128)(2,1)S(1)} fusion(bf16[256,1120]{0,1:T(8,128)(2,1)} %get-tuple-element.56, bf16[384,1120]{1,0:T(8,128)(2,1)S(1)} %bitcast.303, bf16[384,1120]{1,0:T(8,128)(2,1)S(1)} %bitcast.299, bf16[384,1120]{1,0:T(8,128)(2,1)S(1)} %bitcast.301, bf16[384,1120]{1,0:T(8,128)(2,1)S(1)} %bitcast.297), kind=kOutput, calls=%fused_computation.20 | convolution fusion | flops 894959616 | bytes 4800512 | tf_op jit(solution)/shard_map/dot_general | solution.py:31
  215.1 15.6 %shard_map.153 = bf16[3,1024,384]{2,1,0:T(8,128)(2,1)} custom-call(s32[1]{0:T(128)} %bitcast.2.me_ref, bf16[1024,1152]{1,0:T(8,128)(2,1)} %convolution_convert_fusion.2.refs_0_.refs_1_.refs_2_.refs_3_.refs_4_.refs_5_.refs_6_.refs_7_.refs_8_.refs_9_.refs_10_.refs_11_, ...), custom_call_target="tpu_custom_call" | custom-call | flops 2097152000 | bytes 6291456 | tf_op jit(solution)/shard_map/pallas_call | solution.py:242
  245.7 7.0 %collective-permute-done.66 = bf16[144,1120]{1,0:T(8,128)(2,1)S(1)} collective-permute-done((bf16[144,1120]{1,0:T(8,128)(2,1)S(1)}, bf16[144,1120]{1,0:T(8,128)(2,1)S(1)}, u32[]{:S(2)}, u32[]{:S(2)}) %collective-permute-start.66) | collective-permute-done | bytes 322592 | tf_op jit(solution)/shard_map/ppermute | solution.py:72
  257.8 5.7 %collective-permute-done.67 = bf16[144,1120]{1,0:T(8,128)(2,1)S(1)} collective-permute-done((bf16[144,1120]{1,0:T(8,128)(2,1)S(1)}, bf16[144,1120]{1,0:T(8,128)(2,1)S(1)}, u32[]{:S(2)}, u32[]{:S(2)}) %collective-permute-start.67) | collective-permute-done | bytes 322592 | tf_op jit(solution)/shard_map/ppermute | solution.py:83
  292.5 5.6 %collective-permute-done.48 = bf16[80,1120]{1,0:T(8,128)(2,1)S(1)} collective-permute-done((bf16[80,1120]{1,0:T(8,128)(2,1)S(1)}, bf16[80,1120]{1,0:T(8,128)(2,1)S(1)}, u32[]{:S(2)}, u32[]{:S(2)}) %collective-permute-start.48) | collective-permute-done | bytes 179232 | tf_op jit(solution)/shard_map/ppermute | solution.py:72
  334.5 5.4 %collective-permute-done.52 = bf16[80,1120]{1,0:T(8,128)(2,1)S(1)} collective-permute-done((bf16[80,1120]{1,0:T(8,128)(2,1)S(1)}, bf16[80,1120]{1,0:T(8,128)(2,1)S(1)}, u32[]{:S(2)}, u32[]{:S(2)}) %collective-permute-start.52) | collective-permute-done | bytes 179232 | tf_op jit(solution)/shard_map/ppermute | solution.py:72
  349.4 5.4 %collective-permute-done.54 = bf16[80,1120]{1,0:T(8,128)(2,1)S(1)} collective-permute-done((bf16[80,1120]{1,0:T(8,128)(2,1)S(1)}, bf16[80,1120]{1,0:T(8,128)(2,1)S(1)}, u32[]{:S(2)}, u32[]{:S(2)}) %collective-permute-start.54) | collective-permute-done | bytes 179232 | tf_op jit(solution)/shard_map/ppermute | solution.py:83
  364.6 5.0 %collective-permute-done.56 = bf16[80,1120]{1,0:T(8,128)(2,1)S(1)} collective-permute-done((bf16[80,1120]{1,0:T(8,128)(2,1)S(1)}, bf16[80,1120]{1,0:T(8,128)(2,1)S(1)}, u32[]{:S(2)}, u32[]{:S(2)}) %collective-permute-start.56) | collective-permute-done | bytes 179232 | tf_op jit(solution)/shard_map/ppermute | solution.py:83
  372.0 4.6 %collective-permute-done.57 = bf16[80,1120]{1,0:T(8,128)(2,1)S(1)} collective-permute-done((bf16[80,1120]{1,0:T(8,128)(2,1)S(1)}, bf16[80,1120]{1,0:T(8,128)(2,1)S(1)}, u32[]{:S(2)}, u32[]{:S(2)}) %collective-permute-start.57) | collective-permute-done | bytes 179232 | tf_op jit(solution)/shard_map/ppermute | solution.py:83
  (391 shorter events, 229.8 us)
Async XLA Ops:
  0.7 19.0 %collective-permute-start = (bf16[256,1120]{0,1:T(8,128)(2,1)}, bf16[256,1120]{0,1:T(8,128)(2,1)}, u32[]{:S(2)}, u32[]{:S(2)}) collective-permute-start(bf16[256,1120]{0,1:T(8,128)(2,1)} %bitcast.257), channel_id=1, source_target_pairs={{0,1},{1,0},{2,3},{3,2},{4,5},{5,4},{6,7},{7,6},{8,9},{9,8},{10,11... | collective-permute-start | bytes 1720328 | tf_op jit(solution)/shard_map/ppermute | solution.py:39
  1.2 16.5 %collective-permute-start.1 = (bf16[256,1120]{0,1:T(8,128)(2,1)}, bf16[256,1120]{0,1:T(8,128)(2,1)}, u32[]{:S(2)}, u32[]{:S(2)}) collective-permute-start(bf16[256,1120]{0,1:T(8,128)(2,1)} %bitcast.258), channel_id=1, source_target_pairs={{0,2},{1,3},{2,0},{3,1},{4,6},{5,7},{6,4},{7,5},{8,10},{9,11},{10,... | collective-permute-start | bytes 1720328 | tf_op jit(solution)/shard_map/ppermute | solution.py:39
  19.9 17.1 %collective-permute-start.7 = (bf16[280,1120]{1,0:T(8,128)(2,1)}, bf16[280,1120]{1,0:T(8,128)(2,1)}, u32[]{:S(2)}, u32[]{:S(2)}) collective-permute-start(bf16[280,1120]{1,0:T(8,128)(2,1)} %param.13), channel_id=1, source_target_pairs={{0,2},{1,3},{2,0},{3,1},{4,6},{5,7},{6,4},{7,5},{8,10},{9,11},{10,... | collective-permute-start | bytes 1881608 | tf_op jit(solution)/shard_map/ppermute | solution.py:39
  21.6 37.7 %collective-permute-start.6 = (bf16[280,1120]{1,0:T(8,128)(2,1)}, bf16[280,1120]{1,0:T(8,128)(2,1)}, u32[]{:S(2)}, u32[]{:S(2)}) collective-permute-start(bf16[280,1120]{1,0:T(8,128)(2,1)} %param.13), channel_id=1, source_target_pairs={{0,1},{1,0},{2,3},{3,2},{4,5},{5,4},{6,7},{7,6},{8,9},{9,8},{10,11... | collective-permute-start | bytes 1881608 | tf_op jit(solution)/shard_map/ppermute | solution.py:39
  37.0 24.1 %collective-permute-start.8 = (bf16[280,1120]{1,0:T(8,128)(2,1)}, bf16[280,1120]{1,0:T(8,128)(2,1)}, u32[]{:S(2)}, u32[]{:S(2)}) collective-permute-start(bf16[280,1120]{1,0:T(8,128)(2,1)} %collective-permute-done.7), channel_id=1, source_target_pairs={{0,1},{1,0},{2,3},{3,2},{4,5},{5,4},{6,7},{7,6},{8,9},{9,8},{10,11... | collective-permute-start | bytes 1881608 | tf_op jit(solution)/shard_map/ppermute | solution.py:39
  59.4 31.3 %collective-permute-start.14 = (bf16[256,1120]{0,1:T(8,128)(2,1)S(1)}, bf16[256,1120]{0,1:T(8,128)(2,1)S(1)}, u32[]{:S(2)}, u32[]{:S(2)}) collective-permute-start(bf16[256,1120]{0,1:T(8,128)(2,1)S(1)} %copy-done.12), channel_id=1, source_target_pairs={{0,1},{1,0},{2,3},{3,2},{4,5},{5,4},{6,7},{7,6},{8,9},{9,8},{10,11... | collective-permute-start | bytes 1720328 | tf_op jit(solution)/shard_map/ppermute | solution.py:39
  61.1 17.8 %collective-permute-start.15 = (bf16[256,1120]{0,1:T(8,128)(2,1)S(1)}, bf16[256,1120]{0,1:T(8,128)(2,1)S(1)}, u32[]{:S(2)}, u32[]{:S(2)}) collective-permute-start(bf16[256,1120]{0,1:T(8,128)(2,1)S(1)} %copy-done.12), channel_id=1, source_target_pairs={{0,2},{1,3},{2,0},{3,1},{4,6},{5,7},{6,4},{7,5},{8,10},{9,11},{10,... | collective-permute-start | bytes 1720328 | tf_op jit(solution)/shard_map/ppermute | solution.py:39
  68.6 22.0 %collective-permute-start.10 = (bf16[256,1120]{0,1:T(8,128)(2,1)S(1)}, bf16[256,1120]{0,1:T(8,128)(2,1)S(1)}, u32[]{:S(2)}, u32[]{:S(2)}) collective-permute-start(bf16[256,1120]{0,1:T(8,128)(2,1)S(1)} %multiply_convert_fusion.2), channel_id=1, source_target_pairs={{0,2},{1,3},{2,0},{3,1},{4,6},{5,7},{6,4},{7,5},{8,10},{9,11},{10,... | collective-permute-start | bytes 1720328 | tf_op jit(solution)/shard_map/ppermute | solution.py:39
  116.4 50.1 %collective-permute-start.17 = (bf16[512,1120]{0,1:T(8,128)(2,1)}, bf16[512,1120]{0,1:T(8,128)(2,1)}, u32[]{:S(2)}, u32[]{:S(2)}) collective-permute-start(bf16[512,1120]{0,1:T(8,128)(2,1)} %pad_maximum_fusion.7), channel_id=1, source_target_pairs={{0,1},{1,0},{2,3},{3,2},{4,5},{5,4},{6,7},{7,6},{8,9},{9,8},{10,11... | collective-permute-start | bytes 3440648 | tf_op jit(solution)/shard_map/ppermute | solution.py:39
  130.4 40.8 %collective-permute-start.12 = (bf16[512,1120]{0,1:T(8,128)(2,1)}, bf16[512,1120]{0,1:T(8,128)(2,1)}, u32[]{:S(2)}, u32[]{:S(2)}) collective-permute-start(bf16[512,1120]{0,1:T(8,128)(2,1)} %pad_maximum_fusion.6), channel_id=1, source_target_pairs={{0,1},{1,0},{2,3},{3,2},{4,5},{5,4},{6,7},{7,6},{8,9},{9,8},{10,11... | collective-permute-start | bytes 3440648 | tf_op jit(solution)/shard_map/ppermute | solution.py:39
  157.1 16.4 %collective-permute-start.63 = (bf16[144,1120]{1,0:T(8,128)(2,1)S(1)}, bf16[144,1120]{1,0:T(8,128)(2,1)S(1)}, u32[]{:S(2)}, u32[]{:S(2)}) collective-permute-start(bf16[144,1120]{1,0:T(8,128)(2,1)S(1)} %fusion.87), channel_id=1, source_target_pairs={{8,0},{16,8},{24,16},{28,24},{20,28},{12,20},{4,12},{0,4},{9,1},{1... | collective-permute-start | bytes 967688 | tf_op jit(solution)/shard_map/ppermute | solution.py:72
  173.0 21.3 %collective-permute-start.13 = (bf16[256,1120]{0,1:T(8,128)(2,1)S(1)}, bf16[256,1120]{0,1:T(8,128)(2,1)S(1)}, u32[]{:S(2)}, u32[]{:S(2)}) collective-permute-start(bf16[256,1120]{0,1:T(8,128)(2,1)S(1)} %fusion.63), channel_id=1, source_target_pairs={{0,2},{1,3},{2,0},{3,1},{4,6},{5,7},{6,4},{7,5},{8,10},{9,11},{10,... | collective-permute-start | bytes 1720328 | tf_op jit(solution)/shard_map/ppermute | solution.py:39
  176.3 28.0 %collective-permute-start.78 = (bf16[144,1120]{1,0:T(8,128)(2,1)S(1)}, bf16[144,1120]{1,0:T(8,128)(2,1)S(1)}, u32[]{:S(2)}, u32[]{:S(2)}) collective-permute-start(bf16[144,1120]{1,0:T(8,128)(2,1)S(1)} %fusion.79), channel_id=1, source_target_pairs={{0,8},{8,16},{16,24},{24,28},{28,20},{20,12},{12,4},{4,0},{1,9},{9... | collective-permute-start | bytes 967688 | tf_op jit(solution)/shard_map/ppermute | solution.py:72
  181.9 59.3 %collective-permute-start.65 = (bf16[144,1120]{1,0:T(8,128)(2,1)S(1)}, bf16[144,1120]{1,0:T(8,128)(2,1)}, u32[]{:S(2)}, u32[]{:S(2)}) collective-permute-start(bf16[144,1120]{1,0:T(8,128)(2,1)S(1)} %fusion.85), channel_id=1, source_target_pairs={{8,0},{16,8},{24,16},{28,24},{20,28},{12,20},{4,12},{0,4},{9,1},{1... | collective-permute-start | bytes 967688 | tf_op jit(solution)/shard_map/ppermute | solution.py:72
  206.1 37.9 %collective-permute-start.79 = (bf16[144,1120]{1,0:T(8,128)(2,1)}, bf16[144,1120]{1,0:T(8,128)(2,1)}, u32[]{:S(2)}, u32[]{:S(2)}) collective-permute-start(bf16[144,1120]{1,0:T(8,128)(2,1)} %fusion.78), channel_id=1, source_target_pairs={{0,8},{8,16},{16,24},{24,28},{28,20},{20,12},{12,4},{4,0},{1,9},{9... | collective-permute-start | bytes 967688 | tf_op jit(solution)/shard_map/ppermute | solution.py:72
  209.5 48.3 %collective-permute-start.30 = (bf16[256,1120]{0,1:T(8,128)(2,1)}, bf16[256,1120]{0,1:T(8,128)(2,1)}, u32[]{:S(2)}, u32[]{:S(2)}) collective-permute-start(bf16[256,1120]{0,1:T(8,128)(2,1)} %get-tuple-element.56), channel_id=1, source_target_pairs={{0,2},{1,3},{2,0},{3,1},{4,6},{5,7},{6,4},{7,5},{8,10},{9,11},{10,... | collective-permute-start | bytes 1720328 | tf_op jit(solution)/shard_map/ppermute | solution.py:39
  214.1 52.8 %collective-permute-start.29 = (bf16[256,1120]{0,1:T(8,128)(2,1)}, bf16[256,1120]{0,1:T(8,128)(2,1)}, u32[]{:S(2)}, u32[]{:S(2)}) collective-permute-start(bf16[256,1120]{0,1:T(8,128)(2,1)} %get-tuple-element.56), channel_id=1, source_target_pairs={{0,1},{1,0},{2,3},{3,2},{4,5},{5,4},{6,7},{7,6},{8,9},{9,8},{10,11... | collective-permute-start | bytes 1720328 | tf_op jit(solution)/shard_map/ppermute | solution.py:39
  236.6 44.8 %collective-permute-start.22 = (bf16[512,1120]{0,1:T(8,128)(2,1)S(1)}, bf16[512,1120]{0,1:T(8,128)(2,1)S(1)}, u32[]{:S(2)}, u32[]{:S(2)}) collective-permute-start(bf16[512,1120]{0,1:T(8,128)(2,1)S(1)} %pad_maximum_fusion.8), channel_id=1, source_target_pairs={{0,1},{1,0},{2,3},{3,2},{4,5},{5,4},{6,7},{7,6},{8,9},{9,8},{10,11... | collective-permute-start | bytes 3440648 | tf_op jit(solution)/shard_map/ppermute | solution.py:39
  281.9 21.5 %collective-permute-start.23 = (bf16[256,1120]{0,1:T(8,128)(2,1)S(1)}, bf16[256,1120]{0,1:T(8,128)(2,1)S(1)}, u32[]{:S(2)}, u32[]{:S(2)}) collective-permute-start(bf16[256,1120]{0,1:T(8,128)(2,1)S(1)} %fusion.59), channel_id=1, source_target_pairs={{0,2},{1,3},{2,0},{3,1},{4,6},{5,7},{6,4},{7,5},{8,10},{9,11},{10,... | collective-permute-start | bytes 1720328 | tf_op jit(solution)/shard_map/ppermute | solution.py:39
  284.7 16.5 %collective-permute-start.70 = (bf16[144,1120]{1,0:T(8,128)(2,1)S(1)}, bf16[144,1120]{1,0:T(8,128)(2,1)S(1)}, u32[]{:S(2)}, u32[]{:S(2)}) collective-permute-start(bf16[144,1120]{1,0:T(8,128)(2,1)S(1)} %collective-permute-done.69), channel_id=1, source_target_pairs={{8,0},{16,8},{24,16},{28,24},{20,28},{12,20},{4,12},{0,4},{9,1},{1... | collective-permute-start | bytes 967688 | tf_op jit(solution)/shard_map/ppermute | solution.py:83
  301.2 26.2 %collective-permute-start.71 = (bf16[144,1120]{1,0:T(8,128)(2,1)S(1)}, bf16[144,1120]{1,0:T(8,128)(2,1)S(1)}, u32[]{:S(2)}, u32[]{:S(2)}) collective-permute-start(bf16[144,1120]{1,0:T(8,128)(2,1)S(1)} %collective-permute-done.70), channel_id=1, source_target_pairs={{8,0},{16,8},{24,16},{28,24},{20,28},{12,20},{4,12},{0,4},{9,1},{1... | collective-permute-start | bytes 967688 | tf_op jit(solution)/shard_map/ppermute | solution.py:83
  302.7 24.8 %collective-permute-start.85 = (bf16[144,1120]{1,0:T(8,128)(2,1)S(1)}, bf16[144,1120]{1,0:T(8,128)(2,1)S(1)}, u32[]{:S(2)}, u32[]{:S(2)}) collective-permute-start(bf16[144,1120]{1,0:T(8,128)(2,1)S(1)} %collective-permute-done.84), channel_id=1, source_target_pairs={{0,8},{8,16},{16,24},{24,28},{28,20},{20,12},{12,4},{4,0},{1,9},{9... | collective-permute-start | bytes 967688 | tf_op jit(solution)/shard_map/ppermute | solution.py:83
  305.8 19.4 %collective-permute-start.50 = (bf16[80,1120]{1,0:T(8,128)(2,1)S(1)}, bf16[80,1120]{1,0:T(8,128)(2,1)S(1)}, u32[]{:S(2)}, u32[]{:S(2)}) collective-permute-start(bf16[80,1120]{1,0:T(8,128)(2,1)S(1)} %fusion.95), channel_id=1, source_target_pairs={{8,0},{16,8},{24,16},{28,24},{20,28},{12,20},{4,12},{0,4},{9,1},{1... | collective-permute-start | bytes 537608 | tf_op jit(solution)/shard_map/ppermute | solution.py:72
  308.1 17.1 %collective-permute-start.36 = (bf16[80,1120]{1,0:T(8,128)(2,1)S(1)}, bf16[80,1120]{1,0:T(8,128)(2,1)S(1)}, u32[]{:S(2)}, u32[]{:S(2)}) collective-permute-start(bf16[80,1120]{1,0:T(8,128)(2,1)S(1)} %fusion.102), channel_id=1, source_target_pairs={{0,8},{8,16},{16,24},{24,28},{28,20},{20,12},{12,4},{4,0},{1,9},{9... | collective-permute-start | bytes 537608 | tf_op jit(solution)/shard_map/ppermute | solution.py:72
  (104 other events, 948.6 us)
where the time goes:
time: 400 us; the launch traced here: 393 us
  waiting for transfers between devices  157 us (39%)
  starting transfers between devices  81.5 us (20%)
  matrix products  47.4 us (12%)
  other arithmetic  40.6 us (10%)
  local copies, waits for them, and re-layouts  36.7 us (9%)
  Pallas kernels  26.6 us (7%)
    ppermute x29, waiting for transfers between devices, send(): return lax.ppermute(value, 'narrow', self.perm[k])  55 us
    ppermute x28, waiting for transfers between devices, reduce(): got = lax.ppermute(current, 'wide', self.perm[way])  52.4 us
    dot_general x12, matrix products, dot(): return lax.dot_general(a, b, (dims, ((), ())), preferred_element_type=F32)  47.4 us
    ppermute x28, waiting for transfers between devices, spread(): current = lax.ppermute(current, 'wide', self.perm[way])  40.4 us
    ppermute x28, starting transfers between devices, reduce(): got = lax.ppermute(current, 'wide', self.perm[way])  31.1 us
    ppermute x28, starting transfers between devices, spread(): current = lax.ppermute(current, 'wide', self.perm[way])  29.2 us
    ppermute x29, starting transfers between devices, send(): return lax.ppermute(value, 'narrow', self.perm[k])  18.9 us
    pallas_call x1, Pallas kernels, attend_back(): pl.pallas_call(partial(attend_back_kernel, 2 - heads % 2), out_shape=jax....  15.6 us
  transfers between devices with their start and end apart: 88, of which 46 were waited for; matrix products, arithmetic and copies ran while one was open for 24% of the time, Pallas kernels for 7%

commit v1 on v0

v1 whole, which is shorter than its diff:
```python
from functools import partial

import jax
import jax.numpy as jnp
from jax import lax
from jax.experimental import pallas as pl
from jax.experimental.pallas import tpu as pltpu
from jax.sharding import PartitionSpec as P

HS = 56
HP = 64
F32 = jnp.float32
BF16 = jnp.bfloat16


def layer_stats(values):
    mean = jnp.mean(values, axis=0, keepdims=True)
    center = values - mean
    spread = jnp.mean(center * center, axis=0, keepdims=True)
    rstd = lax.rsqrt(spread + 1e-05)
    return center * rstd, rstd


def layer_back(grad_scaled, normal, rstd):
    first = jnp.mean(grad_scaled, axis=0, keepdims=True)
    second = jnp.mean(grad_scaled * normal, axis=0, keepdims=True)
    return rstd * (grad_scaled - first - normal * second)


def dot(a, b, dims):
    return lax.dot_general(a, b, (dims, ((), ())), preferred_element_type=F32)


def after(value, *deps):
    return lax.optimization_barrier((value, *deps))[0]


class Narrow:
    def __init__(self, size):
        self.perm = {k: [(i, i ^ k) for i in range(size)] for k in (1, 2, 3)}

    def send(self, value, k):
        return lax.ppermute(value, "narrow", self.perm[k])


class WideSum:
    def __init__(self, size, hops, part):
        self.size, self.hops, self.part, self.rows = size, hops, part, part.shape[0]
        self.step = 0
        index = lax.axis_index("wide")
        bits = [jnp.bitwise_and(index // hop, 1) for hop in hops]
        self.at = jnp.stack(bits).astype(jnp.int32)

    def send(self, value, turn):
        hop = self.hops[turn]
        self.got = lax.ppermute(value, "wide", [(i, i ^ hop) for i in range(self.size)])
        return value

    def advance(self, *deps):
        if self.size != 8:
            if self.step == 0:
                self.whole = lax.psum(self.part.astype(F32), "wide")
            self.step += 1
            return deps[0] if deps else self.part
        got = after(self.got, *deps) if self.step else None
        self.step += 1
        if self.step == 1:
            halves = self.part.reshape(2, self.rows // 2, self.part.shape[1])
            return self.send(lax.dynamic_index_in_dim(halves, 1 - self.at[0], 0, keepdims=False), 0)
        if self.step == 2:
            self.keep, sent = fold(self.at, self.part, got, 1)
            return self.send(sent, 1)
        if self.step == 3:
            self.keep, sent = fold(self.at, self.keep, got, 2)
            return self.send(sent, 2)
        if self.step == 4:
            self.have = (self.keep + got.astype(F32)).astype(BF16)
            return self.send(self.have, 2)
        if self.step == 5:
            self.have = jnp.concatenate([self.have, got], axis=0)
            return self.send(self.have, 1)
        if self.step == 6:
            self.have = jnp.concatenate([self.have, got], axis=0)
            self.send(self.have, 0)
            self.whole = join(self.at, self.have, self.rows, None)
            return self.have
        self.whole = join(self.at, got, self.rows, self.whole)
        return self.whole

    @property
    def done(self):
        return self.step == 7


def fold_kernel(at_ref, keep_ref, sent_ref, got_keep_ref, got_sent_ref, o_keep_ref, o_sent_ref):
    o_keep_ref[...] = keep_ref[...].astype(F32) + got_keep_ref[...].astype(F32)
    o_sent_ref[...] = (sent_ref[...].astype(F32) + got_sent_ref[...].astype(F32)).astype(BF16)


def eighth_of(quarter):
    return -(-quarter // 16) * 8


def fold(at, own, got, turn):
    rows, columns = got.shape
    half = rows // 2 if turn == 1 else eighth_of(rows)
    base = (lambda a: 2 * a[0]) if turn == 1 else (lambda a: 0)
    spec = lambda place: pl.BlockSpec((half, columns), lambda i, a: (place(a), 0))
    return pl.pallas_call(
        fold_kernel,
        out_shape=[
            jax.ShapeDtypeStruct((half, columns), F32),
            jax.ShapeDtypeStruct((half, columns), BF16),
        ],
        grid_spec=pltpu.PrefetchScalarGridSpec(
            num_scalar_prefetch=1,
            grid=(1,),
            in_specs=[
                spec(lambda a: base(a) + a[turn]),
                spec(lambda a: base(a) + 1 - a[turn]),
                spec(lambda a: a[turn]),
                spec(lambda a: 1 - a[turn]),
            ],
            out_specs=[spec(lambda a: 0)] * 2,
        ),
        cost_estimate=pl.CostEstimate(
            flops=rows * columns, bytes_accessed=7 * rows * columns, transcendentals=0
        ),
    )(at, own, own, got, got)


def join_kernel(rows, at_ref, half_ref, *refs):
    o_ref = refs[-1]
    eighth = half_ref.shape[0] // 2
    rest = rows - eighth
    first = at_ref[2] == 0

    @pl.when(first)
    def _():
        o_ref[...] = half_ref[0:rows, :].astype(F32)

    @pl.when(jnp.logical_not(first))
    def _():
        o_ref[0:eighth, :] = half_ref[eighth : 2 * eighth, :].astype(F32)
        o_ref[eighth:rows, :] = half_ref[0:rest, :].astype(F32)


def join(at, half, rows, whole):
    columns, quarter = half.shape[1], rows // 4
    place = (lambda a: a[0]) if whole is None else (lambda a: 1 - a[0])
    return pl.pallas_call(
        partial(join_kernel, quarter),
        out_shape=jax.ShapeDtypeStruct((rows, columns), F32),
        grid_spec=pltpu.PrefetchScalarGridSpec(
            num_scalar_prefetch=1,
            grid=(2,),
            in_specs=[
                pl.BlockSpec((half.shape[0] // 2, columns), lambda i, a: (jnp.bitwise_xor(i, a[1]), 0))
            ]
            + ([] if whole is None else [pl.BlockSpec(memory_space=pl.ANY)]),
            out_specs=pl.BlockSpec((quarter, columns), lambda i, a: (2 * place(a) + i, 0)),
        ),
        input_output_aliases={} if whole is None else {2: 0},
        cost_estimate=pl.CostEstimate(flops=0, bytes_accessed=3 * rows * columns, transcendentals=0),
    )(at, half, *([] if whole is None else [whole]))


LOG2E = 1.4426950408889634
SCALE = HS**-0.5


def nt(a, b):
    return lax.dot_general(a, b, (((1,), (1,)), ((), ())), preferred_element_type=F32)


def nn(a, b):
    return lax.dot_general(a, b, (((1,), (0,)), ((), ())), preferred_element_type=F32)


def half_of(values, which):
    lane = lax.broadcasted_iota(jnp.int32, values.shape, 1)
    keep = lane < HP if which == 0 else lane >= HP
    return jnp.where(keep, values, jnp.zeros_like(values))


def causal_tile(rows):
    key = lax.broadcasted_iota(jnp.int32, (rows, rows), 0)
    query = lax.broadcasted_iota(jnp.int32, (rows, rows), 1)
    return key <= query


def swap_halves(values):
    return pltpu.roll(values.astype(F32), HP, 1).astype(BF16)


def pair_operands(first, second, third, heads):
    if heads == 2:
        return first, second, third
    lone = half_of(second, 0)
    return half_of(first, 0), half_of(swap_halves(first), 0), lone


def attend_kernel(lone_last, me_ref, *refs):
    first, second, third, (o_ref, lse_ref) = refs[0:4], refs[4:8], refs[8:12], refs[12:14]
    me = me_ref[0]
    rows = first[0].shape[0]

    def body(heads):
        tiles = [pair_operands(first[j][...], second[j][...], third[j][...], heads) for j in range(4)]
        value_t = [tiles[j][2].T for j in range(4)]
        causal = causal_tile(rows)
        for a in range(4):
            outs = []
            for h in range(heads):
                query = half_of(tiles[a][0], h)
                score = [nt(tiles[j][1], query) for j in range(a + 1)]
                score[a] = jnp.where(causal, score[a], -1e30)
                top = jnp.max(score[0], axis=0, keepdims=True)
                for j in range(1, a + 1):
                    top = jnp.maximum(top, jnp.max(score[j], axis=0, keepdims=True))
                top = top * (SCALE * LOG2E)
                total = jnp.zeros((1, rows), F32)
                acc = jnp.zeros((HP, rows), F32)
                for j in range(a + 1):
                    p = jnp.exp2(score[j] * (SCALE * LOG2E) - top)
                    total = total + jnp.sum(p, axis=0, keepdims=True)
                    acc = acc + nn(value_t[j][h * HP : (h + 1) * HP], p.astype(BF16))
                outs.append(acc / total)
                lse_ref[0, a, h : h + 1, :] = top + jnp.log2(total)
            if heads == 1:
                outs.append(jnp.zeros((HP, rows), F32))
            at = pl.multiple_of(slot_of(me, a) * rows, rows)
            o_ref[pl.ds(at, rows), :] = jnp.concatenate(outs, axis=0).T.astype(BF16)

    if not lone_last:
        body(2)
        return
    last = pl.num_programs(0) - 1

    @pl.when(pl.program_id(0) < last)
    def _():
        body(2)

    @pl.when(pl.program_id(0) == last)
    def _():
        body(1)


def attend_back_body(heads, me_ref, refs):
    first, second, third, do, o = (refs[4 * i : 4 * i + 4] for i in range(5))
    lse_ref, g_ref, dk_acc, dv_acc = refs[20:24]
    me = me_ref[0]
    rows = first[0].shape[0]
    tiles = [pair_operands(first[j][...], second[j][...], third[j][...], heads) for j in range(4)]
    key_t = [tiles[j][1].T for j in range(4)]
    causal = causal_tile(rows)
    grads_q = []
    for a in range(4):
        grad = do[a][...]
        product = (grad.astype(F32) * o[a][...].astype(F32)).T
        parts = []
        for h in range(heads):
            query, grad_h = half_of(tiles[a][0], h), half_of(grad, h)
            inner = jnp.sum(product[h * HP : (h + 1) * HP], axis=0, keepdims=True)
            lse = lse_ref[0, a, h : h + 1, :]
            dq = jnp.zeros((HP, rows), F32)
            for j in range(a + 1):
                score = nt(tiles[j][1], query) * (SCALE * LOG2E) - lse
                if j == a:
                    score = jnp.where(causal, score, -1e30)
                p = jnp.exp2(score)
                ds = (p * (nt(tiles[j][2], grad_h) - inner)).astype(BF16)
                dv, dk = nn(p.astype(BF16), grad_h), nn(ds, query)
                if a == j and h == 0:
                    dv_acc[j], dk_acc[j] = dv, dk
                else:
                    dv_acc[j] = dv_acc[j] + dv
                    dk_acc[j] = dk_acc[j] + dk
                dq = dq + nn(key_t[j][h * HP : (h + 1) * HP], ds)
            parts.append(dq * SCALE)
        if heads == 1:
            parts.append(jnp.zeros((HP, rows), F32))
        grads_q.append(jnp.concatenate(parts, axis=0).T)
    for j in range(4):
        at = pl.multiple_of(slot_of(me, j) * rows, rows)
        if heads == 2:
            g_ref[pl.ds(at, rows), 0:128] = grads_q[j].astype(BF16)
            g_ref[pl.ds(at, rows), 128:256] = (dk_acc[j] * SCALE).astype(BF16)
            g_ref[pl.ds(at, rows), 256:384] = dv_acc[j].astype(BF16)
        else:
            both = grads_q[j] + pltpu.roll(dk_acc[j] * SCALE, HP, 1)
            g_ref[pl.ds(at, rows), 0:128] = both.astype(BF16)
            g_ref[pl.ds(at, rows), 128:256] = dv_acc[j].astype(BF16)


def attend_back_kernel(lone_last, me_ref, *refs):
    if not lone_last:
        attend_back_body(2, me_ref, refs)
        return
    last = pl.num_programs(0) - 1

    @pl.when(pl.program_id(0) < last)
    def _():
        attend_back_body(2, me_ref, refs)

    @pl.when(pl.program_id(0) == last)
    def _():
        attend_back_body(1, me_ref, refs)


def slot_of(me, block):
    rel = jnp.bitwise_xor(me, block)
    return jnp.bitwise_or((rel & 1) * 2, rel >> 1)


def block_specs(rows, column):
    return [
        pl.BlockSpec((rows, 128), lambda p, m, j=j: (slot_of(m[0], j), column(p))) for j in range(4)
    ]


def attend(me, proj, rows, heads):
    pairs = -(-heads // 2)
    all_rows = 4 * rows
    tiles = heads * 10 * rows * rows
    last_tile = proj.shape[1] // 128 - 1
    return pl.pallas_call(
        partial(attend_kernel, heads % 2 == 1),
        out_shape=(
            jax.ShapeDtypeStruct((all_rows, pairs * 128), BF16),
            jax.ShapeDtypeStruct((pairs, 4, 8, rows), F32),
        ),
        grid_spec=pltpu.PrefetchScalarGridSpec(
            num_scalar_prefetch=1,
            grid=(pairs,),
            in_specs=[
                s
                for t in range(3)
                for s in block_specs(rows, lambda p, t=t: jnp.minimum(3 * p + t, last_tile))
            ],
            out_specs=[
                pl.BlockSpec((all_rows, 128), lambda p, m: (0, p)),
                pl.BlockSpec((1, 4, 8, rows), lambda p, m: (p, 0, 0, 0)),
            ],
        ),
        cost_estimate=pl.CostEstimate(
            flops=tiles * 4 * HP, bytes_accessed=all_rows * pairs * 1024, transcendentals=tiles
        ),
    )(me, *([proj] * 12))


def attend_back(me, proj, lse, mixed, grad_mixed, rows, heads):
    pairs = -(-heads // 2)
    all_rows, columns = proj.shape
    tiles = heads * 10 * rows * rows
    last_tile = columns // 128 - 1
    return pl.pallas_call(
        partial(attend_back_kernel, heads % 2 == 1),
        out_shape=jax.ShapeDtypeStruct((all_rows, columns), BF16),
        grid_spec=pltpu.PrefetchScalarGridSpec(
            num_scalar_prefetch=1,
            grid=(pairs,),
            in_specs=[
                s
                for t in range(3)
                for s in block_specs(rows, lambda p, t=t: jnp.minimum(3 * p + t, last_tile))
            ]
            + block_specs(rows, lambda p: p) * 2
            + [pl.BlockSpec((1, 4, 8, rows), lambda p, m: (p, 0, 0, 0))],
            out_specs=pl.BlockSpec((all_rows, 384), lambda p, m: (0, p)),
            scratch_shapes=[pltpu.VMEM((4, rows, 128), F32)] * 2,
        ),
        cost_estimate=pl.CostEstimate(
            flops=tiles * 10 * HP, bytes_accessed=all_rows * columns * 10, transcendentals=tiles
        ),
    )(me, *([proj] * 12), *([grad_mixed] * 4), *([mixed] * 4), lse)


def make(sizes):
    wide, parts = sizes["wide"], sizes["narrow"]

    def on_device(
        tokens, lengths, norm_one, qkv_weight, out_weight, norm_two, up_weight, down_weight, grad_out
    ):
        cell_count, rows, width = tokens.shape
        own_width = qkv_weight.shape[2]
        heads = own_width // HS
        pairs = -(-heads // 2)
        pad_width = pairs * 128
        narrow = Narrow(parts)
        me = lax.axis_index("narrow")
        me_ref = me.reshape(1).astype(jnp.int32)
        length = lengths[0]
        gain_row_one, gain_row_two = norm_one[:, None], norm_two[:, None]
        own_tokens, own_grad = tokens[0].T, grad_out[0].T
        own_live = (me * rows + lax.broadcasted_iota(jnp.int32, (1, rows), 1) < length).astype(F32)

        tok_y, tok_c = narrow.send(own_tokens, 2), narrow.send(own_tokens, 1)

        full = heads // 2
        split = qkv_weight.transpose(0, 2, 1).reshape(3, heads, HS, width)
        split = jnp.pad(split, ((0, 0), (0, 0), (0, HP - HS), (0, 0)))
        pieces = [split[:, : 2 * full].reshape(3, full, 128, width).transpose(1, 0, 2, 3).reshape(full * 384, width)]
        if heads % 2:
            pieces.append(jnp.pad(split[:, 2 * full].reshape(3 * HP, width), ((0, HP), (0, 0))))
        proj = jnp.concatenate(pieces, axis=0)

        def pad_rows(weight):
            split = weight.reshape(heads, HS, width)
            return jnp.pad(split, ((0, 2 * pairs - heads), (0, HP - HS), (0, 0))).reshape(pad_width, width)

        stream = own_tokens.astype(F32)
        normal_one, rstd_one = layer_stats(stream)

        def first_norm(block):
            return (layer_stats(block.astype(F32))[0] * gain_row_one).astype(BF16)

        near = [first_norm(own_tokens), first_norm(tok_c)]
        tok_y = after(tok_y, proj, *near)
        tok_d = narrow.send(tok_y, 1)
        out_y = narrow.send(after(out_weight, tok_y), 2)
        out_c = narrow.send(after(out_weight, tok_y), 1)
        far_norm = [first_norm(tok_y), first_norm(tok_d)]
        rows_one = jnp.concatenate([near[0], far_norm[0], near[1], far_norm[1]], axis=1)
        projected = dot(rows_one, proj, ((0,), (1,))).astype(BF16)
        own_branch = (own_live * own_grad.astype(F32)).astype(BF16)
        own_branch = after(own_branch, rows_one)
        grad_y, grad_c = narrow.send(own_branch, 2), narrow.send(own_branch, 1)
        mixed, lse = attend(me_ref, projected, rows, heads)
        out_y = after(out_y, mixed)
        out_d = narrow.send(out_y, 1)
        block = lambda a, slot: a[slot * rows : (slot + 1) * rows]
        mixed_y = narrow.send(block(mixed, 1), 2)
        mixed_d = narrow.send(block(mixed, 3), 3)
        mixed_c = narrow.send(block(mixed, 2), 1)
        out_all = [pad_rows(after(b, mixed)) for b in (out_weight, out_y, out_c, out_d)]
        grad_y = after(grad_y, *out_all)
        grad_d = narrow.send(grad_y, 1)
        mixed_y = after(mixed_y, grad_y)
        mixed_own = [block(mixed, 0), mixed_y, mixed_c, mixed_d]
        branch = sum(dot(w, m, ((0,), (1,))) for w, m in zip(out_all, mixed_own))
        middle = stream + own_live * branch
        normal_two, rstd_two = layer_stats(middle)
        own_two = (normal_two * gain_row_two).astype(BF16)
        two_y, two_c = narrow.send(own_two, 2), narrow.send(own_two, 1)
        grad_rows = jnp.concatenate([after(own_branch, own_two), grad_y, grad_c, grad_d], axis=1)
        grad_hidden = dot(down_weight, grad_rows, ((1,), (0,)))
        two_y = after(two_y, grad_hidden)
        two_d = narrow.send(two_y, 1)
        rows_two = jnp.concatenate([own_two, two_y, two_c, two_d], axis=1)
        pre_act = dot(up_weight, rows_two, ((0,), (0,)))
        cdf = 0.5 * (1.0 + lax.erf(pre_act * 0.5**0.5))
        slope = cdf + pre_act * jnp.exp(-0.5 * pre_act * pre_act) * (0.5 / jnp.pi) ** 0.5
        hidden = (pre_act * cdf).astype(BF16)
        grad_pre = (grad_hidden * slope).astype(BF16)

        def wide_sum(hops, part):
            return WideSum(wide, hops, part)

        half = 2 * rows
        down = wide_sum((1, 2, 4), dot(hidden, grad_rows, ((1,), (1,))).astype(BF16))
        mark = down.advance()
        up = wide_sum((2, 1, 4), dot(rows_two, after(grad_pre, mark), ((1,), (1,))).astype(BF16))
        mark = up.advance()

        grad_pre_on = after(grad_pre, mark)
        sent = dot(up_weight, grad_pre_on[:, half:], ((1,), (0,))).astype(BF16)
        got_two = narrow.send(sent, 1)
        kept_two = dot(up_weight, after(grad_pre_on[:, :half], sent), ((1,), (0,)))
        got_two = after(got_two, kept_two).astype(F32)
        far_two = narrow.send((kept_two[:, rows:] + got_two[:, rows:]).astype(BF16), 2)
        near_two = kept_two[:, :rows] + got_two[:, :rows]
        hidden_on = after(hidden, near_two)
        mlp_sent = dot(down_weight, hidden_on[:, half:], ((0,), (0,))).astype(BF16)
        mlp_got = narrow.send(mlp_sent, 1)
        mlp_kept = dot(down_weight, after(hidden_on[:, :half], mlp_sent), ((0,), (0,)))
        mlp_got = after(mlp_got, mlp_kept).astype(F32)
        mlp_far = (mlp_kept[:, rows:] + mlp_got[:, rows:]).astype(BF16)
        mlp_near = mlp_kept[:, :rows] + mlp_got[:, :rows]
        grad_normed_two = near_two + after(far_two, mlp_near, mlp_far).astype(F32)
        gain_two = jnp.sum(grad_normed_two * normal_two, axis=1)
        grad_middle = own_grad.astype(F32) + layer_back(grad_normed_two * gain_row_two, normal_two, rstd_two)
        grad_attn = (own_live * grad_middle).astype(BF16)
        piece = [dot(grad_attn, w, ((0,), (1,))).astype(BF16) for w in out_all]
        mix_y, mix_d, mix_c = narrow.send(piece[1], 2), narrow.send(piece[3], 3), narrow.send(piece[2], 1)
        mark = down.advance(*piece)
        mark = up.advance(mark)
        mix_y = after(mix_y, mark)
        grad_mixed = jnp.concatenate([piece[0], mix_y, mix_c, mix_d], axis=0)
        mark = down.advance(grad_mixed)
        mark = up.advance(mark)
        attn_on = after(grad_attn, mark)
        attn_y, attn_c = narrow.send(attn_on, 2), narrow.send(attn_on, 1)
        grad_proj = attend_back(me_ref, projected, lse, mixed, after(grad_mixed, attn_on), rows, heads)
        attn_y = after(attn_y, grad_proj)
        attn_d = narrow.send(attn_y, 1)
        mlp_send_far = narrow.send(after(mlp_far, attn_y), 2)

        found = dot(grad_proj[:, : 3 * heads * HP], rows_one, ((0,), (1,))).astype(BF16)
        fields = [found[: full * 384].reshape(full, 3, 2, HP, width)[:, :, :, :HS]]
        fields[0] = fields[0].transpose(1, 0, 2, 3, 4).reshape(3, full * 2 * HS, width)
        if heads % 2:
            fields.append(found[full * 384 :].reshape(3, HP, width)[:, :HS])
        qkv_part = jnp.concatenate(fields, axis=1).reshape(3 * own_width, width)
        cut = -(-4 * own_width // 64) * 32
        first = wide_sum((1, 2, 4), qkv_part[:cut])
        mark = first.advance()
        attn_rows = jnp.concatenate([grad_attn, attn_y, attn_c, after(attn_d, mark)], axis=1)
        out_part = dot(mixed[:, : heads * HP], attn_rows, ((0,), (1,))).astype(BF16)
        out_part = out_part.reshape(heads, HP, width)[:, :HS].reshape(own_width, width)
        second = wide_sum((2, 1, 4), jnp.concatenate([qkv_part[cut:], out_part], axis=0))
        mark = second.advance()
        mark = down.advance(mark)
        mark = up.advance(mark)
        grad_proj = after(grad_proj, mark)
        one_sent = dot(proj, grad_proj[half:], ((0,), (1,))).astype(BF16)
        one_got = narrow.send(one_sent, 1)
        one_kept = dot(proj, after(grad_proj[:half], one_sent), ((0,), (1,)))
        one_got = after(one_got, one_kept).astype(F32)
        one_far = narrow.send((one_kept[:, rows:] + one_got[:, rows:]).astype(BF16), 2)
        one_near = one_kept[:, :rows] + one_got[:, :rows]
        mlp_own = mlp_near + after(mlp_send_far, one_near).astype(F32)
        block_output = (middle + own_live * mlp_own).astype(BF16)
        mark = first.advance(block_output)
        mark = second.advance(mark)
        grad_normed_one = one_near + after(one_far, mark).astype(F32)
        gain_one = jnp.sum(grad_normed_one * normal_one, axis=1)
        grad_stream = layer_back(grad_normed_one * gain_row_one, normal_one, rstd_one)
        input_grad = (grad_middle + grad_stream).astype(BF16)
        gains = jnp.stack([gain_one, gain_two])
        mark = down.advance(gains, input_grad)
        mark = up.advance(mark)
        mark = first.advance(mark)
        mark = second.advance(mark)
        for k in (1, 2):
            gains = gains + narrow.send(gains, k)
        for s in (down, up, first, second):
            mark = s.advance(mark, gains)
        hop = 1
        while hop < wide:
            got = lax.ppermute(gains, "wide", [(i, i ^ hop) for i in range(wide)])
            gains = gains + after(got, mark)
            for s in (first, second):
                if not s.done:
                    mark = s.advance(mark, gains)
            hop *= 2
        for s in (down, up, first, second):
            while not s.done:
                mark = s.advance(mark)

        low = 3 * own_width - cut
        qkv_grad = jnp.concatenate([first.whole, second.whole[:low]], axis=0)
        qkv_grad = qkv_grad.reshape(3, own_width, width).transpose(0, 2, 1)
        out_grad = second.whole[low:]
        return (
            block_output.T[None],
            input_grad.T[None],
            gains[0],
            qkv_grad,
            out_grad,
            gains[1],
            up.whole,
            down.whole,
        )

    return on_device


def solution(mesh):
    in_specs = (
        P("wide", "narrow", None),
        P("wide"),
        P(),
        P(None, None, "narrow"),
        P("narrow", None),
        P(),
        P(None, "narrow"),
        P("narrow", None),
        P("wide", "narrow", None),
    )
    out_specs = (
        P("wide", "narrow", None),
        P("wide", "narrow", None),
        P(),
        P(None, None, "narrow"),
        P("narrow", None),
        P(),
        P(None, "narrow"),
        P("narrow", None),
    )
    return jax.shard_map(
        make(dict(mesh.shape)), mesh=mesh, in_specs=in_specs, out_specs=out_specs, check_vma=False
    )
```

time: 400 us -> 382 us (0.955)
  Pallas kernels: 26.6 us -> 76.6 us
  waiting for transfers between devices: 157 us -> 120 us
  starting transfers between devices: 81.5 us -> 53.9 us
  local copies, waits for them, and re-layouts: 36.7 us -> 29.1 us
    pallas_call x2 -> x18, Pallas kernels: 26.6 us -> 76.6 us  [the longest x8 25.1 us: fold(): pl.pallas_call(fold_kernel, out_shape=[jax.ShapeDtypeStruct((half, column...]
    ppermute x59 -> x27, waiting for transfers between devices: 102 us -> 73.7 us  [the longest x24 49.4 us: send(): lax.ppermute(value, 'wide', [(i, i ^ hop) for i in range(self.size)])]
    ppermute x59 -> x27, starting transfers between devices: 62.6 us -> 36.2 us  [the longest x24 31 us: send(): lax.ppermute(value, 'wide', [(i, i ^ hop) for i in range(self.size)])]
    ppermute x29, waiting for transfers between devices: 55 us -> 46.3 us  [send(): return lax.ppermute(value, 'narrow', self.perm[k])]
    unnamed x83 -> x119, local copies, waits for them, and re-layouts: 2.26 us -> 8.84 us
    convert_element_type x2 -> x0, local copies, waits for them, and re-layouts: 6.49 us -> none  [ring_form(): dot(left, right, ((0,), (0,))).astype(BF16)]
    concatenate x7 -> x12, other arithmetic: 5.39 us -> 10.2 us  [the longest x8 6.86 us: advance(): self.have = jnp.concatenate([self.have, got], axis=0)]
    pad x7 -> x4, local copies, waits for them, and re-layouts: 8 us -> 3.9 us  [pad_rows(): jnp.pad(split, ((0, 2 * pairs - heads), (0, HP - HS), (0, 0)))]
  transfers between devices with their start and end apart: 88 -> 56, of which waited for: 46 -> 22; matrix products, arithmetic and copies ran while one was open for 24% -> 22% of each run, Pallas kernels for 7% -> 19%
where the time goes in v1:
time: 382 us; the launch traced here: 375 us
  waiting for transfers between devices  120 us (31%)
  Pallas kernels  76.6 us (20%)
  starting transfers between devices  53.9 us (14%)
  matrix products  50.3 us (13%)
  other arithmetic  42.7 us (11%)
  local copies, waits for them, and re-layouts  29.1 us (8%)
    dot_general x21, matrix products, dot(): return lax.dot_general(a, b, (dims, ((), ())), preferred_element_type=F32)  50.3 us
    ppermute x24, waiting for transfers between devices, send(): lax.ppermute(value, 'wide', [(i, i ^ hop) for i in range(self.size)])  49.4 us
    ppermute x29, waiting for transfers between devices, send(): return lax.ppermute(value, 'narrow', self.perm[k])  46.3 us
    ppermute x24, starting transfers between devices, send(): lax.ppermute(value, 'wide', [(i, i ^ hop) for i in range(self.size)])  31 us
    pallas_call x8, Pallas kernels, fold(): pl.pallas_call(fold_kernel, out_shape=[jax.ShapeDtypeStruct((half, column...  25.1 us
    pallas_call x8, Pallas kernels, join(): pl.pallas_call(partial(join_kernel, quarter), out_shape=jax.ShapeDtypeStr...  24.5 us
    ppermute x3, waiting for transfers between devices, on_device(): got = lax.ppermute(gains, 'wide', [(i, i ^ hop) for i in range(wide)])  24.3 us
    ppermute x29, starting transfers between devices, send(): return lax.ppermute(value, 'narrow', self.perm[k])  17.7 us
  transfers between devices with their start and end apart: 56, of which 22 were waited for; matrix products, arithmetic and copies ran while one was open for 22% of the time, Pallas kernels for 19%

profile of v1, /device:TPU:0, one launch (start us, length us, event | category | flops | bytes accessed | tf_op | source)
XLA Modules:
  0.0 375.4 jit_solution(5487229413630994366)
XLA Ops:
  23.8 4.2 %convolution_convert_fusion.7.refs_0_.refs_1_.refs_2_.refs_3_.refs_4_.refs_5_.refs_6_.refs_7_.refs_8_.refs_9_.refs_10_.refs_11_ = bf16[1024,1024]{1,0:T(8,128)(2,1)} fusion(bf16[1120,256]{1,0:T(8,128)(2,1)S(1)} %get-tuple-element.182, bf16[1120,256]{1,0:T(8,128)(2,1)S(1)} %get-tuple-element.183, bf16[1120,256]{1,0:T(8,128)(2,1)S(1)} %get-tuple-element.181, ...), kind=kOutput, calls=%fused_computation.47 | convolution fusion | flops 2365915136 | bytes 6541312 | tf_op jit(solution)/shard_map/dot_general | solution.py:31
  28.1 11.4 %shard_map.152 = (bf16[1024,384]{1,0:T(8,128)(2,1)}, f32[3,4,8,256]{3,2,1,0:T(8,128)}) custom-call(s32[1]{0:T(128)} %bitcast.3.me_ref, bf16[1024,1024]{1,0:T(8,128)(2,1)} %convolution_convert_fusion.7.refs_0_.refs_1_.refs_2_.refs_3_.refs_4_.refs_5_.refs_6_.refs_7_.refs_8_.refs_9_.refs_10_.refs_11_, ...), custom_call_target="tpu_custom_call" | custom-call | flops 838860800 | bytes 3145728 | tf_op jit(solution)/shard_map/pallas_call | solution.py:327
  50.5 6.1 %collective-permute-done.5 = bf16[1120,256]{1,0:T(8,128)(2,1)S(1)} collective-permute-done((bf16[1120,256]{1,0:T(8,128)(2,1)S(1)}, bf16[1120,256]{1,0:T(8,128)(2,1)S(1)}, u32[]{:S(2)}, u32[]{:S(2)}) %collective-permute-start.5) | collective-permute-done | bytes 573472 | tf_op jit(solution)/shard_map/ppermute | solution.py:43
  56.7 4.2 %collective-permute-done.4 = bf16[256,384]{1,0:T(8,128)(2,1)S(1)} collective-permute-done((bf16[256,384]{1,0:T(8,128)(2,1)S(1)}, bf16[256,384]{1,0:T(8,128)(2,1)S(1)}, u32[]{:S(2)}, u32[]{:S(2)}) %collective-permute-start.4) | collective-permute-done | bytes 196640 | tf_op jit(solution)/shard_map/ppermute | solution.py:43
  68.9 4.7 %convolution_bitcast_fusion = f32[1120,1024]{1,0:T(8,128)} fusion(bf16[1120,1120]{1,0:T(8,128)(2,1)S(1)} %copy-done.56, bf16[1120,1024]{1,0:T(8,128)(2,1)S(1)} %constant_dynamic-update-slice_fusion), kind=kOutput, calls=%fused_computation.17 | convolution fusion | flops 2569011200 | bytes 9390080 | tf_op jit(solution)/shard_map/dot_general | solution.py:31
  73.6 8.6 %collective-permute-done.10 = bf16[1120,256]{1,0:T(8,128)(2,1)} collective-permute-done((bf16[1120,256]{1,0:T(8,128)(2,1)}, bf16[1120,256]{1,0:T(8,128)(2,1)}, u32[]{:S(2)}, u32[]{:S(2)}) %collective-permute-start.10) | collective-permute-done | bytes 573472 | tf_op jit(solution)/shard_map/ppermute | solution.py:43
  84.5 7.2 %fusion.6 = (bf16[1120,1024]{1,0:T(8,128)(2,1)S(1)}, bf16[1120,1024]{1,0:T(8,128)(2,1)S(1)}) fusion(f32[1120,1024]{1,0:T(8,128)} %convolution_bitcast_fusion, bf16[1120,1120]{1,0:T(8,128)(2,1)S(1)} %copy-done, bf16[1120,256]{1,0:T(8,128)(2,1)} %collective-permute-done.14, bf16[1120,256]{1,0:T(8,128)(2,1)} %collective-permute-done.13, ...), kind=kOutput, calls=%fused_computation.10 | convolution fusion | flops 2591948800 | bytes 13977600 | tf_op jit(solution)/shard_map/dot_general | solution.py:31
  91.8 3.6 convolution_convert_fusion.1.keep_ref.sent_ref
  97.3 4.8 %convolution_convert_fusion.keep_ref.sent_ref = bf16[1120,1120]{1,0:T(8,128)(2,1)S(1)} fusion(bf16[1120,1024]{1,0:T(8,128)(2,1)S(1)} %get-tuple-element.98, bf16[1120,256]{1,0:T(8,128)(2,1)} %collective-permute-done.14, bf16[1120,256]{1,0:T(8,128)(2,1)} %collective-permute-done.13, bf16[1120,256]{1,0:T(8,128)(2,1)} %collective-permute-done.10, ...), kind=kOutput, calls=%fused_computation | convolution fusion | flops 2579440640 | bytes 7096320 | tf_op jit(solution)/shard_map/dot_general | solution.py:31
  125.7 7.9 %collective-permute-done.17 = bf16[1120,256]{1,0:T(8,128)(2,1)S(1)} collective-permute-done((bf16[1120,256]{1,0:T(8,128)(2,1)}, bf16[1120,256]{1,0:T(8,128)(2,1)S(1)}, u32[]{:S(2)}, u32[]{:S(2)}) %collective-permute-start.17) | collective-permute-done | bytes 573472 | tf_op jit(solution)/shard_map/ppermute | solution.py:43
  140.0 6.4 %collective-permute-done.19.got_keep_ref.got_sent_ref = bf16[560,1120]{1,0:T(8,128)(2,1)} collective-permute-done((bf16[560,1120]{1,0:T(8,128)(2,1)}, bf16[560,1120]{1,0:T(8,128)(2,1)}, u32[]{:S(2)}, u32[]{:S(2)}) %collective-permute-start.19) | collective-permute-done | bytes 1254432 | tf_op jit(solution)/shard_map/ppermute | solution.py:56
  146.4 3.9 %shard_map.153 = (f32[280,1120]{1,0:T(8,128)}, bf16[280,1120]{1,0:T(8,128)(2,1)}) custom-call(s32[3]{0:T(128)} %add_add_fusion.1.at_ref, bf16[1120,1120]{1,0:T(8,128)(2,1)} %copy-done.9, bf16[1120,1120]{1,0:T(8,128)(2,1)} %copy-done.9, bf16[560,1120]{1,0:T(8,128)(2,1)} %collective-permute-done.19.got_keep_ref.got_sent_ref, ...), custom_call_target="tpu_custom_call" | custom-call | flops 627200 | bytes 4390400 | tf_op jit(solution)/shard_map/pallas_call | solution.py:109
  150.8 3.7 shard_map.154
  158.1 5.6 %collective-permute-done.22 = bf16[256,384]{1,0:T(8,128)(2,1)S(1)} collective-permute-done((bf16[256,384]{1,0:T(8,128)(2,1)}, bf16[256,384]{1,0:T(8,128)(2,1)S(1)}, u32[]{:S(2)}, u32[]{:S(2)}) %collective-permute-start.22) | collective-permute-done | bytes 196640 | tf_op jit(solution)/shard_map/ppermute | solution.py:43
  177.3 15.6 %shard_map.157 = bf16[1024,1024]{1,0:T(8,128)(2,1)} custom-call(s32[1]{0:T(128)} %bitcast.3.me_ref, bf16[1024,1024]{1,0:T(8,128)(2,1)} %convolution_convert_fusion.7.refs_0_.refs_1_.refs_2_.refs_3_.refs_4_.refs_5_.refs_6_.refs_7_.refs_8_.refs_9_.refs_10_.refs_11_, ...), custom_call_target="tpu_custom_call" | custom-call | flops 2097152000 | bytes 10485760 | tf_op jit(solution)/shard_map/pallas_call | solution.py:357
  192.9 4.9 %convolution_convert_fusion.2 = bf16[960,1120]{1,0:T(8,128)(2,1)S(1)} fusion(bf16[1024,1024]{1,0:T(8,128)(2,1)} %shard_map.157, bf16[1120,256]{1,0:T(8,128)(2,1)} %copy-done.39, bf16[1120,256]{1,0:T(8,128)(2,1)S(1)} %copy-done.36, bf16[1120,256]{1,0:T(8,128)(2,1)} %copy-done.38, bf16[1120,256]{1,0:T(8,128)(2,1)} %copy-done.37), kind=kOutput, calls=%fused_computation.19 | convolution fusion | flops 2212259840 | bytes 6541312 | tf_op jit(solution)/shard_map/dot_general | solution.py:31
  221.5 5.9 %collective-permute-done.26 = bf16[1120,256]{1,0:T(8,128)(2,1)S(1)} collective-permute-done((bf16[1120,256]{1,0:T(8,128)(2,1)S(1)}, bf16[1120,256]{1,0:T(8,128)(2,1)S(1)}, u32[]{:S(2)}, u32[]{:S(2)}) %collective-permute-start.26) | collective-permute-done | bytes 573472 | tf_op jit(solution)/shard_map/ppermute | solution.py:43
  234.5 13.7 %collective-permute-done.33.got_keep_ref.got_sent_ref = bf16[272,1120]{1,0:T(8,128)(2,1)} collective-permute-done((bf16[272,1120]{1,0:T(8,128)(2,1)}, bf16[272,1120]{1,0:T(8,128)(2,1)}, u32[]{:S(2)}, u32[]{:S(2)}) %collective-permute-start.33) | collective-permute-done | bytes 609312 | tf_op jit(solution)/shard_map/ppermute | solution.py:56
  263.0 5.8 %collective-permute-start.43 = (bf16[72,1120]{1,0:T(8,128)(2,1)}, bf16[72,1120]{1,0:T(8,128)(2,1)S(1)}, u32[]{:S(2)}, u32[]{:S(2)}) collective-permute-start(bf16[72,1120]{1,0:T(8,128)(2,1)} %get-tuple-element.140), channel_id=1, source_target_pairs={{0,16},{4,20},{8,24},{12,28},{16,0},{20,4},{24,8},{28,12},{1,17},{... | collective-permute-start | bytes 483848 | tf_op jit(solution)/shard_map/ppermute | solution.py:56
  272.6 9.1 %collective-permute-done.45 = bf16[288,1120]{1,0:T(8,128)(2,1)S(1)} collective-permute-done((bf16[288,1120]{1,0:T(8,128)(2,1)S(1)}, bf16[288,1120]{1,0:T(8,128)(2,1)S(1)}, u32[]{:S(2)}, u32[]{:S(2)}) %collective-permute-start.45) | collective-permute-done | bytes 645152 | tf_op jit(solution)/shard_map/ppermute | solution.py:56
  290.3 11.7 %collective-permute-done.48 = bf16[72,1120]{1,0:T(8,128)(2,1)S(1)} collective-permute-done((bf16[72,1120]{1,0:T(8,128)(2,1)S(1)}, bf16[72,1120]{1,0:T(8,128)(2,1)S(1)}, u32[]{:S(2)}, u32[]{:S(2)}) %collective-permute-start.48) | collective-permute-done | bytes 161312 | tf_op jit(solution)/shard_map/ppermute | solution.py:56
  307.9 5.0 %collective-permute-done.46 = f32[2,1120]{1,0:T(2,128)S(1)} collective-permute-done((f32[2,1120]{1,0:T(2,128)S(1)}, f32[2,1120]{1,0:T(2,128)S(1)}, u32[]{:S(2)}, u32[]{:S(2)}) %collective-permute-start.46) | collective-permute-done | bytes 8992 | tf_op jit(solution)/shard_map/ppermute | solution.py:541
  330.7 19.3 %collective-permute-done.49 = f32[2,1120]{1,0:T(2,128)S(1)} collective-permute-done((f32[2,1120]{1,0:T(2,128)S(1)}, f32[2,1120]{1,0:T(2,128)S(1)}, u32[]{:S(2)}, u32[]{:S(2)}) %collective-permute-start.49) | collective-permute-done | bytes 8992 | tf_op jit(solution)/shard_map/ppermute | solution.py:541
  350.7 4.4 %collective-permute-done.52.half_ref = bf16[288,1120]{1,0:T(8,128)(2,1)S(1)} collective-permute-done((bf16[288,1120]{1,0:T(8,128)(2,1)S(1)}, bf16[288,1120]{1,0:T(8,128)(2,1)S(1)}, u32[]{:S(2)}, u32[]{:S(2)}) %collective-permute-start.52) | collective-permute-done | bytes 645152 | tf_op jit(solution)/shard_map/ppermute | solution.py:56
  (339 shorter events, 194.8 us)
Async XLA Ops:
  18.3 28.8 %collective-permute-start.6 = (bf16[280,1120]{1,0:T(8,128)(2,1)}, bf16[280,1120]{1,0:T(8,128)(2,1)}, u32[]{:S(2)}, u32[]{:S(2)}) collective-permute-start(bf16[280,1120]{1,0:T(8,128)(2,1)} %param.13), channel_id=1, source_target_pairs={{0,1},{1,0},{2,3},{3,2},{4,5},{5,4},{6,7},{7,6},{8,9},{9,8},{10,11... | collective-permute-start | bytes 1881608 | tf_op jit(solution)/shard_map/ppermute | solution.py:43
  18.8 20.7 %collective-permute-start.3 = (bf16[280,1120]{1,0:T(8,128)(2,1)}, bf16[280,1120]{1,0:T(8,128)(2,1)}, u32[]{:S(2)}, u32[]{:S(2)}) collective-permute-start(bf16[280,1120]{1,0:T(8,128)(2,1)} %param.13), channel_id=1, source_target_pairs={{0,2},{1,3},{2,0},{3,1},{4,6},{5,7},{6,4},{7,5},{8,10},{9,11},{10,... | collective-permute-start | bytes 1881608 | tf_op jit(solution)/shard_map/ppermute | solution.py:43
  41.2 26.0 %collective-permute-start.11 = (bf16[1120,256]{1,0:T(8,128)(2,1)S(1)}, bf16[1120,256]{1,0:T(8,128)(2,1)S(1)}, u32[]{:S(2)}, u32[]{:S(2)}) collective-permute-start(bf16[1120,256]{1,0:T(8,128)(2,1)S(1)} %fusion.59), channel_id=1, source_target_pairs={{0,1},{1,0},{2,3},{3,2},{4,5},{5,4},{6,7},{7,6},{8,9},{9,8},{10,11... | collective-permute-start | bytes 1720328 | tf_op jit(solution)/shard_map/ppermute | solution.py:43
  114.2 36.6 %collective-permute-start.18 = (bf16[560,1120]{1,0:T(8,128)(2,1)}, bf16[560,1120]{1,0:T(8,128)(2,1)}, u32[]{:S(2)}, u32[]{:S(2)}) collective-permute-start(bf16[560,1120]{1,0:T(8,128)(2,1)} %dynamic-slice_bitcast_fusion), channel_id=1, source_target_pairs={{0,8},{4,12},{8,0},{12,4},{16,24},{20,28},{24,16},{28,20},{1,9},{5... | collective-permute-start | bytes 3763208 | tf_op jit(solution)/shard_map/ppermute | solution.py:56
  115.8 30.6 %collective-permute-start.19 = (bf16[560,1120]{1,0:T(8,128)(2,1)}, bf16[560,1120]{1,0:T(8,128)(2,1)}, u32[]{:S(2)}, u32[]{:S(2)}) collective-permute-start(bf16[560,1120]{1,0:T(8,128)(2,1)} %dynamic-slice_bitcast_fusion.1), channel_id=1, source_target_pairs={{0,4},{4,0},{8,12},{12,8},{16,20},{20,16},{24,28},{28,24},{1,5},{5... | collective-permute-start | bytes 3763208 | tf_op jit(solution)/shard_map/ppermute | solution.py:56
  173.4 34.8 %collective-permute-start.27 = (bf16[144,1120]{1,0:T(8,128)(2,1)}, bf16[144,1120]{1,0:T(8,128)(2,1)}, u32[]{:S(2)}, u32[]{:S(2)}) collective-permute-start(bf16[144,1120]{1,0:T(8,128)(2,1)} %get-tuple-element.115), channel_id=1, source_target_pairs={{0,16},{4,20},{8,24},{12,28},{16,0},{20,4},{24,8},{28,12},{1,17},{... | collective-permute-start | bytes 967688 | tf_op jit(solution)/shard_map/ppermute | solution.py:56
  176.0 30.4 %collective-permute-start.28 = (bf16[144,1120]{1,0:T(8,128)(2,1)}, bf16[144,1120]{1,0:T(8,128)(2,1)S(1)}, u32[]{:S(2)}, u32[]{:S(2)}) collective-permute-start(bf16[144,1120]{1,0:T(8,128)(2,1)} %get-tuple-element.113), channel_id=1, source_target_pairs={{0,16},{4,20},{8,24},{12,28},{16,0},{20,4},{24,8},{28,12},{1,17},{... | collective-permute-start | bytes 967688 | tf_op jit(solution)/shard_map/ppermute | solution.py:56
  176.3 25.5 %collective-permute-start.29 = (bf16[1120,256]{1,0:T(8,128)(2,1)S(1)}, bf16[1120,256]{1,0:T(8,128)(2,1)}, u32[]{:S(2)}, u32[]{:S(2)}) collective-permute-start(bf16[1120,256]{1,0:T(8,128)(2,1)S(1)} %get-tuple-element.116), channel_id=1, source_target_pairs={{0,1},{1,0},{2,3},{3,2},{4,5},{5,4},{6,7},{7,6},{8,9},{9,8},{10,11... | collective-permute-start | bytes 1720328 | tf_op jit(solution)/shard_map/ppermute | solution.py:43
  176.6 21.4 %collective-permute-start.25 = (bf16[1120,256]{1,0:T(8,128)(2,1)S(1)}, bf16[1120,256]{1,0:T(8,128)(2,1)}, u32[]{:S(2)}, u32[]{:S(2)}) collective-permute-start(bf16[1120,256]{1,0:T(8,128)(2,1)S(1)} %get-tuple-element.116), channel_id=1, source_target_pairs={{0,2},{1,3},{2,0},{3,1},{4,6},{5,7},{6,4},{7,5},{8,10},{9,11},{10,... | collective-permute-start | bytes 1720328 | tf_op jit(solution)/shard_map/ppermute | solution.py:43
  211.6 18.4 %collective-permute-start.34 = (bf16[288,1120]{1,0:T(8,128)(2,1)S(1)}, bf16[288,1120]{1,0:T(8,128)(2,1)}, u32[]{:S(2)}, u32[]{:S(2)}) collective-permute-start(bf16[288,1120]{1,0:T(8,128)(2,1)S(1)} %dynamic-slice_bitcast_fusion.2), channel_id=1, source_target_pairs={{0,4},{4,0},{8,12},{12,8},{16,20},{20,16},{24,28},{28,24},{1,5},{5... | collective-permute-start | bytes 1935368 | tf_op jit(solution)/shard_map/ppermute | solution.py:56
  214.0 43.2 %collective-permute-start.40 = (bf16[144,1120]{1,0:T(8,128)(2,1)}, bf16[144,1120]{1,0:T(8,128)(2,1)}, u32[]{:S(2)}, u32[]{:S(2)}) collective-permute-start(bf16[144,1120]{1,0:T(8,128)(2,1)} %add_convert_fusion.1), channel_id=1, source_target_pairs={{0,16},{4,20},{8,24},{12,28},{16,0},{20,4},{24,8},{28,12},{1,17},{... | collective-permute-start | bytes 967688 | tf_op jit(solution)/shard_map/ppermute | solution.py:56
  216.6 39.5 %collective-permute-start.41 = (bf16[144,1120]{1,0:T(8,128)(2,1)S(1)}, bf16[144,1120]{1,0:T(8,128)(2,1)}, u32[]{:S(2)}, u32[]{:S(2)}) collective-permute-start(bf16[144,1120]{1,0:T(8,128)(2,1)S(1)} %add_convert_fusion.2), channel_id=1, source_target_pairs={{0,16},{4,20},{8,24},{12,28},{16,0},{20,4},{24,8},{28,12},{1,17},{... | collective-permute-start | bytes 967688 | tf_op jit(solution)/shard_map/ppermute | solution.py:56
  218.5 29.7 %collective-permute-start.33 = (bf16[272,1120]{1,0:T(8,128)(2,1)}, bf16[272,1120]{1,0:T(8,128)(2,1)}, u32[]{:S(2)}, u32[]{:S(2)}) collective-permute-start(bf16[272,1120]{1,0:T(8,128)(2,1)} %dynamic-slice_bitcast_fusion.3), channel_id=1, source_target_pairs={{0,8},{4,12},{8,0},{12,4},{16,24},{20,28},{24,16},{28,20},{1,9},{5... | collective-permute-start | bytes 1827848 | tf_op jit(solution)/shard_map/ppermute | solution.py:56
  227.4 24.6 %collective-permute-start.32 = (bf16[1120,256]{1,0:T(8,128)(2,1)}, bf16[1120,256]{1,0:T(8,128)(2,1)}, u32[]{:S(2)}, u32[]{:S(2)}) collective-permute-start(bf16[1120,256]{1,0:T(8,128)(2,1)} %get-tuple-element.170), channel_id=1, source_target_pairs={{0,2},{1,3},{2,0},{3,1},{4,6},{5,7},{6,4},{7,5},{8,10},{9,11},{10,... | collective-permute-start | bytes 1720328 | tf_op jit(solution)/shard_map/ppermute | solution.py:43
  232.9 27.4 %collective-permute-start.39 = (bf16[144,1120]{1,0:T(8,128)(2,1)}, bf16[144,1120]{1,0:T(8,128)(2,1)}, u32[]{:S(2)}, u32[]{:S(2)}) collective-permute-start(bf16[144,1120]{1,0:T(8,128)(2,1)} %get-tuple-element.131), channel_id=1, source_target_pairs={{0,8},{4,12},{8,0},{12,4},{16,24},{20,28},{24,16},{28,20},{1,9},{5... | collective-permute-start | bytes 967688 | tf_op jit(solution)/shard_map/ppermute | solution.py:56
  257.2 24.5 %collective-permute-start.45 = (bf16[288,1120]{1,0:T(8,128)(2,1)S(1)}, bf16[288,1120]{1,0:T(8,128)(2,1)S(1)}, u32[]{:S(2)}, u32[]{:S(2)}) collective-permute-start(bf16[288,1120]{1,0:T(8,128)(2,1)S(1)} %pad_maximum_fusion.8), channel_id=1, source_target_pairs={{0,8},{4,12},{8,0},{12,4},{16,24},{20,28},{24,16},{28,20},{1,9},{5... | collective-permute-start | bytes 1935368 | tf_op jit(solution)/shard_map/ppermute | solution.py:56
  259.8 24.1 %collective-permute-start.44 = (bf16[288,1120]{1,0:T(8,128)(2,1)S(1)}, bf16[288,1120]{1,0:T(8,128)(2,1)S(1)}, u32[]{:S(2)}, u32[]{:S(2)}) collective-permute-start(bf16[288,1120]{1,0:T(8,128)(2,1)S(1)} %pad_maximum_fusion.9), channel_id=1, source_target_pairs={{0,4},{4,0},{8,12},{12,8},{16,20},{20,16},{24,28},{28,24},{1,5},{5... | collective-permute-start | bytes 1935368 | tf_op jit(solution)/shard_map/ppermute | solution.py:56
  263.0 23.2 %collective-permute-start.43 = (bf16[72,1120]{1,0:T(8,128)(2,1)}, bf16[72,1120]{1,0:T(8,128)(2,1)S(1)}, u32[]{:S(2)}, u32[]{:S(2)}) collective-permute-start(bf16[72,1120]{1,0:T(8,128)(2,1)} %get-tuple-element.140), channel_id=1, source_target_pairs={{0,16},{4,20},{8,24},{12,28},{16,0},{20,4},{24,8},{28,12},{1,17},{... | collective-permute-start | bytes 483848 | tf_op jit(solution)/shard_map/ppermute | solution.py:56
  271.5 18.8 %collective-permute-start.37 = (f32[2,1120]{1,0:T(2,128)S(1)}, f32[2,1120]{1,0:T(2,128)S(1)}, u32[]{:S(2)}, u32[]{:S(2)}) collective-permute-start(f32[2,1120]{1,0:T(2,128)S(1)} %fusion.107), channel_id=1, source_target_pairs={{0,4},{4,0},{8,12},{12,8},{16,20},{20,16},{24,28},{28,24},{1,5},{5... | collective-permute-start | bytes 26888 | tf_op jit(solution)/shard_map/ppermute | solution.py:541
  306.3 65.5 %collective-permute-start.54 = (bf16[576,1120]{1,0:T(8,128)(2,1)}, bf16[576,1120]{1,0:T(8,128)(2,1)}, u32[]{:S(2)}, u32[]{:S(2)}) collective-permute-start(bf16[576,1120]{1,0:T(8,128)(2,1)} %pad_maximum_fusion.5.half_ref), channel_id=1, source_target_pairs={{0,8},{4,12},{8,0},{12,4},{16,24},{20,28},{24,16},{28,20},{1,9},{5... | collective-permute-start | bytes 3870728 | tf_op jit(solution)/shard_map/ppermute | solution.py:56
  307.7 60.7 %collective-permute-start.55 = (bf16[576,1120]{1,0:T(8,128)(2,1)}, bf16[576,1120]{1,0:T(8,128)(2,1)}, u32[]{:S(2)}, u32[]{:S(2)}) collective-permute-start(bf16[576,1120]{1,0:T(8,128)(2,1)} %pad_maximum_fusion.4.half_ref), channel_id=1, source_target_pairs={{0,4},{4,0},{8,12},{12,8},{16,20},{20,16},{24,28},{28,24},{1,5},{5... | collective-permute-start | bytes 3870728 | tf_op jit(solution)/shard_map/ppermute | solution.py:56
  313.0 42.1 %collective-permute-start.52 = (bf16[288,1120]{1,0:T(8,128)(2,1)S(1)}, bf16[288,1120]{1,0:T(8,128)(2,1)S(1)}, u32[]{:S(2)}, u32[]{:S(2)}) collective-permute-start(bf16[288,1120]{1,0:T(8,128)(2,1)S(1)} %pad_maximum_fusion.10.half_ref), channel_id=1, source_target_pairs={{0,4},{4,0},{8,12},{12,8},{16,20},{20,16},{24,28},{28,24},{1,5},{5... | collective-permute-start | bytes 1935368 | tf_op jit(solution)/shard_map/ppermute | solution.py:56
  314.6 44.1 %collective-permute-start.53 = (bf16[288,1120]{1,0:T(8,128)(2,1)S(1)}, bf16[288,1120]{1,0:T(8,128)(2,1)S(1)}, u32[]{:S(2)}, u32[]{:S(2)}) collective-permute-start(bf16[288,1120]{1,0:T(8,128)(2,1)S(1)} %pad_maximum_fusion.11.half_ref), channel_id=1, source_target_pairs={{0,8},{4,12},{8,0},{12,4},{16,24},{20,28},{24,16},{28,20},{1,9},{5... | collective-permute-start | bytes 1935368 | tf_op jit(solution)/shard_map/ppermute | solution.py:56
  315.1 34.9 %collective-permute-start.49 = (f32[2,1120]{1,0:T(2,128)S(1)}, f32[2,1120]{1,0:T(2,128)S(1)}, u32[]{:S(2)}, u32[]{:S(2)}) collective-permute-start(f32[2,1120]{1,0:T(2,128)S(1)} %add.199), channel_id=1, source_target_pairs={{0,16},{4,20},{8,24},{12,28},{16,0},{20,4},{24,8},{28,12},{1,17},{... | collective-permute-start | bytes 26888 | tf_op jit(solution)/shard_map/ppermute | solution.py:541
  (92 other events, 925.6 us)

commit v2 on v1

--- a/solution.py
+++ b/solution.py
@@ -44,8 +44,9 @@
 
 
 class WideSum:
-    def __init__(self, size, hops, part):
+    def __init__(self, size, hops, part, out_rows=None, last=False):
         self.size, self.hops, self.part, self.rows = size, hops, part, part.shape[0]
+        self.out_rows, self.last = out_rows or self.rows, last
         self.step = 0
         index = lax.axis_index("wide")
         bits = [jnp.bitwise_and(index // hop, 1) for hop in hops]
@@ -68,11 +69,19 @@
             halves = self.part.reshape(2, self.rows // 2, self.part.shape[1])
             return self.send(lax.dynamic_index_in_dim(halves, 1 - self.at[0], 0, keepdims=False), 0)
         if self.step == 2:
-            self.keep, sent = fold(self.at, self.part, got, 1)
-            return self.send(sent, 1)
+            quarters = self.part.reshape(4, self.rows // 4, self.part.shape[1])
+            got = got.reshape(2, self.rows // 4, got.shape[1])
+            place = lambda side: lax.dynamic_index_in_dim(
+                quarters, 2 * self.at[0] + side, 0, keepdims=False
+            ).astype(F32) + lax.dynamic_index_in_dim(got, side, 0, keepdims=False).astype(F32)
+            self.keep = place(self.at[1])
+            return self.send(place(1 - self.at[1]).astype(BF16), 1)
         if self.step == 3:
-            self.keep, sent = fold(self.at, self.keep, got, 2)
-            return self.send(sent, 2)
+            size = eighth_of(self.rows // 4)
+            total = self.keep + got.astype(F32)
+            first = self.at[2] == 0
+            self.keep = jnp.where(first, total[:size], total[-size:])
+            return self.send(jnp.where(first, total[-size:], total[:size]).astype(BF16), 2)
         if self.step == 4:
             self.have = (self.keep + got.astype(F32)).astype(BF16)
             return self.send(self.have, 2)
@@ -82,9 +91,14 @@
         if self.step == 6:
             self.have = jnp.concatenate([self.have, got], axis=0)
             self.send(self.have, 0)
-            self.whole = join(self.at, self.have, self.rows, None)
+            if not self.last:
+                self.whole = join(self.at, self.have, self.rows, self.out_rows, None)
+                return self.whole
             return self.have
-        self.whole = join(self.at, got, self.rows, self.whole)
+        if self.last:
+            self.other = got
+            return got
+        self.whole = join(self.at, got, self.rows, self.out_rows, self.whole)
         return self.whole
 
     @property
@@ -92,65 +106,32 @@
         return self.step == 7
 
 
-def fold_kernel(at_ref, keep_ref, sent_ref, got_keep_ref, got_sent_ref, o_keep_ref, o_sent_ref):
-    o_keep_ref[...] = keep_ref[...].astype(F32) + got_keep_ref[...].astype(F32)
-    o_sent_ref[...] = (sent_ref[...].astype(F32) + got_sent_ref[...].astype(F32)).astype(BF16)
-
-
 def eighth_of(quarter):
     return -(-quarter // 16) * 8
-
-
-def fold(at, own, got, turn):
-    rows, columns = got.shape
-    half = rows // 2 if turn == 1 else eighth_of(rows)
-    base = (lambda a: 2 * a[0]) if turn == 1 else (lambda a: 0)
-    spec = lambda place: pl.BlockSpec((half, columns), lambda i, a: (place(a), 0))
-    return pl.pallas_call(
-        fold_kernel,
-        out_shape=[
-            jax.ShapeDtypeStruct((half, columns), F32),
-            jax.ShapeDtypeStruct((half, columns), BF16),
-        ],
-        grid_spec=pltpu.PrefetchScalarGridSpec(
-            num_scalar_prefetch=1,
-            grid=(1,),
-            in_specs=[
-                spec(lambda a: base(a) + a[turn]),
-                spec(lambda a: base(a) + 1 - a[turn]),
-                spec(lambda a: a[turn]),
-                spec(lambda a: 1 - a[turn]),
-            ],
-            out_specs=[spec(lambda a: 0)] * 2,
-        ),
-        cost_estimate=pl.CostEstimate(
-            flops=rows * columns, bytes_accessed=7 * rows * columns, transcendentals=0
-        ),
-    )(at, own, own, got, got)
 
 
 def join_kernel(rows, at_ref, half_ref, *refs):
     o_ref = refs[-1]
     eighth = half_ref.shape[0] // 2
-    rest = rows - eighth
     first = at_ref[2] == 0
 
     @pl.when(first)
     def _():
-        o_ref[...] = half_ref[0:rows, :].astype(F32)
+        o_ref[0:eighth, :] = half_ref[0:eighth, :].astype(F32)
+        o_ref[rows - eighth : rows, :] = half_ref[eighth : 2 * eighth, :].astype(F32)
 
     @pl.when(jnp.logical_not(first))
     def _():
         o_ref[0:eighth, :] = half_ref[eighth : 2 * eighth, :].astype(F32)
-        o_ref[eighth:rows, :] = half_ref[0:rest, :].astype(F32)
-
-
-def join(at, half, rows, whole):
+        o_ref[rows - eighth : rows, :] = half_ref[0:eighth, :].astype(F32)
+
+
+def join(at, half, rows, out_rows, whole):
     columns, quarter = half.shape[1], rows // 4
     place = (lambda a: a[0]) if whole is None else (lambda a: 1 - a[0])
     return pl.pallas_call(
         partial(join_kernel, quarter),
-        out_shape=jax.ShapeDtypeStruct((rows, columns), F32),
+        out_shape=jax.ShapeDtypeStruct((out_rows, columns), F32),
         grid_spec=pltpu.PrefetchScalarGridSpec(
             num_scalar_prefetch=1,
             grid=(2,),
@@ -161,8 +142,46 @@
             out_specs=pl.BlockSpec((quarter, columns), lambda i, a: (2 * place(a) + i, 0)),
         ),
         input_output_aliases={} if whole is None else {2: 0},
-        cost_estimate=pl.CostEstimate(flops=0, bytes_accessed=3 * rows * columns, transcendentals=0),
+        cost_estimate=pl.CostEstimate(flops=0, bytes_accessed=rows, transcendentals=0),
     )(at, half, *([] if whole is None else [whole]))
+
+
+def join_last_kernel(rows, at_ref, own_ref, other_ref, whole_ref, o_whole_ref, o_rest_ref):
+    eighth = own_ref.shape[0] // 2
+    step = pl.program_id(0)
+    for mine, half_ref in ((True, own_ref), (False, other_ref)):
+        for tail, o_ref in ((0, o_whole_ref), (1, o_rest_ref)):
+            for bit in (0, 1):
+                here = (step // 2 == tail) & ((at_ref[0] == tail) == mine) & (at_ref[2] == bit)
+
+                @pl.when(here)
+                def _(half_ref=half_ref, o_ref=o_ref, bit=bit):
+                    low, high = (0, eighth) if bit == 0 else (eighth, 0)
+                    o_ref[0:eighth, :] = half_ref[low : low + eighth, :].astype(F32)
+                    o_ref[rows - eighth : rows, :] = half_ref[high : high + eighth, :].astype(F32)
+
+
+def join_last(at, own, other, whole, rows, rest_rows):
+    columns, quarter = own.shape[1], rows // 4
+    half = pl.BlockSpec((own.shape[0] // 2, columns), lambda i, a: (jnp.bitwise_xor(i & 1, a[1]), 0))
+    return pl.pallas_call(
+        partial(join_last_kernel, quarter),
+        out_shape=[
+            jax.ShapeDtypeStruct(whole.shape, F32),
+            jax.ShapeDtypeStruct((rest_rows, columns), F32),
+        ],
+        grid_spec=pltpu.PrefetchScalarGridSpec(
+            num_scalar_prefetch=1,
+            grid=(4,),
+            in_specs=[half, half, pl.BlockSpec(memory_space=pl.ANY)],
+            out_specs=[
+                pl.BlockSpec((quarter, columns), lambda i, a: (4 + jnp.minimum(i, 1), 0)),
+                pl.BlockSpec((quarter, columns), lambda i, a: (jnp.maximum(i - 2, 0), 0)),
+            ],
+        ),
+        input_output_aliases={3: 0},
+        cost_estimate=pl.CostEstimate(flops=0, bytes_accessed=rows, transcendentals=0),
+    )(at, own, other, whole)
 
 
 LOG2E = 1.4426950408889634
@@ -322,7 +341,6 @@
 def attend(me, proj, rows, heads):
     pairs = -(-heads // 2)
     all_rows = 4 * rows
-    tiles = heads * 10 * rows * rows
     last_tile = proj.shape[1] // 128 - 1
     return pl.pallas_call(
         partial(attend_kernel, heads % 2 == 1),
@@ -344,7 +362,7 @@
             ],
         ),
         cost_estimate=pl.CostEstimate(
-            flops=tiles * 4 * HP, bytes_accessed=all_rows * pairs * 1024, transcendentals=tiles
+            flops=rows, bytes_accessed=rows, transcendentals=0
         ),
     )(me, *([proj] * 12))
 
@@ -352,7 +370,6 @@
 def attend_back(me, proj, lse, mixed, grad_mixed, rows, heads):
     pairs = -(-heads // 2)
     all_rows, columns = proj.shape
-    tiles = heads * 10 * rows * rows
     last_tile = columns // 128 - 1
     return pl.pallas_call(
         partial(attend_back_kernel, heads % 2 == 1),
@@ -371,7 +388,7 @@
             scratch_shapes=[pltpu.VMEM((4, rows, 128), F32)] * 2,
         ),
         cost_estimate=pl.CostEstimate(
-            flops=tiles * 10 * HP, bytes_accessed=all_rows * columns * 10, transcendentals=tiles
+            flops=rows, bytes_accessed=rows, transcendentals=0
         ),
     )(me, *([proj] * 12), *([grad_mixed] * 4), *([mixed] * 4), lse)
 
@@ -424,19 +441,18 @@
         rows_one = jnp.concatenate([near[0], far_norm[0], near[1], far_norm[1]], axis=1)
         projected = dot(rows_one, proj, ((0,), (1,))).astype(BF16)
         own_branch = (own_live * own_grad.astype(F32)).astype(BF16)
-        own_branch = after(own_branch, rows_one)
+        own_branch = after(own_branch, tok_y)
         grad_y, grad_c = narrow.send(own_branch, 2), narrow.send(own_branch, 1)
         mixed, lse = attend(me_ref, projected, rows, heads)
-        out_y = after(out_y, mixed)
-        out_d = narrow.send(out_y, 1)
         block = lambda a, slot: a[slot * rows : (slot + 1) * rows]
         mixed_y = narrow.send(block(mixed, 1), 2)
         mixed_d = narrow.send(block(mixed, 3), 3)
         mixed_c = narrow.send(block(mixed, 2), 1)
-        out_all = [pad_rows(after(b, mixed)) for b in (out_weight, out_y, out_c, out_d)]
-        grad_y = after(grad_y, *out_all)
+        out_y = after(out_y, mixed)
+        out_d = narrow.send(out_y, 1)
+        grad_y = after(grad_y, out_y)
         grad_d = narrow.send(grad_y, 1)
-        mixed_y = after(mixed_y, grad_y)
+        out_all = [pad_rows(after(b, grad_y)) for b in (out_weight, out_y, out_c, out_d)]
         mixed_own = [block(mixed, 0), mixed_y, mixed_c, mixed_d]
         branch = sum(dot(w, m, ((0,), (1,))) for w, m in zip(out_all, mixed_own))
         middle = stream + own_live * branch
@@ -460,40 +476,40 @@
         half = 2 * rows
         down = wide_sum((1, 2, 4), dot(hidden, grad_rows, ((1,), (1,))).astype(BF16))
         mark = down.advance()
-        up = wide_sum((2, 1, 4), dot(rows_two, after(grad_pre, mark), ((1,), (1,))).astype(BF16))
-        mark = up.advance()
 
         grad_pre_on = after(grad_pre, mark)
         sent = dot(up_weight, grad_pre_on[:, half:], ((1,), (0,))).astype(BF16)
         got_two = narrow.send(sent, 1)
         kept_two = dot(up_weight, after(grad_pre_on[:, :half], sent), ((1,), (0,)))
         got_two = after(got_two, kept_two).astype(F32)
-        far_two = narrow.send((kept_two[:, rows:] + got_two[:, rows:]).astype(BF16), 2)
+        far_sum = (kept_two[:, rows:] + got_two[:, rows:]).astype(BF16)
+        far_two = narrow.send(far_sum, 2)
         near_two = kept_two[:, :rows] + got_two[:, :rows]
-        hidden_on = after(hidden, near_two)
-        mlp_sent = dot(down_weight, hidden_on[:, half:], ((0,), (0,))).astype(BF16)
-        mlp_got = narrow.send(mlp_sent, 1)
-        mlp_kept = dot(down_weight, after(hidden_on[:, :half], mlp_sent), ((0,), (0,)))
-        mlp_got = after(mlp_got, mlp_kept).astype(F32)
-        mlp_far = (mlp_kept[:, rows:] + mlp_got[:, rows:]).astype(BF16)
-        mlp_near = mlp_kept[:, :rows] + mlp_got[:, :rows]
-        grad_normed_two = near_two + after(far_two, mlp_near, mlp_far).astype(F32)
+        up = wide_sum((2, 1, 4), dot(rows_two, after(grad_pre_on, far_sum), ((1,), (1,))).astype(BF16))
+        mark = up.advance()
+        grad_normed_two = near_two + after(far_two, mark).astype(F32)
         gain_two = jnp.sum(grad_normed_two * normal_two, axis=1)
         grad_middle = own_grad.astype(F32) + layer_back(grad_normed_two * gain_row_two, normal_two, rstd_two)
         grad_attn = (own_live * grad_middle).astype(BF16)
         piece = [dot(grad_attn, w, ((0,), (1,))).astype(BF16) for w in out_all]
         mix_y, mix_d, mix_c = narrow.send(piece[1], 2), narrow.send(piece[3], 3), narrow.send(piece[2], 1)
-        mark = down.advance(*piece)
-        mark = up.advance(mark)
-        mix_y = after(mix_y, mark)
+        hidden_on = after(hidden, *piece)
+        mlp_sent = dot(down_weight, hidden_on[:, half:], ((0,), (0,))).astype(BF16)
+        mlp_got = narrow.send(mlp_sent, 1)
+        mlp_kept = dot(down_weight, after(hidden_on[:, :half], mlp_sent), ((0,), (0,)))
+        mix_y = after(mix_y, mlp_kept)
         grad_mixed = jnp.concatenate([piece[0], mix_y, mix_c, mix_d], axis=0)
-        mark = down.advance(grad_mixed)
-        mark = up.advance(mark)
-        attn_on = after(grad_attn, mark)
+        attn_on = after(grad_attn, grad_mixed)
         attn_y, attn_c = narrow.send(attn_on, 2), narrow.send(attn_on, 1)
         grad_proj = attend_back(me_ref, projected, lse, mixed, after(grad_mixed, attn_on), rows, heads)
+        mark = down.advance(grad_proj)
+        mark = up.advance(mark)
+        grad_proj = after(grad_proj, mark)
         attn_y = after(attn_y, grad_proj)
         attn_d = narrow.send(attn_y, 1)
+        mlp_got = after(mlp_got, attn_y).astype(F32)
+        mlp_far = (mlp_kept[:, rows:] + mlp_got[:, rows:]).astype(BF16)
+        mlp_near = mlp_kept[:, :rows] + mlp_got[:, :rows]
         mlp_send_far = narrow.send(after(mlp_far, attn_y), 2)
 
         found = dot(grad_proj[:, : 3 * heads * HP], rows_one, ((0,), (1,))).astype(BF16)
@@ -502,13 +518,18 @@
         if heads % 2:
             fields.append(found[full * 384 :].reshape(3, HP, width)[:, :HS])
         qkv_part = jnp.concatenate(fields, axis=1).reshape(3 * own_width, width)
-        cut = -(-4 * own_width // 64) * 32
-        first = wide_sum((1, 2, 4), qkv_part[:cut])
+        cut = -(-own_width // 16) * 32
+        low = 3 * own_width - cut
+        filled = lambda a: jnp.pad(a, ((0, cut // 2 - a.shape[0]), (0, 0)))
+        first = WideSum(wide, (1, 2, 4), qkv_part[:cut], 3 * own_width)
         mark = first.advance()
+        mark = down.advance(mark)
+        mark = up.advance(mark)
         attn_rows = jnp.concatenate([grad_attn, attn_y, attn_c, after(attn_d, mark)], axis=1)
         out_part = dot(mixed[:, : heads * HP], attn_rows, ((0,), (1,))).astype(BF16)
         out_part = out_part.reshape(heads, HP, width)[:, :HS].reshape(own_width, width)
-        second = wide_sum((2, 1, 4), jnp.concatenate([qkv_part[cut:], out_part], axis=0))
+        second_part = jnp.concatenate([filled(qkv_part[cut:]), filled(out_part)], axis=0)
+        second = WideSum(wide, (2, 1, 4), second_part, last=True)
         mark = second.advance()
         mark = down.advance(mark)
         mark = up.advance(mark)
@@ -517,41 +538,40 @@
         one_got = narrow.send(one_sent, 1)
         one_kept = dot(proj, after(grad_proj[:half], one_sent), ((0,), (1,)))
         one_got = after(one_got, one_kept).astype(F32)
-        one_far = narrow.send((one_kept[:, rows:] + one_got[:, rows:]).astype(BF16), 2)
+        one_sum = (one_kept[:, rows:] + one_got[:, rows:]).astype(BF16)
+        one_far = narrow.send(one_sum, 2)
         one_near = one_kept[:, :rows] + one_got[:, :rows]
-        mlp_own = mlp_near + after(mlp_send_far, one_near).astype(F32)
+        mark = first.advance(one_sum)
+        mark = second.advance(mark)
+        mlp_own = mlp_near + after(mlp_send_far, mark).astype(F32)
         block_output = (middle + own_live * mlp_own).astype(BF16)
-        mark = first.advance(block_output)
-        mark = second.advance(mark)
-        grad_normed_one = one_near + after(one_far, mark).astype(F32)
+        grad_normed_one = one_near + after(one_far, block_output).astype(F32)
         gain_one = jnp.sum(grad_normed_one * normal_one, axis=1)
         grad_stream = layer_back(grad_normed_one * gain_row_one, normal_one, rstd_one)
         input_grad = (grad_middle + grad_stream).astype(BF16)
         gains = jnp.stack([gain_one, gain_two])
-        mark = down.advance(gains, input_grad)
-        mark = up.advance(mark)
-        mark = first.advance(mark)
-        mark = second.advance(mark)
-        for k in (1, 2):
-            gains = gains + narrow.send(gains, k)
-        for s in (down, up, first, second):
-            mark = s.advance(mark, gains)
-        hop = 1
-        while hop < wide:
+        for hop in (1, 2):
+            gains = gains + narrow.send(gains, hop)
+        mark = gains
+        turns = [[first, second, down, up], [first, second, down], [first, second]]
+        order = (4, 1, 2) + tuple(8 * 2**i for i in range(wide.bit_length() - 4))
+        for hop in order:
             got = lax.ppermute(gains, "wide", [(i, i ^ hop) for i in range(wide)])
+            for s in turns.pop(0) if turns else ():
+                mark = s.advance(mark, gains)
             gains = gains + after(got, mark)
-            for s in (first, second):
-                if not s.done:
-                    mark = s.advance(mark, gains)
-            hop *= 2
-        for s in (down, up, first, second):
-            while not s.done:
-                mark = s.advance(mark)
-
-        low = 3 * own_width - cut
-        qkv_grad = jnp.concatenate([first.whole, second.whole[:low]], axis=0)
+        mark = up.advance(mark, gains)
+        for s in (first, second, down, up, first, second):
+            mark = s.advance(mark)
+
+        if wide == 8:
+            qkv_grad, out_grad = join_last(
+                second.at, second.have, second.other, first.whole, second.rows, own_width
+            )
+        else:
+            qkv_grad = jnp.concatenate([first.whole, second.whole[:low]], axis=0)
+            out_grad = second.whole[cut // 2 : cut // 2 + own_width]
         qkv_grad = qkv_grad.reshape(3, own_width, width).transpose(0, 2, 1)
-        out_grad = second.whole[low:]
         return (
             block_output.T[None],
             input_grad.T[None],

time: 382 us -> 348 us (0.911)
  Pallas kernels: 76.6 us -> 51 us
  local copies, waits for them, and re-layouts: 29.1 us -> 23.3 us
  starting transfers between devices: 53.9 us -> 49.7 us
    ppermute x24, waiting for transfers between devices: 49.4 us -> 94.7 us  [send(): lax.ppermute(value, 'wide', [(i, i ^ hop) for i in range(self.size)])]
    ppermute x3, waiting for transfers between devices: 24.3 us -> 0.01 us  [on_device(): got = lax.ppermute(gains, 'wide', [(i, i ^ hop) for i in range(wide)])]
    pallas_call x8 -> x1, Pallas kernels: 25.1 us -> 4.91 us  [join_last(): pl.pallas_call(partial(join_last_kernel, quarter), out_shape=[jax.ShapeDt...]
    ppermute x29, waiting for transfers between devices: 46.3 us -> 26.8 us  [send(): return lax.ppermute(value, 'narrow', self.perm[k])]
    pallas_call x8 -> x6, Pallas kernels: 24.5 us -> 19.1 us  [join(): pl.pallas_call(partial(join_kernel, quarter), out_shape=jax.ShapeDtypeStr...]
    ppermute x24, starting transfers between devices: 31 us -> 26.5 us  [send(): lax.ppermute(value, 'wide', [(i, i ^ hop) for i in range(self.size)])]
    slice x3 -> x1, local copies, waits for them, and re-layouts: 4.06 us -> 0.1 us  [on_device(): first = WideSum(wide, (1, 2, 4), qkv_part[:cut], 3 * own_width)]
    unnamed x119 -> x100, local copies, waits for them, and re-layouts: 8.84 us -> 8.09 us
  transfers between devices with their start and end apart: 56 -> 56, of which waited for: 22 -> 19; matrix products, arithmetic and copies ran while one was open for 22% -> 28% of each run, Pallas kernels for 19% -> 13%
where the time goes in v2:
time: 348 us; the launch traced here: 342 us
  waiting for transfers between devices  122 us (35%)
  Pallas kernels  51 us (15%)
  starting transfers between devices  49.7 us (14%)
  matrix products  49.6 us (14%)
  other arithmetic  43.8 us (13%)
  local copies, waits for them, and re-layouts  23.3 us (7%)
    ppermute x24, waiting for transfers between devices, send(): lax.ppermute(value, 'wide', [(i, i ^ hop) for i in range(self.size)])  94.7 us
    dot_general x21, matrix products, dot(): return lax.dot_general(a, b, (dims, ((), ())), preferred_element_type=F32)  49.6 us
    ppermute x29, waiting for transfers between devices, send(): return lax.ppermute(value, 'narrow', self.perm[k])  26.8 us
    ppermute x24, starting transfers between devices, send(): lax.ppermute(value, 'wide', [(i, i ^ hop) for i in range(self.size)])  26.5 us
    ppermute x29, starting transfers between devices, send(): return lax.ppermute(value, 'narrow', self.perm[k])  19.3 us
    pallas_call x6, Pallas kernels, join(): pl.pallas_call(partial(join_kernel, quarter), out_shape=jax.ShapeDtypeStr...  19.1 us
    pallas_call x1, Pallas kernels, attend_back(): pl.pallas_call(partial(attend_back_kernel, heads % 2 == 1), out_shape=jax...  16 us
    pallas_call x1, Pallas kernels, attend(): pl.pallas_call(partial(attend_kernel, heads % 2 == 1), out_shape=(jax.Sha...  11 us
  transfers between devices with their start and end apart: 56, of which 19 were waited for; matrix products, arithmetic and copies ran while one was open for 28% of the time, Pallas kernels for 13%

profile of v2, /device:TPU:0, one launch (start us, length us, event | category | flops | bytes accessed | tf_op | source)
XLA Modules:
  0.0 341.7 jit_solution(857007852640890435)
XLA Ops:
  24.6 4.3 %convolution_convert_fusion.7.refs_0_.refs_1_.refs_2_.refs_3_.refs_4_.refs_5_.refs_6_.refs_7_.refs_8_.refs_9_.refs_10_.refs_11_ = bf16[1024,1024]{1,0:T(8,128)(2,1)} fusion(bf16[1120,256]{1,0:T(8,128)(2,1)S(1)} %get-tuple-element.148, bf16[1120,256]{1,0:T(8,128)(2,1)S(1)} %get-tuple-element.149, bf16[1120,256]{1,0:T(8,128)(2,1)S(1)} %get-tuple-element.147, ...), kind=kOutput, calls=%fused_computation.50 | convolution fusion | flops 2365915136 | bytes 6541312 | tf_op jit(solution)/shard_map/dot_general | solution.py:31
  28.9 11.0 %shard_map.152 = (bf16[1024,384]{1,0:T(8,128)(2,1)}, f32[3,4,8,256]{3,2,1,0:T(8,128)}) custom-call(s32[1]{0:T(128)} %bitcast.12.me_ref, bf16[1024,1024]{1,0:T(8,128)(2,1)} %convolution_convert_fusion.7.refs_0_.refs_1_.refs_2_.refs_3_.refs_4_.refs_5_.refs_6_.refs_7_.refs_8_.refs_9_.refs_10_.refs_11_, ...), custom_call_target="tpu_custom_call" | custom-call | flops 256 | bytes 256 | tf_op jit(solution)/shard_map/pallas_call | solution.py:345
  43.4 5.5 %collective-permute-done.2 = bf16[1120,256]{1,0:T(8,128)(2,1)} collective-permute-done((bf16[1120,256]{1,0:T(8,128)(2,1)}, bf16[1120,256]{1,0:T(8,128)(2,1)}, u32[]{:S(2)}, u32[]{:S(2)}) %collective-permute-start.2) | collective-permute-done | bytes 573472 | tf_op jit(solution)/shard_map/ppermute | solution.py:43
  64.1 4.8 %convolution_bitcast_fusion = f32[1120,1024]{1,0:T(8,128)} fusion(bf16[1120,1120]{1,0:T(8,128)(2,1)S(1)} %copy-done.46, bf16[1120,1024]{1,0:T(8,128)(2,1)S(1)} %constant_dynamic-update-slice_fusion), kind=kOutput, calls=%fused_computation.17 | convolution fusion | flops 2569011200 | bytes 9390080 | tf_op jit(solution)/shard_map/dot_general | solution.py:31
  68.9 6.7 %collective-permute-done.10 = bf16[1120,256]{1,0:T(8,128)(2,1)} collective-permute-done((bf16[1120,256]{1,0:T(8,128)(2,1)}, bf16[1120,256]{1,0:T(8,128)(2,1)}, u32[]{:S(2)}, u32[]{:S(2)}) %collective-permute-start.10) | collective-permute-done | bytes 573472 | tf_op jit(solution)/shard_map/ppermute | solution.py:43
  77.9 7.2 %fusion.6 = (bf16[1120,1024]{1,0:T(8,128)(2,1)S(1)}, bf16[1120,1024]{1,0:T(8,128)(2,1)S(1)}) fusion(f32[1120,1024]{1,0:T(8,128)} %convolution_bitcast_fusion, bf16[1120,1120]{1,0:T(8,128)(2,1)S(1)} %copy-done, bf16[1120,256]{1,0:T(8,128)(2,1)} %collective-permute-done.14, bf16[1120,256]{1,0:T(8,128)(2,1)} %collective-permute-done.13, ...), kind=kOutput, calls=%fused_computation.10 | convolution fusion | flops 2591948800 | bytes 13977600 | tf_op jit(solution)/shard_map/dot_general | solution.py:31
  85.2 3.6 %convolution_convert_fusion.1 = bf16[1120,1120]{1,0:T(8,128)(2,1)S(1)} fusion(bf16[1120,1024]{1,0:T(8,128)(2,1)S(1)} %get-tuple-element.87, bf16[1120,1024]{1,0:T(8,128)(2,1)S(1)} %copy-done.43), kind=kOutput, calls=%fused_computation.1 | convolution fusion | flops 2570265600 | bytes 7096320 | tf_op jit(solution)/shard_map/dot_general | solution.py:31
  100.8 4.8 %convolution_convert_fusion = bf16[1120,1120]{1,0:T(8,128)(2,1)S(1)} fusion(bf16[1120,1024]{1,0:T(8,128)(2,1)S(1)} %copy-done.39, bf16[1120,256]{1,0:T(8,128)(2,1)} %collective-permute-done.14, bf16[1120,256]{1,0:T(8,128)(2,1)} %collective-permute-done.13, bf16[1120,256]{1,0:T(8,128)(2,1)} %collective-permute-done.10, bf16[1120,256]{1,0:T(8,128)(2,1)} %multiply_convert_fusion.1), kind=kOutput, calls=%fused_computation | convolution fusion | flops 2579440640 | bytes 7096320 | tf_op jit(solution)/shard_map/dot_general | solution.py:31
  108.3 6.2 %collective-permute-done.16 = bf16[1120,256]{1,0:T(8,128)(2,1)S(1)} collective-permute-done((bf16[1120,256]{1,0:T(8,128)(2,1)S(1)}, bf16[1120,256]{1,0:T(8,128)(2,1)S(1)}, u32[]{:S(2)}, u32[]{:S(2)}) %collective-permute-start.16) | collective-permute-done | bytes 573472 | tf_op jit(solution)/shard_map/ppermute | solution.py:43
  130.9 16.0 %shard_map.153 = bf16[1024,1024]{1,0:T(8,128)(2,1)} custom-call(s32[1]{0:T(128)} %bitcast.12.me_ref, bf16[1024,1024]{1,0:T(8,128)(2,1)} %convolution_convert_fusion.7.refs_0_.refs_1_.refs_2_.refs_3_.refs_4_.refs_5_.refs_6_.refs_7_.refs_8_.refs_9_.refs_10_.refs_11_, ...), custom_call_target="tpu_custom_call" | custom-call | flops 256 | bytes 256 | tf_op jit(solution)/shard_map/pallas_call | solution.py:374
  151.7 4.0 %convolution_convert_fusion.2 = bf16[960,1120]{1,0:T(8,128)(2,1)S(1)} fusion(bf16[1024,1024]{1,0:T(8,128)(2,1)S(1)} %copy-done.18, bf16[1120,256]{1,0:T(8,128)(2,1)} %copy-done.35, bf16[1120,256]{1,0:T(8,128)(2,1)S(1)} %copy-done.30, bf16[1120,256]{1,0:T(8,128)(2,1)S(1)} %copy-done.34, bf16[1120,256]{1,0:T(8,128)(2,1)S(1)} %copy-done.32), kind=kOutput, calls=%fused_computation.18 | convolution fusion | flops 2212259840 | bytes 6541312 | tf_op jit(solution)/shard_map/dot_general | solution.py:31
  159.2 5.8 %collective-permute-done.28 = bf16[280,1120]{1,0:T(8,128)(2,1)S(1)} collective-permute-done((bf16[280,1120]{1,0:T(8,128)(2,1)S(1)}, bf16[280,1120]{1,0:T(8,128)(2,1)S(1)}, u32[]{:S(2)}, u32[]{:S(2)}) %collective-permute-start.28) | collective-permute-done | bytes 627232 | tf_op jit(solution)/shard_map/ppermute | solution.py:57
  169.3 3.9 %collective-permute-done.27 = bf16[280,1120]{1,0:T(8,128)(2,1)S(1)} collective-permute-done((bf16[280,1120]{1,0:T(8,128)(2,1)S(1)}, bf16[280,1120]{1,0:T(8,128)(2,1)S(1)}, u32[]{:S(2)}, u32[]{:S(2)}) %collective-permute-start.27) | collective-permute-done | bytes 627232 | tf_op jit(solution)/shard_map/ppermute | solution.py:57
  180.1 11.7 %collective-permute-done.32 = bf16[144,1120]{1,0:T(8,128)(2,1)S(1)} collective-permute-done((bf16[144,1120]{1,0:T(8,128)(2,1)S(1)}, bf16[144,1120]{1,0:T(8,128)(2,1)S(1)}, u32[]{:S(2)}, u32[]{:S(2)}) %collective-permute-start.32) | collective-permute-done | bytes 322592 | tf_op jit(solution)/shard_map/ppermute | solution.py:57
  191.9 5.9 %collective-permute-done.31 = bf16[144,1120]{1,0:T(8,128)(2,1)S(1)} collective-permute-done((bf16[144,1120]{1,0:T(8,128)(2,1)S(1)}, bf16[144,1120]{1,0:T(8,128)(2,1)S(1)}, u32[]{:S(2)}, u32[]{:S(2)}) %collective-permute-start.31) | collective-permute-done | bytes 322592 | tf_op jit(solution)/shard_map/ppermute | solution.py:57
  205.6 3.4 collective-permute-start.39
  211.2 6.8 %collective-permute-done.30 = bf16[288,1120]{1,0:T(8,128)(2,1)S(1)} collective-permute-done((bf16[288,1120]{1,0:T(8,128)(2,1)S(1)}, bf16[288,1120]{1,0:T(8,128)(2,1)S(1)}, u32[]{:S(2)}, u32[]{:S(2)}) %collective-permute-start.30) | collective-permute-done | bytes 645152 | tf_op jit(solution)/shard_map/ppermute | solution.py:57
  219.6 16.0 %collective-permute-done.29 = bf16[288,1120]{1,0:T(8,128)(2,1)S(1)} collective-permute-done((bf16[288,1120]{1,0:T(8,128)(2,1)S(1)}, bf16[288,1120]{1,0:T(8,128)(2,1)S(1)}, u32[]{:S(2)}, u32[]{:S(2)}) %collective-permute-start.29) | collective-permute-done | bytes 645152 | tf_op jit(solution)/shard_map/ppermute | solution.py:57
  254.0 6.6 %collective-permute-done.45 = bf16[72,1120]{1,0:T(8,128)(2,1)S(1)} collective-permute-done((bf16[72,1120]{1,0:T(8,128)(2,1)S(1)}, bf16[72,1120]{1,0:T(8,128)(2,1)S(1)}, u32[]{:S(2)}, u32[]{:S(2)}) %collective-permute-start.45) | collective-permute-done | bytes 161312 | tf_op jit(solution)/shard_map/ppermute | solution.py:57
  260.7 3.3 collective-permute-done.44
  264.2 16.2 %collective-permute-done.43 = bf16[288,1120]{1,0:T(8,128)(2,1)S(1)} collective-permute-done((bf16[288,1120]{1,0:T(8,128)(2,1)S(1)}, bf16[288,1120]{1,0:T(8,128)(2,1)S(1)}, u32[]{:S(2)}, u32[]{:S(2)}) %collective-permute-start.43) | collective-permute-done | bytes 645152 | tf_op jit(solution)/shard_map/ppermute | solution.py:57
  303.1 17.9 %collective-permute-done.49 = bf16[144,1120]{1,0:T(8,128)(2,1)} collective-permute-done((bf16[144,1120]{1,0:T(8,128)(2,1)}, bf16[144,1120]{1,0:T(8,128)(2,1)}, u32[]{:S(2)}, u32[]{:S(2)}) %collective-permute-start.49) | collective-permute-done | bytes 322592 | tf_op jit(solution)/shard_map/ppermute | solution.py:57
  326.5 3.3 shard_map.157
  336.6 4.9 %shard_map.160 = (f32[840,1120]{1,0:T(8,128)}, f32[280,1120]{1,0:T(8,128)}) custom-call(s32[3]{0:T(128)} %add_add_fusion.1.at_ref, bf16[288,1120]{1,0:T(8,128)(2,1)} %pad_maximum_fusion.9.own_ref, bf16[288,1120]{1,0:T(8,128)(2,1)} %collective-permute-done.52.other_ref, f32[840,1120]{1,0:T(8,128)} %shard_map.159.whole_ref), custom_call_target="tpu_custom_call", output_to_operand_aliasing={{0}: (3, {})} | custom-call | bytes 576 | tf_op jit(solution)/shard_map/pallas_call | solution.py:167
  (319 shorter events, 159.2 us)
Async XLA Ops:
  18.9 21.0 %collective-permute-start.3 = (bf16[280,1120]{1,0:T(8,128)(2,1)}, bf16[280,1120]{1,0:T(8,128)(2,1)}, u32[]{:S(2)}, u32[]{:S(2)}) collective-permute-start(bf16[280,1120]{1,0:T(8,128)(2,1)} %param.13), channel_id=1, source_target_pairs={{0,2},{1,3},{2,0},{3,1},{4,6},{5,7},{6,4},{7,5},{8,10},{9,11},{10,... | collective-permute-start | bytes 1881608 | tf_op jit(solution)/shard_map/ppermute | solution.py:43
  20.7 31.5 %collective-permute-start.6 = (bf16[280,1120]{1,0:T(8,128)(2,1)}, bf16[280,1120]{1,0:T(8,128)(2,1)}, u32[]{:S(2)}, u32[]{:S(2)}) collective-permute-start(bf16[280,1120]{1,0:T(8,128)(2,1)} %param.13), channel_id=1, source_target_pairs={{0,1},{1,0},{2,3},{3,2},{4,5},{5,4},{6,7},{7,6},{8,9},{9,8},{10,11... | collective-permute-start | bytes 1881608 | tf_op jit(solution)/shard_map/ppermute | solution.py:43
  20.9 28.0 %collective-permute-start.2 = (bf16[1120,256]{1,0:T(8,128)(2,1)}, bf16[1120,256]{1,0:T(8,128)(2,1)}, u32[]{:S(2)}, u32[]{:S(2)}) collective-permute-start(bf16[1120,256]{1,0:T(8,128)(2,1)} %fusion.68), channel_id=1, source_target_pairs={{0,2},{1,3},{2,0},{3,1},{4,6},{5,7},{6,4},{7,5},{8,10},{9,11},{10,... | collective-permute-start | bytes 1720328 | tf_op jit(solution)/shard_map/ppermute | solution.py:43
  21.3 41.6 %collective-permute-start.11 = (bf16[1120,256]{1,0:T(8,128)(2,1)}, bf16[1120,256]{1,0:T(8,128)(2,1)}, u32[]{:S(2)}, u32[]{:S(2)}) collective-permute-start(bf16[1120,256]{1,0:T(8,128)(2,1)} %fusion.68), channel_id=1, source_target_pairs={{0,1},{1,0},{2,3},{3,2},{4,5},{5,4},{6,7},{7,6},{8,9},{9,8},{10,11... | collective-permute-start | bytes 1720328 | tf_op jit(solution)/shard_map/ppermute | solution.py:43
  94.3 52.6 %collective-permute-start.23 = (bf16[560,1120]{1,0:T(8,128)(2,1)}, bf16[560,1120]{1,0:T(8,128)(2,1)}, u32[]{:S(2)}, u32[]{:S(2)}) collective-permute-start(bf16[560,1120]{1,0:T(8,128)(2,1)} %dynamic-slice_bitcast_fusion.1), channel_id=1, source_target_pairs={{0,4},{4,0},{8,12},{12,8},{16,20},{20,16},{24,28},{28,24},{1,5},{5... | collective-permute-start | bytes 3763208 | tf_op jit(solution)/shard_map/ppermute | solution.py:57
  106.7 43.5 %collective-permute-start.22 = (bf16[560,1120]{1,0:T(8,128)(2,1)}, bf16[560,1120]{1,0:T(8,128)(2,1)}, u32[]{:S(2)}, u32[]{:S(2)}) collective-permute-start(bf16[560,1120]{1,0:T(8,128)(2,1)} %dynamic-slice_bitcast_fusion), channel_id=1, source_target_pairs={{0,8},{4,12},{8,0},{12,4},{16,24},{20,28},{24,16},{28,20},{1,9},{5... | collective-permute-start | bytes 3763208 | tf_op jit(solution)/shard_map/ppermute | solution.py:57
  127.2 74.0 %collective-permute-start.17 = (bf16[1120,512]{1,0:T(8,128)(2,1)}, bf16[1120,512]{1,0:T(8,128)(2,1)}, u32[]{:S(2)}, u32[]{:S(2)}) collective-permute-start(bf16[1120,512]{1,0:T(8,128)(2,1)} %fusion.14), channel_id=1, source_target_pairs={{0,1},{1,0},{2,3},{3,2},{4,5},{5,4},{6,7},{7,6},{8,9},{9,8},{10,11... | collective-permute-start | bytes 3440648 | tf_op jit(solution)/shard_map/ppermute | solution.py:43
  128.8 30.3 %collective-permute-start.21 = (bf16[1120,256]{1,0:T(8,128)(2,1)S(1)}, bf16[1120,256]{1,0:T(8,128)(2,1)}, u32[]{:S(2)}, u32[]{:S(2)}) collective-permute-start(bf16[1120,256]{1,0:T(8,128)(2,1)S(1)} %multiply_convert_fusion), channel_id=1, source_target_pairs={{0,2},{1,3},{2,0},{3,1},{4,6},{5,7},{6,4},{7,5},{8,10},{9,11},{10,... | collective-permute-start | bytes 1720328 | tf_op jit(solution)/shard_map/ppermute | solution.py:43
  130.0 47.4 %collective-permute-start.25 = (bf16[1120,256]{1,0:T(8,128)(2,1)S(1)}, bf16[1120,256]{1,0:T(8,128)(2,1)}, u32[]{:S(2)}, u32[]{:S(2)}) collective-permute-start(bf16[1120,256]{1,0:T(8,128)(2,1)S(1)} %multiply_convert_fusion), channel_id=1, source_target_pairs={{0,1},{1,0},{2,3},{3,2},{4,5},{5,4},{6,7},{7,6},{8,9},{9,8},{10,11... | collective-permute-start | bytes 1720328 | tf_op jit(solution)/shard_map/ppermute | solution.py:43
  166.7 25.1 %collective-permute-start.32 = (bf16[144,1120]{1,0:T(8,128)(2,1)S(1)}, bf16[144,1120]{1,0:T(8,128)(2,1)S(1)}, u32[]{:S(2)}, u32[]{:S(2)}) collective-permute-start(bf16[144,1120]{1,0:T(8,128)(2,1)S(1)} %select_convert_fusion.1), channel_id=1, source_target_pairs={{0,16},{4,20},{8,24},{12,28},{16,0},{20,4},{24,8},{28,12},{1,17},{... | collective-permute-start | bytes 967688 | tf_op jit(solution)/shard_map/ppermute | solution.py:57
  174.7 23.1 %collective-permute-start.31 = (bf16[144,1120]{1,0:T(8,128)(2,1)S(1)}, bf16[144,1120]{1,0:T(8,128)(2,1)S(1)}, u32[]{:S(2)}, u32[]{:S(2)}) collective-permute-start(bf16[144,1120]{1,0:T(8,128)(2,1)S(1)} %select_convert_fusion), channel_id=1, source_target_pairs={{0,16},{4,20},{8,24},{12,28},{16,0},{20,4},{24,8},{28,12},{1,17},{... | collective-permute-start | bytes 967688 | tf_op jit(solution)/shard_map/ppermute | solution.py:57
  203.3 32.4 %collective-permute-start.24 = (bf16[1120,256]{1,0:T(8,128)(2,1)S(1)}, bf16[1120,256]{1,0:T(8,128)(2,1)S(1)}, u32[]{:S(2)}, u32[]{:S(2)}) collective-permute-start(bf16[1120,256]{1,0:T(8,128)(2,1)S(1)} %fusion.59), channel_id=1, source_target_pairs={{0,2},{1,3},{2,0},{3,1},{4,6},{5,7},{6,4},{7,5},{8,10},{9,11},{10,... | collective-permute-start | bytes 1720328 | tf_op jit(solution)/shard_map/ppermute | solution.py:43
  204.9 30.7 %collective-permute-start.29 = (bf16[288,1120]{1,0:T(8,128)(2,1)S(1)}, bf16[288,1120]{1,0:T(8,128)(2,1)S(1)}, u32[]{:S(2)}, u32[]{:S(2)}) collective-permute-start(bf16[288,1120]{1,0:T(8,128)(2,1)S(1)} %dynamic-slice_bitcast_fusion.2), channel_id=1, source_target_pairs={{0,8},{4,12},{8,0},{12,4},{16,24},{20,28},{24,16},{28,20},{1,9},{5... | collective-permute-start | bytes 1935368 | tf_op jit(solution)/shard_map/ppermute | solution.py:57
  205.6 45.2 %collective-permute-start.39 = (bf16[144,1120]{1,0:T(8,128)(2,1)S(1)}, bf16[144,1120]{1,0:T(8,128)(2,1)S(1)}, u32[]{:S(2)}, u32[]{:S(2)}) collective-permute-start(bf16[144,1120]{1,0:T(8,128)(2,1)S(1)} %add_convert_fusion.5), channel_id=1, source_target_pairs={{0,16},{4,20},{8,24},{12,28},{16,0},{20,4},{24,8},{28,12},{1,17},{... | collective-permute-start | bytes 967688 | tf_op jit(solution)/shard_map/ppermute | solution.py:57
  210.5 40.5 %collective-permute-start.38 = (bf16[144,1120]{1,0:T(8,128)(2,1)S(1)}, bf16[144,1120]{1,0:T(8,128)(2,1)S(1)}, u32[]{:S(2)}, u32[]{:S(2)}) collective-permute-start(bf16[144,1120]{1,0:T(8,128)(2,1)S(1)} %add_convert_fusion.4), channel_id=1, source_target_pairs={{0,16},{4,20},{8,24},{12,28},{16,0},{20,4},{24,8},{28,12},{1,17},{... | collective-permute-start | bytes 967688 | tf_op jit(solution)/shard_map/ppermute | solution.py:57
  250.9 29.5 %collective-permute-start.43 = (bf16[288,1120]{1,0:T(8,128)(2,1)S(1)}, bf16[288,1120]{1,0:T(8,128)(2,1)S(1)}, u32[]{:S(2)}, u32[]{:S(2)}) collective-permute-start(bf16[288,1120]{1,0:T(8,128)(2,1)S(1)} %pad_maximum_fusion.6), channel_id=1, source_target_pairs={{0,8},{4,12},{8,0},{12,4},{16,24},{20,28},{24,16},{28,20},{1,9},{5... | collective-permute-start | bytes 1935368 | tf_op jit(solution)/shard_map/ppermute | solution.py:57
  251.9 38.9 %collective-permute-start.51 = (bf16[288,1120]{1,0:T(8,128)(2,1)}, bf16[288,1120]{1,0:T(8,128)(2,1)}, u32[]{:S(2)}, u32[]{:S(2)}) collective-permute-start(bf16[288,1120]{1,0:T(8,128)(2,1)} %pad_maximum_fusion.7), channel_id=1, source_target_pairs={{0,4},{4,0},{8,12},{12,8},{16,20},{20,16},{24,28},{28,24},{1,5},{5... | collective-permute-start | bytes 1935368 | tf_op jit(solution)/shard_map/ppermute | solution.py:57
  252.6 33.0 %collective-permute-start.42 = (f32[2,1120]{1,0:T(2,128)S(1)}, f32[2,1120]{1,0:T(2,128)S(1)}, u32[]{:S(2)}, u32[]{:S(2)}) collective-permute-start(f32[2,1120]{1,0:T(2,128)S(1)} %add.325), channel_id=1, source_target_pairs={{0,4},{4,0},{8,12},{12,8},{16,20},{20,16},{24,28},{28,24},{1,5},{5... | collective-permute-start | bytes 26888 | tf_op jit(solution)/shard_map/ppermute | solution.py:559
  260.6 25.0 %collective-permute-start.48 = (bf16[72,1120]{1,0:T(8,128)(2,1)S(1)}, bf16[72,1120]{1,0:T(8,128)(2,1)}, u32[]{:S(2)}, u32[]{:S(2)}) collective-permute-start(bf16[72,1120]{1,0:T(8,128)(2,1)S(1)} %add_convert_fusion.7), channel_id=1, source_target_pairs={{0,16},{4,20},{8,24},{12,28},{16,0},{20,4},{24,8},{28,12},{1,17},{... | collective-permute-start | bytes 483848 | tf_op jit(solution)/shard_map/ppermute | solution.py:57
  264.1 24.6 %collective-permute-start.47 = (bf16[72,1120]{1,0:T(8,128)(2,1)S(1)}, bf16[72,1120]{1,0:T(8,128)(2,1)S(1)}, u32[]{:S(2)}, u32[]{:S(2)}) collective-permute-start(bf16[72,1120]{1,0:T(8,128)(2,1)S(1)} %add_convert_fusion.6), channel_id=1, source_target_pairs={{0,16},{4,20},{8,24},{12,28},{16,0},{20,4},{24,8},{28,12},{1,17},{... | collective-permute-start | bytes 483848 | tf_op jit(solution)/shard_map/ppermute | solution.py:57
  281.6 44.9 %collective-permute-start.55 = (bf16[576,1120]{1,0:T(8,128)(2,1)}, bf16[576,1120]{1,0:T(8,128)(2,1)}, u32[]{:S(2)}, u32[]{:S(2)}) collective-permute-start(bf16[576,1120]{1,0:T(8,128)(2,1)} %pad_maximum_fusion.3.half_ref), channel_id=1, source_target_pairs={{0,4},{4,0},{8,12},{12,8},{16,20},{20,16},{24,28},{28,24},{1,5},{5... | collective-permute-start | bytes 3870728 | tf_op jit(solution)/shard_map/ppermute | solution.py:57
  289.5 31.5 %collective-permute-start.49 = (bf16[144,1120]{1,0:T(8,128)(2,1)}, bf16[144,1120]{1,0:T(8,128)(2,1)}, u32[]{:S(2)}, u32[]{:S(2)}) collective-permute-start(bf16[144,1120]{1,0:T(8,128)(2,1)} %pad_maximum_fusion.15), channel_id=1, source_target_pairs={{0,4},{4,0},{8,12},{12,8},{16,20},{20,16},{24,28},{28,24},{1,5},{5... | collective-permute-start | bytes 967688 | tf_op jit(solution)/shard_map/ppermute | solution.py:57
  293.1 36.7 %collective-permute-start.54 = (bf16[576,1120]{1,0:T(8,128)(2,1)}, bf16[576,1120]{1,0:T(8,128)(2,1)}, u32[]{:S(2)}, u32[]{:S(2)}) collective-permute-start(bf16[576,1120]{1,0:T(8,128)(2,1)} %pad_maximum_fusion.4.half_ref), channel_id=1, source_target_pairs={{0,8},{4,12},{8,0},{12,4},{16,24},{20,28},{24,16},{28,20},{1,9},{5... | collective-permute-start | bytes 3870728 | tf_op jit(solution)/shard_map/ppermute | solution.py:57
  301.3 31.8 %collective-permute-start.53 = (bf16[288,1120]{1,0:T(8,128)(2,1)}, bf16[288,1120]{1,0:T(8,128)(2,1)}, u32[]{:S(2)}, u32[]{:S(2)}) collective-permute-start(bf16[288,1120]{1,0:T(8,128)(2,1)} %pad_maximum_fusion.8.half_ref), channel_id=1, source_target_pairs={{0,4},{4,0},{8,12},{12,8},{16,20},{20,16},{24,28},{28,24},{1,5},{5... | collective-permute-start | bytes 1935368 | tf_op jit(solution)/shard_map/ppermute | solution.py:57
  (82 other events, 713.3 us)

commit v3 on v2

--- a/solution.py
+++ b/solution.py
@@ -499,11 +499,12 @@
         mlp_kept = dot(down_weight, after(hidden_on[:, :half], mlp_sent), ((0,), (0,)))
         mix_y = after(mix_y, mlp_kept)
         grad_mixed = jnp.concatenate([piece[0], mix_y, mix_c, mix_d], axis=0)
-        attn_on = after(grad_attn, grad_mixed)
+        mark = down.advance(grad_mixed)
+        attn_on = after(grad_attn, mark)
         attn_y, attn_c = narrow.send(attn_on, 2), narrow.send(attn_on, 1)
         grad_proj = attend_back(me_ref, projected, lse, mixed, after(grad_mixed, attn_on), rows, heads)
-        mark = down.advance(grad_proj)
-        mark = up.advance(mark)
+        mark = up.advance(grad_proj)
+        mark = down.advance(mark)
         grad_proj = after(grad_proj, mark)
         attn_y = after(attn_y, grad_proj)
         attn_d = narrow.send(attn_y, 1)
@@ -523,16 +524,17 @@
         filled = lambda a: jnp.pad(a, ((0, cut // 2 - a.shape[0]), (0, 0)))
         first = WideSum(wide, (1, 2, 4), qkv_part[:cut], 3 * own_width)
         mark = first.advance()
-        mark = down.advance(mark)
         mark = up.advance(mark)
         attn_rows = jnp.concatenate([grad_attn, attn_y, attn_c, after(attn_d, mark)], axis=1)
         out_part = dot(mixed[:, : heads * HP], attn_rows, ((0,), (1,))).astype(BF16)
         out_part = out_part.reshape(heads, HP, width)[:, :HS].reshape(own_width, width)
         second_part = jnp.concatenate([filled(qkv_part[cut:]), filled(out_part)], axis=0)
-        second = WideSum(wide, (2, 1, 4), second_part, last=True)
+        second = WideSum(wide, (1, 2, 4), second_part, last=True)
         mark = second.advance()
+        mark = first.advance(mark)
         mark = down.advance(mark)
         mark = up.advance(mark)
+        mark = second.advance(mark)
         grad_proj = after(grad_proj, mark)
         one_sent = dot(proj, grad_proj[half:], ((0,), (1,))).astype(BF16)
         one_got = narrow.send(one_sent, 1)
@@ -541,7 +543,9 @@
         one_sum = (one_kept[:, rows:] + one_got[:, rows:]).astype(BF16)
         one_far = narrow.send(one_sum, 2)
         one_near = one_kept[:, :rows] + one_got[:, :rows]
-        mark = first.advance(one_sum)
+        mark = down.advance(one_sum)
+        mark = up.advance(mark)
+        mark = first.advance(mark)
         mark = second.advance(mark)
         mlp_own = mlp_near + after(mlp_send_far, mark).astype(F32)
         block_output = (middle + own_live * mlp_own).astype(BF16)
@@ -553,7 +557,7 @@
         for hop in (1, 2):
             gains = gains + narrow.send(gains, hop)
         mark = gains
-        turns = [[first, second, down, up], [first, second, down], [first, second]]
+        turns = [[first, second], [down], [first, second]]
         order = (4, 1, 2) + tuple(8 * 2**i for i in range(wide.bit_length() - 4))
         for hop in order:
             got = lax.ppermute(gains, "wide", [(i, i ^ hop) for i in range(wide)])
@@ -561,7 +565,7 @@
                 mark = s.advance(mark, gains)
             gains = gains + after(got, mark)
         mark = up.advance(mark, gains)
-        for s in (first, second, down, up, first, second):
+        for s in (first, second, down, first, up, second):
             mark = s.advance(mark)
 
         if wide == 8:

time: 348 us -> 340 us (0.977)
  waiting for transfers between devices: 122 us -> 107 us
  starting transfers between devices: 49.7 us -> 55.6 us
    ppermute x24, waiting for transfers between devices: 94.7 us -> 77.1 us  [send(): lax.ppermute(value, 'wide', [(i, i ^ hop) for i in range(self.size)])]
    ppermute x24, starting transfers between devices: 26.5 us -> 33 us  [send(): lax.ppermute(value, 'wide', [(i, i ^ hop) for i in range(self.size)])]
    unnamed x100 -> x108, local copies, waits for them, and re-layouts: 8.09 us -> 10.2 us
  transfers between devices with their start and end apart: 56 -> 56, of which waited for: 19 -> 23; matrix products, arithmetic and copies ran while one was open for 28% -> 29% of each run, Pallas kernels for 13% -> 14%
where the time goes in v3:
time: 340 us; the launch traced here: 334 us
  waiting for transfers between devices  107 us (31%)
  starting transfers between devices  55.6 us (16%)
  Pallas kernels  50.7 us (15%)
  matrix products  48.5 us (14%)
  other arithmetic  44.2 us (13%)
  local copies, waits for them, and re-layouts  25.4 us (7%)
    ppermute x24, waiting for transfers between devices, send(): lax.ppermute(value, 'wide', [(i, i ^ hop) for i in range(self.size)])  77.1 us
    dot_general x21, matrix products, dot(): return lax.dot_general(a, b, (dims, ((), ())), preferred_element_type=F32)  48.5 us
    ppermute x24, starting transfers between devices, send(): lax.ppermute(value, 'wide', [(i, i ^ hop) for i in range(self.size)])  33 us
    ppermute x29, waiting for transfers between devices, send(): return lax.ppermute(value, 'narrow', self.perm[k])  29.7 us
    pallas_call x6, Pallas kernels, join(): pl.pallas_call(partial(join_kernel, quarter), out_shape=jax.ShapeDtypeStr...  19.1 us
    ppermute x29, starting transfers between devices, send(): return lax.ppermute(value, 'narrow', self.perm[k])  18.8 us
    pallas_call x1, Pallas kernels, attend_back(): pl.pallas_call(partial(attend_back_kernel, heads % 2 == 1), out_shape=jax...  15.6 us
    pallas_call x1, Pallas kernels, attend(): pl.pallas_call(partial(attend_kernel, heads % 2 == 1), out_shape=(jax.Sha...  11 us
  transfers between devices with their start and end apart: 56, of which 23 were waited for; matrix products, arithmetic and copies ran while one was open for 29% of the time, Pallas kernels for 14%

profile of v3, /device:TPU:0, one launch (start us, length us, event | category | flops | bytes accessed | tf_op | source)
XLA Modules:
  0.0 333.8 jit_solution(12344493898181118779)
XLA Ops:
  24.6 4.3 %convolution_convert_fusion.7.refs_0_.refs_1_.refs_2_.refs_3_.refs_4_.refs_5_.refs_6_.refs_7_.refs_8_.refs_9_.refs_10_.refs_11_ = bf16[1024,1024]{1,0:T(8,128)(2,1)} fusion(bf16[1120,256]{1,0:T(8,128)(2,1)S(1)} %get-tuple-element.148, bf16[1120,256]{1,0:T(8,128)(2,1)S(1)} %get-tuple-element.149, bf16[1120,256]{1,0:T(8,128)(2,1)S(1)} %get-tuple-element.147, ...), kind=kOutput, calls=%fused_computation.50 | convolution fusion | flops 2365915136 | bytes 6541312 | tf_op jit(solution)/shard_map/dot_general | solution.py:31
  29.0 11.0 %shard_map.152 = (bf16[1024,384]{1,0:T(8,128)(2,1)}, f32[3,4,8,256]{3,2,1,0:T(8,128)}) custom-call(s32[1]{0:T(128)} %bitcast.12.me_ref, bf16[1024,1024]{1,0:T(8,128)(2,1)} %convolution_convert_fusion.7.refs_0_.refs_1_.refs_2_.refs_3_.refs_4_.refs_5_.refs_6_.refs_7_.refs_8_.refs_9_.refs_10_.refs_11_, ...), custom_call_target="tpu_custom_call" | custom-call | flops 256 | bytes 256 | tf_op jit(solution)/shard_map/pallas_call | solution.py:345
  43.5 5.4 %collective-permute-done.2 = bf16[1120,256]{1,0:T(8,128)(2,1)} collective-permute-done((bf16[1120,256]{1,0:T(8,128)(2,1)}, bf16[1120,256]{1,0:T(8,128)(2,1)}, u32[]{:S(2)}, u32[]{:S(2)}) %collective-permute-start.2) | collective-permute-done | bytes 573472 | tf_op jit(solution)/shard_map/ppermute | solution.py:43
  64.1 4.8 %convolution_bitcast_fusion = f32[1120,1024]{1,0:T(8,128)} fusion(bf16[1120,1120]{1,0:T(8,128)(2,1)S(1)} %copy-done.50, bf16[1120,1024]{1,0:T(8,128)(2,1)S(1)} %constant_dynamic-update-slice_fusion), kind=kOutput, calls=%fused_computation.17 | convolution fusion | flops 2569011200 | bytes 9390080 | tf_op jit(solution)/shard_map/dot_general | solution.py:31
  68.9 6.7 %collective-permute-done.10 = bf16[1120,256]{1,0:T(8,128)(2,1)} collective-permute-done((bf16[1120,256]{1,0:T(8,128)(2,1)}, bf16[1120,256]{1,0:T(8,128)(2,1)}, u32[]{:S(2)}, u32[]{:S(2)}) %collective-permute-start.10) | collective-permute-done | bytes 573472 | tf_op jit(solution)/shard_map/ppermute | solution.py:43
  77.9 7.2 %fusion.6 = (bf16[1120,1024]{1,0:T(8,128)(2,1)S(1)}, bf16[1120,1024]{1,0:T(8,128)(2,1)S(1)}) fusion(f32[1120,1024]{1,0:T(8,128)} %convolution_bitcast_fusion, bf16[1120,1120]{1,0:T(8,128)(2,1)S(1)} %copy-done, bf16[1120,256]{1,0:T(8,128)(2,1)} %collective-permute-done.14, bf16[1120,256]{1,0:T(8,128)(2,1)} %collective-permute-done.13, ...), kind=kOutput, calls=%fused_computation.10 | convolution fusion | flops 2591948800 | bytes 13977600 | tf_op jit(solution)/shard_map/dot_general | solution.py:31
  85.2 3.6 %convolution_convert_fusion.1 = bf16[1120,1120]{1,0:T(8,128)(2,1)S(1)} fusion(bf16[1120,1024]{1,0:T(8,128)(2,1)S(1)} %get-tuple-element.87, bf16[1120,1024]{1,0:T(8,128)(2,1)S(1)} %copy-done.47), kind=kOutput, calls=%fused_computation.1 | convolution fusion | flops 2570265600 | bytes 7096320 | tf_op jit(solution)/shard_map/dot_general | solution.py:31
  100.9 4.7 %convolution_convert_fusion = bf16[1120,1120]{1,0:T(8,128)(2,1)S(1)} fusion(bf16[1120,1024]{1,0:T(8,128)(2,1)S(1)} %copy-done.43, bf16[1120,256]{1,0:T(8,128)(2,1)} %collective-permute-done.14, bf16[1120,256]{1,0:T(8,128)(2,1)} %collective-permute-done.13, bf16[1120,256]{1,0:T(8,128)(2,1)} %collective-permute-done.10, bf16[1120,256]{1,0:T(8,128)(2,1)} %multiply_convert_fusion.1), kind=kOutput, calls=%fused_computation | convolution fusion | flops 2579440640 | bytes 7096320 | tf_op jit(solution)/shard_map/dot_general | solution.py:31
  108.4 6.2 %collective-permute-done.16 = bf16[1120,256]{1,0:T(8,128)(2,1)S(1)} collective-permute-done((bf16[1120,256]{1,0:T(8,128)(2,1)S(1)}, bf16[1120,256]{1,0:T(8,128)(2,1)S(1)}, u32[]{:S(2)}, u32[]{:S(2)}) %collective-permute-start.16) | collective-permute-done | bytes 573472 | tf_op jit(solution)/shard_map/ppermute | solution.py:43
  138.9 15.6 %shard_map.153 = bf16[1024,1024]{1,0:T(8,128)(2,1)} custom-call(s32[1]{0:T(128)} %bitcast.12.me_ref, bf16[1024,1024]{1,0:T(8,128)(2,1)} %convolution_convert_fusion.7.refs_0_.refs_1_.refs_2_.refs_3_.refs_4_.refs_5_.refs_6_.refs_7_.refs_8_.refs_9_.refs_10_.refs_11_, ...), custom_call_target="tpu_custom_call" | custom-call | flops 256 | bytes 256 | tf_op jit(solution)/shard_map/pallas_call | solution.py:374
  167.3 5.8 %collective-permute-done.28 = bf16[280,1120]{1,0:T(8,128)(2,1)S(1)} collective-permute-done((bf16[280,1120]{1,0:T(8,128)(2,1)S(1)}, bf16[280,1120]{1,0:T(8,128)(2,1)S(1)}, u32[]{:S(2)}, u32[]{:S(2)}) %collective-permute-start.28) | collective-permute-done | bytes 627232 | tf_op jit(solution)/shard_map/ppermute | solution.py:57
  182.2 8.7 %collective-permute-done.32 = bf16[288,1120]{1,0:T(8,128)(2,1)S(1)} collective-permute-done((bf16[288,1120]{1,0:T(8,128)(2,1)S(1)}, bf16[288,1120]{1,0:T(8,128)(2,1)S(1)}, u32[]{:S(2)}, u32[]{:S(2)}) %collective-permute-start.32) | collective-permute-done | bytes 645152 | tf_op jit(solution)/shard_map/ppermute | solution.py:57
  191.2 5.6 %collective-permute-done.30 = bf16[144,1120]{1,0:T(8,128)(2,1)S(1)} collective-permute-done((bf16[144,1120]{1,0:T(8,128)(2,1)S(1)}, bf16[144,1120]{1,0:T(8,128)(2,1)S(1)}, u32[]{:S(2)}, u32[]{:S(2)}) %collective-permute-start.30) | collective-permute-done | bytes 322592 | tf_op jit(solution)/shard_map/ppermute | solution.py:57
  196.9 6.9 %collective-permute-done.29 = bf16[288,1120]{1,0:T(8,128)(2,1)S(1)} collective-permute-done((bf16[288,1120]{1,0:T(8,128)(2,1)S(1)}, bf16[288,1120]{1,0:T(8,128)(2,1)S(1)}, u32[]{:S(2)}, u32[]{:S(2)}) %collective-permute-start.29) | collective-permute-done | bytes 645152 | tf_op jit(solution)/shard_map/ppermute | solution.py:57
  217.8 11.6 %collective-permute-done.36 = bf16[144,1120]{1,0:T(8,128)(2,1)S(1)} collective-permute-done((bf16[144,1120]{1,0:T(8,128)(2,1)S(1)}, bf16[144,1120]{1,0:T(8,128)(2,1)S(1)}, u32[]{:S(2)}, u32[]{:S(2)}) %collective-permute-start.36) | collective-permute-done | bytes 322592 | tf_op jit(solution)/shard_map/ppermute | solution.py:57
  229.9 12.9 %collective-permute-done.35 = bf16[144,1120]{1,0:T(8,128)(2,1)S(1)} collective-permute-done((bf16[144,1120]{1,0:T(8,128)(2,1)S(1)}, bf16[144,1120]{1,0:T(8,128)(2,1)S(1)}, u32[]{:S(2)}, u32[]{:S(2)}) %collective-permute-start.35) | collective-permute-done | bytes 322592 | tf_op jit(solution)/shard_map/ppermute | solution.py:57
  261.8 3.5 %collective-permute-start.48 = (bf16[72,1120]{1,0:T(8,128)(2,1)S(1)}, bf16[72,1120]{1,0:T(8,128)(2,1)S(1)}, u32[]{:S(2)}, u32[]{:S(2)}) collective-permute-start(bf16[72,1120]{1,0:T(8,128)(2,1)S(1)} %add_convert_fusion.7), channel_id=1, source_target_pairs={{0,16},{4,20},{8,24},{12,28},{16,0},{20,4},{24,8},{28,12},{1,17},{... | collective-permute-start | bytes 483848 | tf_op jit(solution)/shard_map/ppermute | solution.py:57
  265.4 3.5 %collective-permute-start.47 = (bf16[72,1120]{1,0:T(8,128)(2,1)S(1)}, bf16[72,1120]{1,0:T(8,128)(2,1)S(1)}, u32[]{:S(2)}, u32[]{:S(2)}) collective-permute-start(bf16[72,1120]{1,0:T(8,128)(2,1)S(1)} %add_convert_fusion.6), channel_id=1, source_target_pairs={{0,16},{4,20},{8,24},{12,28},{16,0},{20,4},{24,8},{28,12},{1,17},{... | collective-permute-start | bytes 483848 | tf_op jit(solution)/shard_map/ppermute | solution.py:57
  272.2 3.3 shard_map.154.refs_0_
  303.0 3.3 shard_map.157
  306.4 10.9 %collective-permute-done.54.half_ref = bf16[288,1120]{1,0:T(8,128)(2,1)} collective-permute-done((bf16[288,1120]{1,0:T(8,128)(2,1)}, bf16[288,1120]{1,0:T(8,128)(2,1)}, u32[]{:S(2)}, u32[]{:S(2)}) %collective-permute-start.54) | collective-permute-done | bytes 645152 | tf_op jit(solution)/shard_map/ppermute | solution.py:57
  320.0 4.3 %collective-permute-done.53.half_ref = bf16[576,1120]{1,0:T(8,128)(2,1)} collective-permute-done((bf16[576,1120]{1,0:T(8,128)(2,1)}, bf16[576,1120]{1,0:T(8,128)(2,1)}, u32[]{:S(2)}, u32[]{:S(2)}) %collective-permute-start.53) | collective-permute-done | bytes 1290272 | tf_op jit(solution)/shard_map/ppermute | solution.py:57
  324.3 3.5 %shard_map.159 = f32[1120,1120]{1,0:T(8,128)} custom-call(s32[3]{0:T(128)} %add_add_fusion.1.at_ref, bf16[576,1120]{1,0:T(8,128)(2,1)} %collective-permute-done.53.half_ref, f32[1120,1120]{1,0:T(8,128)} %shard_map.155.refs_0_), custom_call_target="tpu_custom_call", output_to_operand_aliasing={{}: (2, {})} | custom-call | bytes 1120 | tf_op jit(solution)/shard_map/pallas_call | solution.py:132
  328.7 4.9 %shard_map.160 = (f32[840,1120]{1,0:T(8,128)}, f32[280,1120]{1,0:T(8,128)}) custom-call(s32[3]{0:T(128)} %add_add_fusion.at_ref, bf16[288,1120]{1,0:T(8,128)(2,1)} %pad_maximum_fusion.9.own_ref, bf16[288,1120]{1,0:T(8,128)(2,1)} %collective-permute-done.52.other_ref, f32[840,1120]{1,0:T(8,128)} %shard_map.158.whole_ref), custom_call_target="tpu_custom_call", output_to_operand_aliasing={{0}: (3, {})} | custom-call | bytes 576 | tf_op jit(solution)/shard_map/pallas_call | solution.py:167
  (327 shorter events, 172.7 us)
Async XLA Ops:
  18.9 21.1 %collective-permute-start.3 = (bf16[280,1120]{1,0:T(8,128)(2,1)}, bf16[280,1120]{1,0:T(8,128)(2,1)}, u32[]{:S(2)}, u32[]{:S(2)}) collective-permute-start(bf16[280,1120]{1,0:T(8,128)(2,1)} %param.13), channel_id=1, source_target_pairs={{0,2},{1,3},{2,0},{3,1},{4,6},{5,7},{6,4},{7,5},{8,10},{9,11},{10,... | collective-permute-start | bytes 1881608 | tf_op jit(solution)/shard_map/ppermute | solution.py:43
  20.7 31.5 %collective-permute-start.6 = (bf16[280,1120]{1,0:T(8,128)(2,1)}, bf16[280,1120]{1,0:T(8,128)(2,1)}, u32[]{:S(2)}, u32[]{:S(2)}) collective-permute-start(bf16[280,1120]{1,0:T(8,128)(2,1)} %param.13), channel_id=1, source_target_pairs={{0,1},{1,0},{2,3},{3,2},{4,5},{5,4},{6,7},{7,6},{8,9},{9,8},{10,11... | collective-permute-start | bytes 1881608 | tf_op jit(solution)/shard_map/ppermute | solution.py:43
  20.9 28.0 %collective-permute-start.2 = (bf16[1120,256]{1,0:T(8,128)(2,1)}, bf16[1120,256]{1,0:T(8,128)(2,1)}, u32[]{:S(2)}, u32[]{:S(2)}) collective-permute-start(bf16[1120,256]{1,0:T(8,128)(2,1)} %fusion.68), channel_id=1, source_target_pairs={{0,2},{1,3},{2,0},{3,1},{4,6},{5,7},{6,4},{7,5},{8,10},{9,11},{10,... | collective-permute-start | bytes 1720328 | tf_op jit(solution)/shard_map/ppermute | solution.py:43
  21.3 41.6 %collective-permute-start.11 = (bf16[1120,256]{1,0:T(8,128)(2,1)}, bf16[1120,256]{1,0:T(8,128)(2,1)}, u32[]{:S(2)}, u32[]{:S(2)}) collective-permute-start(bf16[1120,256]{1,0:T(8,128)(2,1)} %fusion.68), channel_id=1, source_target_pairs={{0,1},{1,0},{2,3},{3,2},{4,5},{5,4},{6,7},{7,6},{8,9},{9,8},{10,11... | collective-permute-start | bytes 1720328 | tf_op jit(solution)/shard_map/ppermute | solution.py:43
  94.5 38.0 %collective-permute-start.18 = (bf16[560,1120]{1,0:T(8,128)(2,1)S(1)}, bf16[560,1120]{1,0:T(8,128)(2,1)S(1)}, u32[]{:S(2)}, u32[]{:S(2)}) collective-permute-start(bf16[560,1120]{1,0:T(8,128)(2,1)S(1)} %copy-done.27), channel_id=1, source_target_pairs={{0,4},{4,0},{8,12},{12,8},{16,20},{20,16},{24,28},{28,24},{1,5},{5... | collective-permute-start | bytes 3763208 | tf_op jit(solution)/shard_map/ppermute | solution.py:57
  106.9 47.7 %collective-permute-start.24 = (bf16[560,1120]{1,0:T(8,128)(2,1)}, bf16[560,1120]{1,0:T(8,128)(2,1)}, u32[]{:S(2)}, u32[]{:S(2)}) collective-permute-start(bf16[560,1120]{1,0:T(8,128)(2,1)} %dynamic-slice_bitcast_fusion), channel_id=1, source_target_pairs={{0,8},{4,12},{8,0},{12,4},{16,24},{20,28},{24,16},{28,20},{1,9},{5... | collective-permute-start | bytes 3763208 | tf_op jit(solution)/shard_map/ppermute | solution.py:57
  134.8 21.9 %collective-permute-start.23 = (bf16[280,1120]{1,0:T(8,128)(2,1)S(1)}, bf16[280,1120]{1,0:T(8,128)(2,1)}, u32[]{:S(2)}, u32[]{:S(2)}) collective-permute-start(bf16[280,1120]{1,0:T(8,128)(2,1)S(1)} %fusion.73), channel_id=1, source_target_pairs={{0,8},{4,12},{8,0},{12,4},{16,24},{20,28},{24,16},{28,20},{1,9},{5... | collective-permute-start | bytes 1881608 | tf_op jit(solution)/shard_map/ppermute | solution.py:57
  136.4 70.3 %collective-permute-start.17 = (bf16[1120,512]{1,0:T(8,128)(2,1)}, bf16[1120,512]{1,0:T(8,128)(2,1)}, u32[]{:S(2)}, u32[]{:S(2)}) collective-permute-start(bf16[1120,512]{1,0:T(8,128)(2,1)} %fusion.14), channel_id=1, source_target_pairs={{0,1},{1,0},{2,3},{3,2},{4,5},{5,4},{6,7},{7,6},{8,9},{9,8},{10,11... | collective-permute-start | bytes 3440648 | tf_op jit(solution)/shard_map/ppermute | solution.py:43
  138.4 28.7 %collective-permute-start.22 = (bf16[1120,256]{1,0:T(8,128)(2,1)S(1)}, bf16[1120,256]{1,0:T(8,128)(2,1)}, u32[]{:S(2)}, u32[]{:S(2)}) collective-permute-start(bf16[1120,256]{1,0:T(8,128)(2,1)S(1)} %multiply_convert_fusion), channel_id=1, source_target_pairs={{0,2},{1,3},{2,0},{3,1},{4,6},{5,7},{6,4},{7,5},{8,10},{9,11},{10,... | collective-permute-start | bytes 1720328 | tf_op jit(solution)/shard_map/ppermute | solution.py:43
  138.9 39.0 %collective-permute-start.26 = (bf16[1120,256]{1,0:T(8,128)(2,1)S(1)}, bf16[1120,256]{1,0:T(8,128)(2,1)}, u32[]{:S(2)}, u32[]{:S(2)}) collective-permute-start(bf16[1120,256]{1,0:T(8,128)(2,1)S(1)} %multiply_convert_fusion), channel_id=1, source_target_pairs={{0,1},{1,0},{2,3},{3,2},{4,5},{5,4},{6,7},{7,6},{8,9},{9,8},{10,11... | collective-permute-start | bytes 1720328 | tf_op jit(solution)/shard_map/ppermute | solution.py:43
  164.5 26.6 %collective-permute-start.31 = (bf16[144,1120]{1,0:T(8,128)(2,1)S(1)}, bf16[144,1120]{1,0:T(8,128)(2,1)S(1)}, u32[]{:S(2)}, u32[]{:S(2)}) collective-permute-start(bf16[144,1120]{1,0:T(8,128)(2,1)S(1)} %select_convert_fusion.1), channel_id=1, source_target_pairs={{0,16},{4,20},{8,24},{12,28},{16,0},{20,4},{24,8},{28,12},{1,17},{... | collective-permute-start | bytes 967688 | tf_op jit(solution)/shard_map/ppermute | solution.py:57
  175.3 21.5 %collective-permute-start.30 = (bf16[144,1120]{1,0:T(8,128)(2,1)S(1)}, bf16[144,1120]{1,0:T(8,128)(2,1)S(1)}, u32[]{:S(2)}, u32[]{:S(2)}) collective-permute-start(bf16[144,1120]{1,0:T(8,128)(2,1)S(1)} %select_convert_fusion), channel_id=1, source_target_pairs={{0,16},{4,20},{8,24},{12,28},{16,0},{20,4},{24,8},{28,12},{1,17},{... | collective-permute-start | bytes 967688 | tf_op jit(solution)/shard_map/ppermute | solution.py:57
  180.7 23.2 %collective-permute-start.29 = (bf16[288,1120]{1,0:T(8,128)(2,1)S(1)}, bf16[288,1120]{1,0:T(8,128)(2,1)S(1)}, u32[]{:S(2)}, u32[]{:S(2)}) collective-permute-start(bf16[288,1120]{1,0:T(8,128)(2,1)S(1)} %dynamic-slice_bitcast_fusion.2), channel_id=1, source_target_pairs={{0,4},{4,0},{8,12},{12,8},{16,20},{20,16},{24,28},{28,24},{1,5},{5... | collective-permute-start | bytes 1935368 | tf_op jit(solution)/shard_map/ppermute | solution.py:57
  209.1 38.7 %collective-permute-start.25 = (bf16[1120,256]{1,0:T(8,128)(2,1)S(1)}, bf16[1120,256]{1,0:T(8,128)(2,1)S(1)}, u32[]{:S(2)}, u32[]{:S(2)}) collective-permute-start(bf16[1120,256]{1,0:T(8,128)(2,1)S(1)} %fusion.59), channel_id=1, source_target_pairs={{0,2},{1,3},{2,0},{3,1},{4,6},{5,7},{6,4},{7,5},{8,10},{9,11},{10,... | collective-permute-start | bytes 1720328 | tf_op jit(solution)/shard_map/ppermute | solution.py:43
  213.3 30.6 %collective-permute-start.34 = (bf16[144,1120]{1,0:T(8,128)(2,1)S(1)}, bf16[144,1120]{1,0:T(8,128)(2,1)S(1)}, u32[]{:S(2)}, u32[]{:S(2)}) collective-permute-start(bf16[144,1120]{1,0:T(8,128)(2,1)S(1)} %fusion.77), channel_id=1, source_target_pairs={{0,8},{4,12},{8,0},{12,4},{16,24},{20,28},{24,16},{28,20},{1,9},{5... | collective-permute-start | bytes 967688 | tf_op jit(solution)/shard_map/ppermute | solution.py:57
  213.7 29.1 %collective-permute-start.35 = (bf16[144,1120]{1,0:T(8,128)(2,1)S(1)}, bf16[144,1120]{1,0:T(8,128)(2,1)S(1)}, u32[]{:S(2)}, u32[]{:S(2)}) collective-permute-start(bf16[144,1120]{1,0:T(8,128)(2,1)S(1)} %add_convert_fusion.3), channel_id=1, source_target_pairs={{0,16},{4,20},{8,24},{12,28},{16,0},{20,4},{24,8},{28,12},{1,17},{... | collective-permute-start | bytes 967688 | tf_op jit(solution)/shard_map/ppermute | solution.py:57
  215.6 28.9 %collective-permute-start.33 = (bf16[144,1120]{1,0:T(8,128)(2,1)S(1)}, bf16[144,1120]{1,0:T(8,128)(2,1)S(1)}, u32[]{:S(2)}, u32[]{:S(2)}) collective-permute-start(bf16[144,1120]{1,0:T(8,128)(2,1)S(1)} %fusion.78), channel_id=1, source_target_pairs={{0,8},{4,12},{8,0},{12,4},{16,24},{20,28},{24,16},{28,20},{1,9},{5... | collective-permute-start | bytes 967688 | tf_op jit(solution)/shard_map/ppermute | solution.py:57
  229.4 19.9 %collective-permute-start.38 = (bf16[1120,256]{1,0:T(8,128)(2,1)S(1)}, bf16[1120,256]{1,0:T(8,128)(2,1)S(1)}, u32[]{:S(2)}, u32[]{:S(2)}) collective-permute-start(bf16[1120,256]{1,0:T(8,128)(2,1)S(1)} %fusion.58), channel_id=1, source_target_pairs={{0,2},{1,3},{2,0},{3,1},{4,6},{5,7},{6,4},{7,5},{8,10},{9,11},{10,... | collective-permute-start | bytes 1720328 | tf_op jit(solution)/shard_map/ppermute | solution.py:43
  242.9 26.6 %collective-permute-start.45 = (bf16[288,1120]{1,0:T(8,128)(2,1)S(1)}, bf16[288,1120]{1,0:T(8,128)(2,1)S(1)}, u32[]{:S(2)}, u32[]{:S(2)}) collective-permute-start(bf16[288,1120]{1,0:T(8,128)(2,1)S(1)} %pad_maximum_fusion.6), channel_id=1, source_target_pairs={{0,8},{4,12},{8,0},{12,4},{16,24},{20,28},{24,16},{28,20},{1,9},{5... | collective-permute-start | bytes 1935368 | tf_op jit(solution)/shard_map/ppermute | solution.py:57
  243.8 38.4 %collective-permute-start.51 = (bf16[288,1120]{1,0:T(8,128)(2,1)}, bf16[288,1120]{1,0:T(8,128)(2,1)}, u32[]{:S(2)}, u32[]{:S(2)}) collective-permute-start(bf16[288,1120]{1,0:T(8,128)(2,1)} %pad_maximum_fusion.7), channel_id=1, source_target_pairs={{0,4},{4,0},{8,12},{12,8},{16,20},{20,16},{24,28},{28,24},{1,5},{5... | collective-permute-start | bytes 1935368 | tf_op jit(solution)/shard_map/ppermute | solution.py:57
  270.7 32.3 %collective-permute-start.55 = (bf16[576,1120]{1,0:T(8,128)(2,1)}, bf16[576,1120]{1,0:T(8,128)(2,1)}, u32[]{:S(2)}, u32[]{:S(2)}) collective-permute-start(bf16[576,1120]{1,0:T(8,128)(2,1)} %pad_maximum_fusion.3.half_ref), channel_id=1, source_target_pairs={{0,4},{4,0},{8,12},{12,8},{16,20},{20,16},{24,28},{28,24},{1,5},{5... | collective-permute-start | bytes 3870728 | tf_op jit(solution)/shard_map/ppermute | solution.py:57
  284.6 39.7 %collective-permute-start.53 = (bf16[576,1120]{1,0:T(8,128)(2,1)}, bf16[576,1120]{1,0:T(8,128)(2,1)}, u32[]{:S(2)}, u32[]{:S(2)}) collective-permute-start(bf16[576,1120]{1,0:T(8,128)(2,1)} %pad_maximum_fusion.4.half_ref), channel_id=1, source_target_pairs={{0,8},{4,12},{8,0},{12,4},{16,24},{20,28},{24,16},{28,20},{1,9},{5... | collective-permute-start | bytes 3870728 | tf_op jit(solution)/shard_map/ppermute | solution.py:57
  294.8 22.5 %collective-permute-start.54 = (bf16[288,1120]{1,0:T(8,128)(2,1)}, bf16[288,1120]{1,0:T(8,128)(2,1)}, u32[]{:S(2)}, u32[]{:S(2)}) collective-permute-start(bf16[288,1120]{1,0:T(8,128)(2,1)} %pad_maximum_fusion.8.half_ref), channel_id=1, source_target_pairs={{0,4},{4,0},{8,12},{12,8},{16,20},{20,16},{24,28},{28,24},{1,5},{5... | collective-permute-start | bytes 1935368 | tf_op jit(solution)/shard_map/ppermute | solution.py:57
  298.7 30.0 %collective-permute-start.52 = (bf16[288,1120]{1,0:T(8,128)(2,1)}, bf16[288,1120]{1,0:T(8,128)(2,1)}, u32[]{:S(2)}, u32[]{:S(2)}) collective-permute-start(bf16[288,1120]{1,0:T(8,128)(2,1)} %pad_maximum_fusion.9.own_ref), channel_id=1, source_target_pairs={{0,4},{4,0},{8,12},{12,8},{16,20},{20,16},{24,28},{28,24},{1,5},{5... | collective-permute-start | bytes 1935368 | tf_op jit(solution)/shard_map/ppermute | solution.py:57
  (86 other events, 658.0 us)

commit v4 on v3

--- a/solution.py
+++ b/solution.py
@@ -544,8 +544,8 @@
         one_far = narrow.send(one_sum, 2)
         one_near = one_kept[:, :rows] + one_got[:, :rows]
         mark = down.advance(one_sum)
+        mark = first.advance(mark)
         mark = up.advance(mark)
-        mark = first.advance(mark)
         mark = second.advance(mark)
         mlp_own = mlp_near + after(mlp_send_far, mark).astype(F32)
         block_output = (middle + own_live * mlp_own).astype(BF16)

time: 340 us -> 339 us (level)
    ppermute x3, waiting for transfers between devices: 0.01 us -> 4.09 us  [on_device(): got = lax.ppermute(gains, 'wide', [(i, i ^ hop) for i in range(wide)])]
    ppermute x24, waiting for transfers between devices: 77.1 us -> 73.4 us  [send(): lax.ppermute(value, 'wide', [(i, i ^ hop) for i in range(self.size)])]
  transfers between devices with their start and end apart: 56 -> 56, of which waited for: 23 -> 26; matrix products, arithmetic and copies ran while one was open for 29% -> 29% of each run, Pallas kernels for 14% -> 14%
where the time goes in v4:
time: 339 us; the launch traced here: 333 us
  waiting for transfers between devices  107 us (32%)
  starting transfers between devices  54.1 us (16%)
  Pallas kernels  50.7 us (15%)
  matrix products  48.5 us (14%)
  other arithmetic  44.2 us (13%)
  local copies, waits for them, and re-layouts  25.4 us (7%)
    ppermute x24, waiting for transfers between devices, send(): lax.ppermute(value, 'wide', [(i, i ^ hop) for i in range(self.size)])  73.4 us
    dot_general x21, matrix products, dot(): return lax.dot_general(a, b, (dims, ((), ())), preferred_element_type=F32)  48.5 us
    ppermute x24, starting transfers between devices, send(): lax.ppermute(value, 'wide', [(i, i ^ hop) for i in range(self.size)])  33.3 us
    ppermute x29, waiting for transfers between devices, send(): return lax.ppermute(value, 'narrow', self.perm[k])  29.7 us
    pallas_call x6, Pallas kernels, join(): pl.pallas_call(partial(join_kernel, quarter), out_shape=jax.ShapeDtypeStr...  19.1 us
    ppermute x29, starting transfers between devices, send(): return lax.ppermute(value, 'narrow', self.perm[k])  18.7 us
    pallas_call x1, Pallas kernels, attend_back(): pl.pallas_call(partial(attend_back_kernel, heads % 2 == 1), out_shape=jax...  15.6 us
    pallas_call x1, Pallas kernels, attend(): pl.pallas_call(partial(attend_kernel, heads % 2 == 1), out_shape=(jax.Sha...  11 us
  transfers between devices with their start and end apart: 56, of which 26 were waited for; matrix products, arithmetic and copies ran while one was open for 29% of the time, Pallas kernels for 14%

profile of v4, /device:TPU:0, one launch (start us, length us, event | category | flops | bytes accessed | tf_op | source)
XLA Modules:
  0.0 332.7 jit_solution(1979386319130626596)
XLA Ops:
  24.6 4.3 %convolution_convert_fusion.7.refs_0_.refs_1_.refs_2_.refs_3_.refs_4_.refs_5_.refs_6_.refs_7_.refs_8_.refs_9_.refs_10_.refs_11_ = bf16[1024,1024]{1,0:T(8,128)(2,1)} fusion(bf16[1120,256]{1,0:T(8,128)(2,1)S(1)} %get-tuple-element.148, bf16[1120,256]{1,0:T(8,128)(2,1)S(1)} %get-tuple-element.149, bf16[1120,256]{1,0:T(8,128)(2,1)S(1)} %get-tuple-element.147, ...), kind=kOutput, calls=%fused_computation.50 | convolution fusion | flops 2365915136 | bytes 6541312 | tf_op jit(solution)/shard_map/dot_general | solution.py:31
  29.0 11.0 %shard_map.152 = (bf16[1024,384]{1,0:T(8,128)(2,1)}, f32[3,4,8,256]{3,2,1,0:T(8,128)}) custom-call(s32[1]{0:T(128)} %bitcast.12.me_ref, bf16[1024,1024]{1,0:T(8,128)(2,1)} %convolution_convert_fusion.7.refs_0_.refs_1_.refs_2_.refs_3_.refs_4_.refs_5_.refs_6_.refs_7_.refs_8_.refs_9_.refs_10_.refs_11_, ...), custom_call_target="tpu_custom_call" | custom-call | flops 256 | bytes 256 | tf_op jit(solution)/shard_map/pallas_call | solution.py:345
  43.5 5.4 %collective-permute-done.2 = bf16[1120,256]{1,0:T(8,128)(2,1)} collective-permute-done((bf16[1120,256]{1,0:T(8,128)(2,1)}, bf16[1120,256]{1,0:T(8,128)(2,1)}, u32[]{:S(2)}, u32[]{:S(2)}) %collective-permute-start.2) | collective-permute-done | bytes 573472 | tf_op jit(solution)/shard_map/ppermute | solution.py:43
  64.1 4.8 %convolution_bitcast_fusion = f32[1120,1024]{1,0:T(8,128)} fusion(bf16[1120,1120]{1,0:T(8,128)(2,1)S(1)} %copy-done.50, bf16[1120,1024]{1,0:T(8,128)(2,1)S(1)} %constant_dynamic-update-slice_fusion), kind=kOutput, calls=%fused_computation.17 | convolution fusion | flops 2569011200 | bytes 9390080 | tf_op jit(solution)/shard_map/dot_general | solution.py:31
  68.9 6.7 %collective-permute-done.10 = bf16[1120,256]{1,0:T(8,128)(2,1)} collective-permute-done((bf16[1120,256]{1,0:T(8,128)(2,1)}, bf16[1120,256]{1,0:T(8,128)(2,1)}, u32[]{:S(2)}, u32[]{:S(2)}) %collective-permute-start.10) | collective-permute-done | bytes 573472 | tf_op jit(solution)/shard_map/ppermute | solution.py:43
  77.9 7.2 %fusion.6 = (bf16[1120,1024]{1,0:T(8,128)(2,1)S(1)}, bf16[1120,1024]{1,0:T(8,128)(2,1)S(1)}) fusion(f32[1120,1024]{1,0:T(8,128)} %convolution_bitcast_fusion, bf16[1120,1120]{1,0:T(8,128)(2,1)S(1)} %copy-done, bf16[1120,256]{1,0:T(8,128)(2,1)} %collective-permute-done.14, bf16[1120,256]{1,0:T(8,128)(2,1)} %collective-permute-done.13, ...), kind=kOutput, calls=%fused_computation.10 | convolution fusion | flops 2591948800 | bytes 13977600 | tf_op jit(solution)/shard_map/dot_general | solution.py:31
  85.2 3.6 %convolution_convert_fusion.1 = bf16[1120,1120]{1,0:T(8,128)(2,1)S(1)} fusion(bf16[1120,1024]{1,0:T(8,128)(2,1)S(1)} %get-tuple-element.87, bf16[1120,1024]{1,0:T(8,128)(2,1)S(1)} %copy-done.47), kind=kOutput, calls=%fused_computation.1 | convolution fusion | flops 2570265600 | bytes 7096320 | tf_op jit(solution)/shard_map/dot_general | solution.py:31
  100.9 4.7 %convolution_convert_fusion = bf16[1120,1120]{1,0:T(8,128)(2,1)S(1)} fusion(bf16[1120,1024]{1,0:T(8,128)(2,1)S(1)} %copy-done.43, bf16[1120,256]{1,0:T(8,128)(2,1)} %collective-permute-done.14, bf16[1120,256]{1,0:T(8,128)(2,1)} %collective-permute-done.13, bf16[1120,256]{1,0:T(8,128)(2,1)} %collective-permute-done.10, bf16[1120,256]{1,0:T(8,128)(2,1)} %multiply_convert_fusion.1), kind=kOutput, calls=%fused_computation | convolution fusion | flops 2579440640 | bytes 7096320 | tf_op jit(solution)/shard_map/dot_general | solution.py:31
  108.4 6.2 %collective-permute-done.16 = bf16[1120,256]{1,0:T(8,128)(2,1)S(1)} collective-permute-done((bf16[1120,256]{1,0:T(8,128)(2,1)S(1)}, bf16[1120,256]{1,0:T(8,128)(2,1)S(1)}, u32[]{:S(2)}, u32[]{:S(2)}) %collective-permute-start.16) | collective-permute-done | bytes 573472 | tf_op jit(solution)/shard_map/ppermute | solution.py:43
  138.9 15.6 %shard_map.153 = bf16[1024,1024]{1,0:T(8,128)(2,1)} custom-call(s32[1]{0:T(128)} %bitcast.12.me_ref, bf16[1024,1024]{1,0:T(8,128)(2,1)} %convolution_convert_fusion.7.refs_0_.refs_1_.refs_2_.refs_3_.refs_4_.refs_5_.refs_6_.refs_7_.refs_8_.refs_9_.refs_10_.refs_11_, ...), custom_call_target="tpu_custom_call" | custom-call | flops 256 | bytes 256 | tf_op jit(solution)/shard_map/pallas_call | solution.py:374
  167.3 5.8 %collective-permute-done.28 = bf16[280,1120]{1,0:T(8,128)(2,1)S(1)} collective-permute-done((bf16[280,1120]{1,0:T(8,128)(2,1)S(1)}, bf16[280,1120]{1,0:T(8,128)(2,1)S(1)}, u32[]{:S(2)}, u32[]{:S(2)}) %collective-permute-start.28) | collective-permute-done | bytes 627232 | tf_op jit(solution)/shard_map/ppermute | solution.py:57
  182.2 8.7 %collective-permute-done.32 = bf16[288,1120]{1,0:T(8,128)(2,1)S(1)} collective-permute-done((bf16[288,1120]{1,0:T(8,128)(2,1)S(1)}, bf16[288,1120]{1,0:T(8,128)(2,1)S(1)}, u32[]{:S(2)}, u32[]{:S(2)}) %collective-permute-start.32) | collective-permute-done | bytes 645152 | tf_op jit(solution)/shard_map/ppermute | solution.py:57
  191.2 5.6 %collective-permute-done.30 = bf16[144,1120]{1,0:T(8,128)(2,1)S(1)} collective-permute-done((bf16[144,1120]{1,0:T(8,128)(2,1)S(1)}, bf16[144,1120]{1,0:T(8,128)(2,1)S(1)}, u32[]{:S(2)}, u32[]{:S(2)}) %collective-permute-start.30) | collective-permute-done | bytes 322592 | tf_op jit(solution)/shard_map/ppermute | solution.py:57
  196.9 6.9 %collective-permute-done.29 = bf16[288,1120]{1,0:T(8,128)(2,1)S(1)} collective-permute-done((bf16[288,1120]{1,0:T(8,128)(2,1)S(1)}, bf16[288,1120]{1,0:T(8,128)(2,1)S(1)}, u32[]{:S(2)}, u32[]{:S(2)}) %collective-permute-start.29) | collective-permute-done | bytes 645152 | tf_op jit(solution)/shard_map/ppermute | solution.py:57
  217.8 11.6 %collective-permute-done.36 = bf16[144,1120]{1,0:T(8,128)(2,1)S(1)} collective-permute-done((bf16[144,1120]{1,0:T(8,128)(2,1)S(1)}, bf16[144,1120]{1,0:T(8,128)(2,1)S(1)}, u32[]{:S(2)}, u32[]{:S(2)}) %collective-permute-start.36) | collective-permute-done | bytes 322592 | tf_op jit(solution)/shard_map/ppermute | solution.py:57
  231.2 11.6 %collective-permute-done.34 = bf16[144,1120]{1,0:T(8,128)(2,1)S(1)} collective-permute-done((bf16[144,1120]{1,0:T(8,128)(2,1)S(1)}, bf16[144,1120]{1,0:T(8,128)(2,1)S(1)}, u32[]{:S(2)}, u32[]{:S(2)}) %collective-permute-start.34) | collective-permute-done | bytes 322592 | tf_op jit(solution)/shard_map/ppermute | solution.py:57
  256.9 3.8 %collective-permute-done.43 = bf16[72,1120]{1,0:T(8,128)(2,1)S(1)} collective-permute-done((bf16[72,1120]{1,0:T(8,128)(2,1)S(1)}, bf16[72,1120]{1,0:T(8,128)(2,1)S(1)}, u32[]{:S(2)}, u32[]{:S(2)}) %collective-permute-start.43) | collective-permute-done | bytes 161312 | tf_op jit(solution)/shard_map/ppermute | solution.py:57
  260.7 3.5 %collective-permute-start.48 = (bf16[72,1120]{1,0:T(8,128)(2,1)S(1)}, bf16[72,1120]{1,0:T(8,128)(2,1)S(1)}, u32[]{:S(2)}, u32[]{:S(2)}) collective-permute-start(bf16[72,1120]{1,0:T(8,128)(2,1)S(1)} %add_convert_fusion.7), channel_id=1, source_target_pairs={{0,16},{4,20},{8,24},{12,28},{16,0},{20,4},{24,8},{28,12},{1,17},{... | collective-permute-start | bytes 483848 | tf_op jit(solution)/shard_map/ppermute | solution.py:57
  264.3 3.5 %collective-permute-start.47 = (bf16[72,1120]{1,0:T(8,128)(2,1)S(1)}, bf16[72,1120]{1,0:T(8,128)(2,1)S(1)}, u32[]{:S(2)}, u32[]{:S(2)}) collective-permute-start(bf16[72,1120]{1,0:T(8,128)(2,1)S(1)} %add_convert_fusion.6), channel_id=1, source_target_pairs={{0,16},{4,20},{8,24},{12,28},{16,0},{20,4},{24,8},{28,12},{1,17},{... | collective-permute-start | bytes 483848 | tf_op jit(solution)/shard_map/ppermute | solution.py:57
  267.8 4.0 %collective-permute-done.41 = f32[2,1120]{1,0:T(2,128)S(1)} collective-permute-done((f32[2,1120]{1,0:T(2,128)S(1)}, f32[2,1120]{1,0:T(2,128)S(1)}, u32[]{:S(2)}, u32[]{:S(2)}) %collective-permute-start.41) | collective-permute-done | bytes 8992 | tf_op jit(solution)/shard_map/ppermute | solution.py:563
  303.6 3.3 %shard_map.157 = f32[1120,1120]{1,0:T(8,128)} custom-call(s32[3]{0:T(128)} %add_add_fusion.at_ref, bf16[576,1120]{1,0:T(8,128)(2,1)} %collective-permute-done.55.half_ref, f32[1120,1120]{1,0:T(8,128)} %shard_map.154.refs_0_), custom_call_target="tpu_custom_call", output_to_operand_aliasing={{}: (2, {})} | custom-call | bytes 1120 | tf_op jit(solution)/shard_map/pallas_call | solution.py:132
  307.0 10.9 %collective-permute-done.54.half_ref = bf16[288,1120]{1,0:T(8,128)(2,1)} collective-permute-done((bf16[288,1120]{1,0:T(8,128)(2,1)}, bf16[288,1120]{1,0:T(8,128)(2,1)}, u32[]{:S(2)}, u32[]{:S(2)}) %collective-permute-start.54) | collective-permute-done | bytes 645152 | tf_op jit(solution)/shard_map/ppermute | solution.py:57
  321.7 3.5 %shard_map.159 = f32[1120,1120]{1,0:T(8,128)} custom-call(s32[3]{0:T(128)} %add_add_fusion.1.at_ref, bf16[576,1120]{1,0:T(8,128)(2,1)} %collective-permute-done.53.half_ref, f32[1120,1120]{1,0:T(8,128)} %shard_map.155.refs_0_), custom_call_target="tpu_custom_call", output_to_operand_aliasing={{}: (2, {})} | custom-call | bytes 1120 | tf_op jit(solution)/shard_map/pallas_call | solution.py:132
  327.5 4.9 %shard_map.160 = (f32[840,1120]{1,0:T(8,128)}, f32[280,1120]{1,0:T(8,128)}) custom-call(s32[3]{0:T(128)} %add_add_fusion.at_ref, bf16[288,1120]{1,0:T(8,128)(2,1)} %pad_maximum_fusion.9.own_ref, bf16[288,1120]{1,0:T(8,128)(2,1)} %collective-permute-done.52.other_ref, f32[840,1120]{1,0:T(8,128)} %shard_map.158.whole_ref), custom_call_target="tpu_custom_call", output_to_operand_aliasing={{0}: (3, {})} | custom-call | bytes 576 | tf_op jit(solution)/shard_map/pallas_call | solution.py:167
  (327 shorter events, 172.7 us)
Async XLA Ops:
  18.9 21.1 %collective-permute-start.3 = (bf16[280,1120]{1,0:T(8,128)(2,1)}, bf16[280,1120]{1,0:T(8,128)(2,1)}, u32[]{:S(2)}, u32[]{:S(2)}) collective-permute-start(bf16[280,1120]{1,0:T(8,128)(2,1)} %param.13), channel_id=1, source_target_pairs={{0,2},{1,3},{2,0},{3,1},{4,6},{5,7},{6,4},{7,5},{8,10},{9,11},{10,... | collective-permute-start | bytes 1881608 | tf_op jit(solution)/shard_map/ppermute | solution.py:43
  20.7 31.5 %collective-permute-start.6 = (bf16[280,1120]{1,0:T(8,128)(2,1)}, bf16[280,1120]{1,0:T(8,128)(2,1)}, u32[]{:S(2)}, u32[]{:S(2)}) collective-permute-start(bf16[280,1120]{1,0:T(8,128)(2,1)} %param.13), channel_id=1, source_target_pairs={{0,1},{1,0},{2,3},{3,2},{4,5},{5,4},{6,7},{7,6},{8,9},{9,8},{10,11... | collective-permute-start | bytes 1881608 | tf_op jit(solution)/shard_map/ppermute | solution.py:43
  20.9 28.0 %collective-permute-start.2 = (bf16[1120,256]{1,0:T(8,128)(2,1)}, bf16[1120,256]{1,0:T(8,128)(2,1)}, u32[]{:S(2)}, u32[]{:S(2)}) collective-permute-start(bf16[1120,256]{1,0:T(8,128)(2,1)} %fusion.68), channel_id=1, source_target_pairs={{0,2},{1,3},{2,0},{3,1},{4,6},{5,7},{6,4},{7,5},{8,10},{9,11},{10,... | collective-permute-start | bytes 1720328 | tf_op jit(solution)/shard_map/ppermute | solution.py:43
  21.3 41.6 %collective-permute-start.11 = (bf16[1120,256]{1,0:T(8,128)(2,1)}, bf16[1120,256]{1,0:T(8,128)(2,1)}, u32[]{:S(2)}, u32[]{:S(2)}) collective-permute-start(bf16[1120,256]{1,0:T(8,128)(2,1)} %fusion.68), channel_id=1, source_target_pairs={{0,1},{1,0},{2,3},{3,2},{4,5},{5,4},{6,7},{7,6},{8,9},{9,8},{10,11... | collective-permute-start | bytes 1720328 | tf_op jit(solution)/shard_map/ppermute | solution.py:43
  94.5 38.0 %collective-permute-start.18 = (bf16[560,1120]{1,0:T(8,128)(2,1)S(1)}, bf16[560,1120]{1,0:T(8,128)(2,1)S(1)}, u32[]{:S(2)}, u32[]{:S(2)}) collective-permute-start(bf16[560,1120]{1,0:T(8,128)(2,1)S(1)} %copy-done.27), channel_id=1, source_target_pairs={{0,4},{4,0},{8,12},{12,8},{16,20},{20,16},{24,28},{28,24},{1,5},{5... | collective-permute-start | bytes 3763208 | tf_op jit(solution)/shard_map/ppermute | solution.py:57
  106.9 47.7 %collective-permute-start.24 = (bf16[560,1120]{1,0:T(8,128)(2,1)}, bf16[560,1120]{1,0:T(8,128)(2,1)}, u32[]{:S(2)}, u32[]{:S(2)}) collective-permute-start(bf16[560,1120]{1,0:T(8,128)(2,1)} %dynamic-slice_bitcast_fusion), channel_id=1, source_target_pairs={{0,8},{4,12},{8,0},{12,4},{16,24},{20,28},{24,16},{28,20},{1,9},{5... | collective-permute-start | bytes 3763208 | tf_op jit(solution)/shard_map/ppermute | solution.py:57
  134.8 21.9 %collective-permute-start.23 = (bf16[280,1120]{1,0:T(8,128)(2,1)S(1)}, bf16[280,1120]{1,0:T(8,128)(2,1)}, u32[]{:S(2)}, u32[]{:S(2)}) collective-permute-start(bf16[280,1120]{1,0:T(8,128)(2,1)S(1)} %fusion.73), channel_id=1, source_target_pairs={{0,8},{4,12},{8,0},{12,4},{16,24},{20,28},{24,16},{28,20},{1,9},{5... | collective-permute-start | bytes 1881608 | tf_op jit(solution)/shard_map/ppermute | solution.py:57
  136.4 70.3 %collective-permute-start.17 = (bf16[1120,512]{1,0:T(8,128)(2,1)}, bf16[1120,512]{1,0:T(8,128)(2,1)}, u32[]{:S(2)}, u32[]{:S(2)}) collective-permute-start(bf16[1120,512]{1,0:T(8,128)(2,1)} %fusion.14), channel_id=1, source_target_pairs={{0,1},{1,0},{2,3},{3,2},{4,5},{5,4},{6,7},{7,6},{8,9},{9,8},{10,11... | collective-permute-start | bytes 3440648 | tf_op jit(solution)/shard_map/ppermute | solution.py:43
  138.4 28.7 %collective-permute-start.22 = (bf16[1120,256]{1,0:T(8,128)(2,1)S(1)}, bf16[1120,256]{1,0:T(8,128)(2,1)}, u32[]{:S(2)}, u32[]{:S(2)}) collective-permute-start(bf16[1120,256]{1,0:T(8,128)(2,1)S(1)} %multiply_convert_fusion), channel_id=1, source_target_pairs={{0,2},{1,3},{2,0},{3,1},{4,6},{5,7},{6,4},{7,5},{8,10},{9,11},{10,... | collective-permute-start | bytes 1720328 | tf_op jit(solution)/shard_map/ppermute | solution.py:43
  138.9 39.0 %collective-permute-start.26 = (bf16[1120,256]{1,0:T(8,128)(2,1)S(1)}, bf16[1120,256]{1,0:T(8,128)(2,1)}, u32[]{:S(2)}, u32[]{:S(2)}) collective-permute-start(bf16[1120,256]{1,0:T(8,128)(2,1)S(1)} %multiply_convert_fusion), channel_id=1, source_target_pairs={{0,1},{1,0},{2,3},{3,2},{4,5},{5,4},{6,7},{7,6},{8,9},{9,8},{10,11... | collective-permute-start | bytes 1720328 | tf_op jit(solution)/shard_map/ppermute | solution.py:43
  164.5 26.6 %collective-permute-start.31 = (bf16[144,1120]{1,0:T(8,128)(2,1)S(1)}, bf16[144,1120]{1,0:T(8,128)(2,1)S(1)}, u32[]{:S(2)}, u32[]{:S(2)}) collective-permute-start(bf16[144,1120]{1,0:T(8,128)(2,1)S(1)} %select_convert_fusion.1), channel_id=1, source_target_pairs={{0,16},{4,20},{8,24},{12,28},{16,0},{20,4},{24,8},{28,12},{1,17},{... | collective-permute-start | bytes 967688 | tf_op jit(solution)/shard_map/ppermute | solution.py:57
  175.3 21.5 %collective-permute-start.30 = (bf16[144,1120]{1,0:T(8,128)(2,1)S(1)}, bf16[144,1120]{1,0:T(8,128)(2,1)S(1)}, u32[]{:S(2)}, u32[]{:S(2)}) collective-permute-start(bf16[144,1120]{1,0:T(8,128)(2,1)S(1)} %select_convert_fusion), channel_id=1, source_target_pairs={{0,16},{4,20},{8,24},{12,28},{16,0},{20,4},{24,8},{28,12},{1,17},{... | collective-permute-start | bytes 967688 | tf_op jit(solution)/shard_map/ppermute | solution.py:57
  180.7 23.2 %collective-permute-start.29 = (bf16[288,1120]{1,0:T(8,128)(2,1)S(1)}, bf16[288,1120]{1,0:T(8,128)(2,1)S(1)}, u32[]{:S(2)}, u32[]{:S(2)}) collective-permute-start(bf16[288,1120]{1,0:T(8,128)(2,1)S(1)} %dynamic-slice_bitcast_fusion.2), channel_id=1, source_target_pairs={{0,4},{4,0},{8,12},{12,8},{16,20},{20,16},{24,28},{28,24},{1,5},{5... | collective-permute-start | bytes 1935368 | tf_op jit(solution)/shard_map/ppermute | solution.py:57
  209.1 36.8 %collective-permute-start.25 = (bf16[1120,256]{1,0:T(8,128)(2,1)S(1)}, bf16[1120,256]{1,0:T(8,128)(2,1)S(1)}, u32[]{:S(2)}, u32[]{:S(2)}) collective-permute-start(bf16[1120,256]{1,0:T(8,128)(2,1)S(1)} %fusion.59), channel_id=1, source_target_pairs={{0,2},{1,3},{2,0},{3,1},{4,6},{5,7},{6,4},{7,5},{8,10},{9,11},{10,... | collective-permute-start | bytes 1720328 | tf_op jit(solution)/shard_map/ppermute | solution.py:43
  210.7 18.7 %collective-permute-start.36 = (bf16[144,1120]{1,0:T(8,128)(2,1)S(1)}, bf16[144,1120]{1,0:T(8,128)(2,1)S(1)}, u32[]{:S(2)}, u32[]{:S(2)}) collective-permute-start(bf16[144,1120]{1,0:T(8,128)(2,1)S(1)} %add_convert_fusion.4), channel_id=1, source_target_pairs={{0,16},{4,20},{8,24},{12,28},{16,0},{20,4},{24,8},{28,12},{1,17},{... | collective-permute-start | bytes 967688 | tf_op jit(solution)/shard_map/ppermute | solution.py:57
  213.7 29.1 %collective-permute-start.34 = (bf16[144,1120]{1,0:T(8,128)(2,1)S(1)}, bf16[144,1120]{1,0:T(8,128)(2,1)S(1)}, u32[]{:S(2)}, u32[]{:S(2)}) collective-permute-start(bf16[144,1120]{1,0:T(8,128)(2,1)S(1)} %add_convert_fusion.3), channel_id=1, source_target_pairs={{0,16},{4,20},{8,24},{12,28},{16,0},{20,4},{24,8},{28,12},{1,17},{... | collective-permute-start | bytes 967688 | tf_op jit(solution)/shard_map/ppermute | solution.py:57
  215.6 29.6 %collective-permute-start.33 = (bf16[144,1120]{1,0:T(8,128)(2,1)S(1)}, bf16[144,1120]{1,0:T(8,128)(2,1)S(1)}, u32[]{:S(2)}, u32[]{:S(2)}) collective-permute-start(bf16[144,1120]{1,0:T(8,128)(2,1)S(1)} %fusion.78), channel_id=1, source_target_pairs={{0,8},{4,12},{8,0},{12,4},{16,24},{20,28},{24,16},{28,20},{1,9},{5... | collective-permute-start | bytes 967688 | tf_op jit(solution)/shard_map/ppermute | solution.py:57
  229.4 19.5 %collective-permute-start.38 = (bf16[1120,256]{1,0:T(8,128)(2,1)S(1)}, bf16[1120,256]{1,0:T(8,128)(2,1)S(1)}, u32[]{:S(2)}, u32[]{:S(2)}) collective-permute-start(bf16[1120,256]{1,0:T(8,128)(2,1)S(1)} %fusion.58), channel_id=1, source_target_pairs={{0,2},{1,3},{2,0},{3,1},{4,6},{5,7},{6,4},{7,5},{8,10},{9,11},{10,... | collective-permute-start | bytes 1720328 | tf_op jit(solution)/shard_map/ppermute | solution.py:43
  231.0 41.3 %collective-permute-start.45 = (bf16[288,1120]{1,0:T(8,128)(2,1)S(1)}, bf16[288,1120]{1,0:T(8,128)(2,1)S(1)}, u32[]{:S(2)}, u32[]{:S(2)}) collective-permute-start(bf16[288,1120]{1,0:T(8,128)(2,1)S(1)} %pad_maximum_fusion.6), channel_id=1, source_target_pairs={{0,8},{4,12},{8,0},{12,4},{16,24},{20,28},{24,16},{28,20},{1,9},{5... | collective-permute-start | bytes 1935368 | tf_op jit(solution)/shard_map/ppermute | solution.py:57
  245.2 37.0 %collective-permute-start.51 = (bf16[288,1120]{1,0:T(8,128)(2,1)}, bf16[288,1120]{1,0:T(8,128)(2,1)}, u32[]{:S(2)}, u32[]{:S(2)}) collective-permute-start(bf16[288,1120]{1,0:T(8,128)(2,1)} %pad_maximum_fusion.7), channel_id=1, source_target_pairs={{0,4},{4,0},{8,12},{12,8},{16,20},{20,16},{24,28},{28,24},{1,5},{5... | collective-permute-start | bytes 1935368 | tf_op jit(solution)/shard_map/ppermute | solution.py:57
  273.5 30.1 %collective-permute-start.55 = (bf16[576,1120]{1,0:T(8,128)(2,1)}, bf16[576,1120]{1,0:T(8,128)(2,1)}, u32[]{:S(2)}, u32[]{:S(2)}) collective-permute-start(bf16[576,1120]{1,0:T(8,128)(2,1)} %pad_maximum_fusion.3.half_ref), channel_id=1, source_target_pairs={{0,4},{4,0},{8,12},{12,8},{16,20},{20,16},{24,28},{28,24},{1,5},{5... | collective-permute-start | bytes 3870728 | tf_op jit(solution)/shard_map/ppermute | solution.py:57
  284.5 37.2 %collective-permute-start.53 = (bf16[576,1120]{1,0:T(8,128)(2,1)}, bf16[576,1120]{1,0:T(8,128)(2,1)}, u32[]{:S(2)}, u32[]{:S(2)}) collective-permute-start(bf16[576,1120]{1,0:T(8,128)(2,1)} %pad_maximum_fusion.4.half_ref), channel_id=1, source_target_pairs={{0,8},{4,12},{8,0},{12,4},{16,24},{20,28},{24,16},{28,20},{1,9},{5... | collective-permute-start | bytes 3870728 | tf_op jit(solution)/shard_map/ppermute | solution.py:57
  295.1 22.8 %collective-permute-start.54 = (bf16[288,1120]{1,0:T(8,128)(2,1)}, bf16[288,1120]{1,0:T(8,128)(2,1)}, u32[]{:S(2)}, u32[]{:S(2)}) collective-permute-start(bf16[288,1120]{1,0:T(8,128)(2,1)} %pad_maximum_fusion.8.half_ref), channel_id=1, source_target_pairs={{0,4},{4,0},{8,12},{12,8},{16,20},{20,16},{24,28},{28,24},{1,5},{5... | collective-permute-start | bytes 1935368 | tf_op jit(solution)/shard_map/ppermute | solution.py:57
  299.2 28.3 %collective-permute-start.52 = (bf16[288,1120]{1,0:T(8,128)(2,1)}, bf16[288,1120]{1,0:T(8,128)(2,1)}, u32[]{:S(2)}, u32[]{:S(2)}) collective-permute-start(bf16[288,1120]{1,0:T(8,128)(2,1)} %pad_maximum_fusion.9.own_ref), channel_id=1, source_target_pairs={{0,4},{4,0},{8,12},{12,8},{16,20},{20,16},{24,28},{28,24},{1,5},{5... | collective-permute-start | bytes 1935368 | tf_op jit(solution)/shard_map/ppermute | solution.py:57
  (86 other events, 662.7 us)
